TPU v7x, 32 devices: a whole 2x2x4 slice. The times are simulated.
32 devices in a mesh: row: 4 (over z), col: 8 (over y, x, core).
Axes of the slice: x: 2, y: 2, z: 4, core: 2. Of those that a mesh axis runs over, the one named last changes fastest.
Arguments:
- x_blocks: bfloat16 [1024, 1024, 128], P('row', 'col'), may hold values from -0.0625 to 0.0625
- block_ids: int32 [1024, 8], P('row', 'col'), may hold values from 0 to 511, as said below
- margins: float32 [16384], P('row'), may hold values from -6 to 6
- deleted: int32 [2048], P('row'), may hold values from 0 to 16383, as said below
- grads: float32 [16384, 128], P('col'), may hold values from -6 to 6
Outputs:
- solution: float32 [16384, 128], P('col')
- residual: float32 [16384, 128], P('col')
Inputs may be any that keep to these rules, and one draw needn't show every extreme that they name: `block_ids`: each device's 256 entries are distinct and rise; each device lists the first and the last block of its grid. `deleted`: the 512 entries of row shard r are distinct rows of that shard, r * 4096 and up; each shard deletes its first and its last row.
All inputs are finite; a program needn't handle non-finite values.
Results may differ from a plain program's by a relative error of at most 0.015.
Values may be sent and summed in bfloat16 or wider, within the bound.
No kernel may reach another device: no remote copies, remote signals or barrier semaphores. Data moves between devices by JAX's collectives and lax.ppermute only.
A program may use at most 128 MiB of HBM per device.

v0:
```python
import jax
import jax.numpy as jnp
from jax import lax
from jax.sharding import PartitionSpec as P

ITERS = 3


highest = lax.Precision.HIGHEST
ridge_weight = 0.2


def on_device(x_blocks, block_ids, margins, deleted, grads):
    block_width = x_blocks.shape[1]
    feature_rows = grads.shape[0]
    directions = grads.shape[1]
    row_count = margins.shape[0]
    row_blocks = row_count // block_width
    feature_blocks = feature_rows // block_width
    pattern = block_ids[:, 0]
    block_row = pattern // feature_blocks
    block_column = pattern % feature_blocks
    row_select = (block_row[:, None] == jnp.arange(row_blocks, dtype=jnp.int32)[None, :]).astype(
        jnp.float32
    )
    column_select = (
        block_column[:, None] == jnp.arange(feature_blocks, dtype=jnp.int32)[None, :]
    ).astype(jnp.float32)
    global_rows = lax.axis_index("row") * row_count + jnp.arange(row_count, dtype=jnp.int32)
    removed = jnp.any(global_rows[:, None] == deleted[None, :], axis=1)
    logistic = jax.nn.sigmoid(margins)
    weights_flat = jnp.where(removed, 0.0, logistic * (1.0 - logistic))
    weights = weights_flat.reshape(row_blocks, block_width, 1)
    share_rows = feature_rows // lax.axis_size("row")
    offset = lax.axis_index("row") * share_rows

    def own_rows(values):
        return lax.dynamic_slice_in_dim(values, offset, share_rows, 0)

    residual = grads
    solution = jnp.zeros_like(residual)
    direction = residual
    mine = own_rows(residual)
    norm_now = lax.psum(jnp.sum(mine * mine, axis=0), ("row", "col"))
    for iteration in range(ITERS):
        apply_rounded = direction.astype(jnp.bfloat16)
        picked_tiles = apply_rounded.reshape(feature_blocks, block_width, directions)[block_column]
        forward = jnp.einsum(
            "bij,bjk->bik", x_blocks, picked_tiles, preferred_element_type=jnp.float32
        )
        partial_rows = jnp.einsum("br,bik->rik", row_select, forward, precision=highest)
        projected = lax.psum(partial_rows, "col")
        scaled = (weights * projected).astype(jnp.bfloat16)
        picked_rows = scaled[block_row]
        backward = jnp.einsum(
            "bji,bjk->bik", x_blocks, picked_rows, preferred_element_type=jnp.float32
        )
        summed = jnp.einsum("bc,bik->cik", column_select, backward, precision=highest)
        hessian_image = (
            lax.psum(summed.reshape(feature_rows, directions), "row") + ridge_weight * direction
        )
        own_image = own_rows(hessian_image)
        own_residual = own_rows(residual)
        curvature, cross_term, image_square = lax.psum(
            (
                jnp.sum(own_rows(direction) * own_image, axis=0),
                jnp.sum(own_residual * own_image, axis=0),
                jnp.sum(own_image * own_image, axis=0),
            ),
            ("row", "col"),
        )
        step_size = norm_now / curvature
        norm_next = norm_now - 2.0 * step_size * cross_term + step_size * step_size * image_square
        solution = solution + step_size * direction
        residual = residual - step_size * hessian_image
        if iteration + 1 < ITERS:
            direction = residual + norm_next / norm_now * direction
            norm_now = norm_next
    return (solution, residual)


def solution(mesh):
    placed = (P("row", "col", None), P("row", "col"), P("row"), P("row"), P("col", None))
    return jax.shard_map(
        on_device,
        mesh=mesh,
        in_specs=placed,
        out_specs=(P("col", None), P("col", None)),
        check_vma=False,
    )
```

profile of v0, /device:TPU:0, one launch (start us, length us, event | category | flops | bytes accessed | tf_op | source)
XLA Modules:
  0.0 801.8 jit_solution(736054281682014846)
XLA Ops:
  7.9 1.3 convert_element_type.20
  9.2 8.6 %gather_fusion = bf16[256,128,128]{2,1,0:T(8,128)(2,1)} fusion(bf16[16,128,128]{2,1,0:T(8,128)(2,1)S(1)} %bitcast.54, s32[1024]{0:T(1024)S(1)} %pad_clamp_fusion.1), kind=kCustom, calls=%fused_computation | custom fusion | bytes 16778240 | tf_op jit(solution)/shard_map/gather | solution.py:47
  17.8 12.8 %convolution_bitcast_fusion.5 = f32[256,128,128]{1,2,0:T(8,128)} fusion(bf16[256,128,128]{2,1,0:T(8,128)(2,1)} %gather_fusion, bf16[256,128,128]{2,1,0:T(8,128)(2,1)} %param.5), kind=kOutput, calls=%fused_computation.11 | convolution fusion | flops 1073741824 | bytes 33554432 | tf_op jit(solution)/shard_map/bij,bjk->bik/dot_general | solution.py:48
  30.6 17.5 %copy.24 = f32[256,128,128]{2,0,1:T(8,128)} copy(f32[256,128,128]{1,2,0:T(8,128)} %convolution_bitcast_fusion.5) | data formatting | bytes 33554432 | tf_op jit(solution)/shard_map/bij,bjk->bik/dot_general | solution.py:48
  48.1 10.8 %fusion.5 = f32[32,128,128]{2,0,1:T(8,128)} fusion(f32[256,128,128]{2,0,1:T(8,128)} %copy.24, s32[256]{0:T(256)S(1)} %bitcast.61), kind=kOutput, calls=%fused_computation.36 | convolution fusion | flops 1610620928 | bytes 18875392 | tf_op jit(solution)/shard_map/br,bik->rik/dot_general | solution.py:51
  59.2 1.5 compare_reduce_fusion
  60.9 62.6 %all-reduce.9.cloned.1.call-done = f32[32,128,128]{2,0,1:T(8,128)} async-done(((f32[32,128,128]{2,0,1:T(8,128)}), f32[32,128,128]{2,0,1:T(8,128)}) %all-reduce.9.cloned.1.call-update) | async-done | bytes 2097168 | tf_op jit(solution)/shard_map/psum | solution.py:52
  123.5 1.9 multiply_convert_fusion.2
  125.9 8.6 %gather_fusion.1 = bf16[256,128,128]{2,1,0:T(8,128)(2,1)} fusion(bf16[32,128,128]{2,1,0:T(8,128)(2,1)S(1)} %copy.25, s32[1024]{0:T(1024)S(1)} %pad_clamp_fusion), kind=kCustom, calls=%fused_computation.1 | custom fusion | bytes 16778240 | tf_op jit(solution)/shard_map/gather | solution.py:54
  134.5 14.4 %convolution_bitcast_fusion.4 = f32[256,128,128]{1,2,0:T(8,128)} fusion(bf16[256,128,128]{2,1,0:T(8,128)(2,1)} %gather_fusion.1, bf16[256,128,128]{2,1,0:T(8,128)(2,1)} %param.5), kind=kOutput, calls=%fused_computation.10 | convolution fusion | flops 1073741824 | bytes 33554432 | tf_op jit(solution)/shard_map/bji,bjk->bik/dot_general | solution.py:55
  148.9 17.5 %copy.27 = f32[256,128,128]{2,0,1:T(8,128)} copy(f32[256,128,128]{1,2,0:T(8,128)} %convolution_bitcast_fusion.4) | data formatting | bytes 33554432 | tf_op jit(solution)/shard_map/bji,bjk->bik/dot_general | solution.py:55
  166.3 9.1 %fusion.17 = f32[16,128,128]{2,0,1:T(8,128)S(1)} fusion(f32[256,128,128]{2,0,1:T(8,128)} %copy.27, s32[256]{0:T(256)S(1)} %bitcast.58), kind=kOutput, calls=%fused_computation.48 | convolution fusion | flops 805310464 | bytes 17826816 | tf_op jit(solution)/shard_map/bc,bik->cik/dot_general | solution.py:58
  175.5 1.3 copy.28
  176.8 51.1 %all-reduce.11.cloned.1.call-done = f32[2048,128]{1,0:T(8,128)} async-done(((f32[2048,128]{1,0:T(8,128)}), f32[2048,128]{1,0:T(8,128)}) %all-reduce.11.cloned.1.call-update) | async-done | bytes 1048592 | tf_op jit(solution)/shard_map/psum | solution.py:60
  227.9 1.3 multiply_add_fusion.5
  229.3 40.4 %all-reduce.1 = (f32[128]{0:T(128)S(1)}, f32[128]{0:T(128)S(1)}, f32[128]{0:T(128)S(1)}) all-reduce(f32[128]{0:T(128)S(1)} %get-tuple-element.7, f32[128]{0:T(128)S(1)} %get-tuple-element.6, f32[128]{0:T(128)S(1)} %get-tuple-element.5), channel_id=1, replica_groups=mesh['row'=4,'col'=8] {'row','col'}, use_global_device_ids=true, to_apply=%region_1.2 | all-reduce | flops 384 | bytes 3072 | tf_op jit(solution)/shard_map/psum | solution.py:44
  269.8 2.4 fusion.24
  272.2 8.6 %gather_fusion.2 = bf16[256,128,128]{2,1,0:T(8,128)(2,1)} fusion(bf16[16,128,128]{2,1,0:T(8,128)(2,1)S(1)} %bitcast.52, s32[1024]{0:T(1024)S(1)} %pad_clamp_fusion.1), kind=kCustom, calls=%fused_computation.2 | custom fusion | bytes 16778240 | tf_op jit(solution)/shard_map/gather | solution.py:47
  280.8 12.8 %convolution_bitcast_fusion.3 = f32[256,128,128]{1,2,0:T(8,128)} fusion(bf16[256,128,128]{2,1,0:T(8,128)(2,1)} %gather_fusion.2, bf16[256,128,128]{2,1,0:T(8,128)(2,1)} %param.5), kind=kOutput, calls=%fused_computation.9 | convolution fusion | flops 1073741824 | bytes 33554432 | tf_op jit(solution)/shard_map/bij,bjk->bik/dot_general | solution.py:48
  293.6 17.5 %copy.30 = f32[256,128,128]{2,0,1:T(8,128)} copy(f32[256,128,128]{1,2,0:T(8,128)} %convolution_bitcast_fusion.3) | data formatting | bytes 33554432 | tf_op jit(solution)/shard_map/bij,bjk->bik/dot_general | solution.py:48
  311.1 10.7 %fusion.3 = f32[32,128,128]{2,0,1:T(8,128)} fusion(f32[256,128,128]{2,0,1:T(8,128)} %copy.30, s32[256]{0:T(256)S(1)} %bitcast.62), kind=kOutput, calls=%fused_computation.35 | convolution fusion | flops 1610620928 | bytes 18875392 | tf_op jit(solution)/shard_map/br,bik->rik/dot_general | solution.py:51
  322.1 61.0 %all-reduce.13.cloned.1.call-done = f32[32,128,128]{2,0,1:T(8,128)} async-done(((f32[32,128,128]{2,0,1:T(8,128)}), f32[32,128,128]{2,0,1:T(8,128)}) %all-reduce.13.cloned.1.call-update) | async-done | bytes 2097168 | tf_op jit(solution)/shard_map/psum | solution.py:52
  383.1 1.9 multiply_convert_fusion.1
  385.5 8.6 %gather_fusion.3 = bf16[256,128,128]{2,1,0:T(8,128)(2,1)} fusion(bf16[32,128,128]{2,1,0:T(8,128)(2,1)S(1)} %copy.31, s32[1024]{0:T(1024)S(1)} %pad_clamp_fusion), kind=kCustom, calls=%fused_computation.3 | custom fusion | bytes 16778240 | tf_op jit(solution)/shard_map/gather | solution.py:54
  394.1 14.4 %convolution_bitcast_fusion.2 = f32[256,128,128]{1,2,0:T(8,128)} fusion(bf16[256,128,128]{2,1,0:T(8,128)(2,1)} %gather_fusion.3, bf16[256,128,128]{2,1,0:T(8,128)(2,1)} %param.5), kind=kOutput, calls=%fused_computation.8 | convolution fusion | flops 1073741824 | bytes 33554432 | tf_op jit(solution)/shard_map/bji,bjk->bik/dot_general | solution.py:55
  408.4 17.5 %copy.33 = f32[256,128,128]{2,0,1:T(8,128)} copy(f32[256,128,128]{1,2,0:T(8,128)} %convolution_bitcast_fusion.2) | data formatting | bytes 33554432 | tf_op jit(solution)/shard_map/bji,bjk->bik/dot_general | solution.py:55
  425.9 9.0 %fusion.15 = f32[16,128,128]{2,0,1:T(8,128)S(1)} fusion(f32[256,128,128]{2,0,1:T(8,128)} %copy.33, s32[256]{0:T(256)S(1)} %bitcast.59), kind=kOutput, calls=%fused_computation.47 | convolution fusion | flops 805310464 | bytes 17826816 | tf_op jit(solution)/shard_map/bc,bik->cik/dot_general | solution.py:58
  435.0 1.3 copy.34
  436.3 51.1 %all-reduce.15.cloned.1.call-done = f32[2048,128]{1,0:T(8,128)} async-done(((f32[2048,128]{1,0:T(8,128)}), f32[2048,128]{1,0:T(8,128)}) %all-reduce.15.cloned.1.call-update) | async-done | bytes 1048592 | tf_op jit(solution)/shard_map/psum | solution.py:60
  487.4 1.3 multiply_add_fusion.3
  488.8 1.0 multiply_reduce_fusion.2
  489.8 40.2 %all-reduce = (f32[128]{0:T(128)S(1)}, f32[128]{0:T(128)S(1)}, f32[128]{0:T(128)S(1)}) all-reduce(f32[128]{0:T(128)S(1)} %get-tuple-element.3, f32[128]{0:T(128)S(1)} %get-tuple-element.4, f32[128]{0:T(128)S(1)} %get-tuple-element.2), channel_id=1, replica_groups=mesh['row'=4,'col'=8] {'row','col'}, use_global_device_ids=true, to_apply=%region_16.17 | all-reduce | flops 384 | bytes 3072 | tf_op jit(solution)/shard_map/psum | solution.py:64
  530.0 2.8 fusion.22
  532.8 8.6 %gather_fusion.4 = bf16[256,128,128]{2,1,0:T(8,128)(2,1)} fusion(bf16[16,128,128]{2,1,0:T(8,128)(2,1)S(1)} %bitcast.53, s32[1024]{0:T(1024)S(1)} %pad_clamp_fusion.1), kind=kCustom, calls=%fused_computation.4 | custom fusion | bytes 16778240 | tf_op jit(solution)/shard_map/gather | solution.py:47
  541.4 12.8 %convolution_bitcast_fusion.1 = f32[256,128,128]{1,2,0:T(8,128)} fusion(bf16[256,128,128]{2,1,0:T(8,128)(2,1)} %gather_fusion.4, bf16[256,128,128]{2,1,0:T(8,128)(2,1)} %param.5), kind=kOutput, calls=%fused_computation.7 | convolution fusion | flops 1073741824 | bytes 33554432 | tf_op jit(solution)/shard_map/bij,bjk->bik/dot_general | solution.py:48
  554.2 17.5 %copy.36 = f32[256,128,128]{2,0,1:T(8,128)} copy(f32[256,128,128]{1,2,0:T(8,128)} %convolution_bitcast_fusion.1) | data formatting | bytes 33554432 | tf_op jit(solution)/shard_map/bij,bjk->bik/dot_general | solution.py:48
  571.7 10.7 %fusion.1 = f32[32,128,128]{2,0,1:T(8,128)} fusion(f32[256,128,128]{2,0,1:T(8,128)} %copy.36, s32[256]{0:T(256)S(1)} %bitcast.63), kind=kOutput, calls=%fused_computation.34 | convolution fusion | flops 1610620928 | bytes 18875392 | tf_op jit(solution)/shard_map/br,bik->rik/dot_general | solution.py:51
  582.7 61.0 %all-reduce.17.cloned.1.call-done = f32[32,128,128]{2,0,1:T(8,128)} async-done(((f32[32,128,128]{2,0,1:T(8,128)}), f32[32,128,128]{2,0,1:T(8,128)}) %all-reduce.17.cloned.1.call-update) | async-done | bytes 2097168 | tf_op jit(solution)/shard_map/psum | solution.py:52
  643.8 1.9 multiply_convert_fusion
  646.1 8.6 %gather_fusion.5 = bf16[256,128,128]{2,1,0:T(8,128)(2,1)} fusion(bf16[32,128,128]{2,1,0:T(8,128)(2,1)S(1)} %copy.37, s32[1024]{0:T(1024)S(1)} %pad_clamp_fusion), kind=kCustom, calls=%fused_computation.5 | custom fusion | bytes 16778240 | tf_op jit(solution)/shard_map/gather | solution.py:54
  654.7 14.4 %convolution_bitcast_fusion = f32[256,128,128]{1,2,0:T(8,128)} fusion(bf16[256,128,128]{2,1,0:T(8,128)(2,1)} %gather_fusion.5, bf16[256,128,128]{2,1,0:T(8,128)(2,1)} %param.5), kind=kOutput, calls=%fused_computation.6 | convolution fusion | flops 1073741824 | bytes 33554432 | tf_op jit(solution)/shard_map/bji,bjk->bik/dot_general | solution.py:55
  669.1 17.5 %copy.39 = f32[256,128,128]{2,0,1:T(8,128)} copy(f32[256,128,128]{1,2,0:T(8,128)} %convolution_bitcast_fusion) | data formatting | bytes 33554432 | tf_op jit(solution)/shard_map/bji,bjk->bik/dot_general | solution.py:55
  686.6 9.1 %fusion.13 = f32[16,128,128]{2,0,1:T(8,128)S(1)} fusion(f32[256,128,128]{2,0,1:T(8,128)} %copy.39, s32[256]{0:T(256)S(1)} %bitcast.60), kind=kOutput, calls=%fused_computation.46 | convolution fusion | flops 805310464 | bytes 17826816 | tf_op jit(solution)/shard_map/bc,bik->cik/dot_general | solution.py:58
  695.7 1.4 copy.40
  697.1 51.1 %all-reduce.19.cloned.1.call-done = f32[2048,128]{1,0:T(8,128)} async-done(((f32[2048,128]{1,0:T(8,128)}), f32[2048,128]{1,0:T(8,128)}) %all-reduce.19.cloned.1.call-update) | async-done | bytes 1048592 | tf_op jit(solution)/shard_map/psum | solution.py:60
  748.2 1.7 multiply_add_fusion.1
  750.9 40.0 %psum.106 = f32[128]{0:T(128)S(1)} all-reduce(f32[128]{0:T(128)S(1)} %multiply_reduce_fusion), channel_id=1, replica_groups=mesh['row'=4,'col'=8] {'row','col'}, use_global_device_ids=true, to_apply=%region_20.21 | all-reduce | flops 128 | bytes 1024 | tf_op jit(solution)/shard_map/psum | solution.py:64
  790.9 3.6 multiply_subtract_fusion
  (35 shorter events, 4.2 us)
Async XLA Ops:
  7.2 116.3 %all-reduce.9.cloned.1.call-start = ((), (), s32[]{:S(2)}) async-start(), calls=%async_computation | async-start | bytes 4194304 | tf_op jit(solution)/shard_map/psum | solution.py:52
  48.1 11.1 %copy-start.3 = (s32[512]{0:T(512)S(1)}, s32[512]{0:T(512)}, u32[]{:S(2)}) copy-start(s32[512]{0:T(512)} %param.8) | copy-start | bytes 6148
  48.1 12.6 %copy-start.2 = (f32[4096]{0:T(1024)S(1)}, f32[4096]{0:T(1024)}, u32[]{:S(2)}) copy-start(f32[4096]{0:T(1024)} %param.7) | copy-start | bytes 49156
  58.9 169.0 %all-reduce.11.cloned.1.call-start = ((), (), s32[]{:S(2)}) async-start(), calls=%async_computation.1 | async-start | bytes 2097152 | tf_op jit(solution)/shard_map/psum | solution.py:60
  166.3 61.6 %copy-start = (f32[2048,128]{1,0:T(8,128)S(1)}, f32[2048,128]{1,0:T(8,128)}, u32[]{:S(2)}) copy-start(f32[2048,128]{1,0:T(8,128)} %param.9) | copy-start | bytes 3145732
  176.8 206.3 %all-reduce.13.cloned.1.call-start = ((), (), s32[]{:S(2)}) async-start(), calls=%async_computation.2 | async-start | bytes 4194304 | tf_op jit(solution)/shard_map/psum | solution.py:52
  321.9 165.5 %all-reduce.15.cloned.1.call-start = ((), (), s32[]{:S(2)}) async-start(), calls=%async_computation.3 | async-start | bytes 2097152 | tf_op jit(solution)/shard_map/psum | solution.py:60
  436.3 207.5 %all-reduce.17.cloned.1.call-start = ((), (), s32[]{:S(2)}) async-start(), calls=%async_computation.4 | async-start | bytes 4194304 | tf_op jit(solution)/shard_map/psum | solution.py:52
  582.4 165.8 %all-reduce.19.cloned.1.call-start = ((), (), s32[]{:S(2)}) async-start(), calls=%async_computation.5 | async-start | bytes 2097152 | tf_op jit(solution)/shard_map/psum | solution.py:60
  686.6 104.3 %copy-start.1 = (f32[2048,128]{1,0:T(8,128)S(1)}, f32[2048,128]{1,0:T(8,128)}, u32[]{:S(2)}) copy-start(f32[2048,128]{1,0:T(8,128)} %get-tuple-element.21) | copy-start | bytes 3145732
Sparse Core Ops, SparseCore 0:
  59.0 64.4 all-reduce.8
  176.9 50.9 all-reduce.10
  322.0 61.0 all-reduce.12
  436.4 50.9 all-reduce.14
  582.6 61.1 all-reduce.16
  697.2 50.9 all-reduce.18
where the time goes:
time: 810 us; the launch traced here: 802 us
  waiting for transfers between devices  338 us (42%)
  local copies, waits for them, and re-layouts  162 us (20%)
  matrix products  141 us (17%)
  blocking collectives  121 us (15%)
  other arithmetic  24.7 us (3%)
  between operations  14.7 us (2%)
    psum x3, waiting for transfers between devices, on_device(): projected = lax.psum(partial_rows, 'col')  185 us
    psum x3, waiting for transfers between devices, on_device(): lax.psum(summed.reshape(feature_rows, directions), 'row')  153 us
    psum x2, blocking collectives, on_device(): lax.psum((jnp.sum(own_rows(direction) * own_image, axis=0), jnp.sum(own_r...  80.2 us
    dot_general x3, local copies, waits for them, and re-layouts, on_device(): jnp.einsum('bij,bjk->bik', x_blocks, picked_tiles, preferred_element_type...  52.4 us
    dot_general x3, local copies, waits for them, and re-layouts, on_device(): jnp.einsum('bji,bjk->bik', x_blocks, picked_rows, preferred_element_type=...  52.4 us
    dot_general x3, matrix products, on_device(): jnp.einsum('bji,bjk->bik', x_blocks, picked_rows, preferred_element_type=...  43.1 us
    psum x1, blocking collectives, on_device(): norm_now = lax.psum(jnp.sum(mine * mine, axis=0), ('row', 'col'))  40.4 us
    dot_general x3, matrix products, on_device(): jnp.einsum('bij,bjk->bik', x_blocks, picked_tiles, preferred_element_type...  38.5 us
  transfers between devices with their start and end apart: 6, of which 6 were waited for; matrix products, arithmetic and copies ran while one was open for 0% of the time, Pallas kernels for 0%

commit v1 on v0

v1 whole, which is shorter than its diff:
```python
import functools

import jax
import jax.numpy as jnp
from jax import lax
from jax.experimental import pallas as pl
from jax.experimental.pallas import tpu as pltpu
from jax.sharding import PartitionSpec as P

ITERS = 3
RIDGE = 0.2
GROUP = 16
TAIL = 16

f32 = jnp.float32
bf16 = jnp.bfloat16
VMEM = pl.BlockSpec(memory_space=pltpu.VMEM)
SMEM = pl.BlockSpec(memory_space=pltpu.SMEM)


def tree(values):
    while len(values) > 1:
        values = [values[i] + values[i + 1] for i in range(0, len(values), 2)]
    return values[0]


def to_tail(sums):
    rows = lax.broadcasted_iota(jnp.int32, (TAIL, sums[0].shape[1]), 0)
    tile = jnp.zeros(rows.shape, f32)
    for position, value in enumerate(sums):
        for part in range(3):
            piece = value.astype(bf16).astype(f32)
            tile = jnp.where(rows == 3 * position + part, piece, tile)
            value = value - piece
    return tile.astype(bf16)


def from_tail(tile, position=0):
    start = 3 * position
    return tile[start : start + 1] + tile[start + 1 : start + 2] + tile[start + 2 : start + 3]


def tail_of(ref):
    rows = ref.shape[0]
    return ref[rows - TAIL : rows, :].astype(f32)


def column_sum(value):
    return jnp.sum(value, axis=0, keepdims=True)


def forward_kernel(cfg, tails, *refs):
    pieces = len(refs) - 9
    place, ids, x = refs[:3]
    parts = refs[3 : 3 + pieces]
    send, keep, keep_tail, full, held, total = refs[3 + pieces :]
    fb, rb, nb, zb, width = cfg["fb"], cfg["rb"], cfg["nb"], cfg["zb"], cfg["width"]
    chips = cfg["cols"] // 2
    c, z = place[0], place[1]
    if pieces == 1:
        held[...] = parts[0][...].astype(bf16).reshape(held.shape)
    else:
        for k, part in enumerate(parts):
            held[pl.ds((z ^ k) * zb, zb)] = part[: zb * width, :].reshape((zb, width, -1))
    total[...] = jnp.zeros_like(total)

    def step(i, carry):
        products = []
        for u in range(GROUP):
            k = i * GROUP + u
            a = ids[k] // fb
            b = ids[k] - a * fb
            slot = a // nb
            relative = slot ^ c
            target = ((relative & 1) * chips + (relative >> 1)) * nb + (a - slot * nb)
            products.append((target, jnp.dot(x[k], held[b], preferred_element_type=f32)))
        for target, product in products:
            total[target] = total[target] + product
        return carry

    lax.fori_loop(0, x.shape[0] // GROUP, step, 0)
    half = rb // 2
    rows = half * width
    keep[...] = total[:half].reshape(keep.shape)
    send[:rows, :] = total[half:].reshape(keep.shape).astype(bf16)
    if tails:
        tile = to_tail([from_tail(tree([tail_of(part) for part in parts]))])
        send[rows:, :] = tile
        keep_tail[...] = tile
    else:
        send[rows:, :] = jnp.zeros((TAIL, send.shape[1]), bf16)
        keep_tail[...] = jnp.zeros(keep_tail.shape, bf16)
    if pieces > 1:
        full[...] = held[...].reshape(full.shape)
    else:
        full[...] = jnp.zeros_like(full)


def merge_kernel(cfg, *refs):
    keep, keep_tail, received, own, own_tail = refs[:5]
    sends = refs[5:]
    rows = cfg["nb"] * cfg["width"]
    tile = keep_tail[...].astype(f32) + tail_of(received)
    tile = to_tail([from_tail(tile)])
    own[...] = keep[:rows, :] + received[:rows, :].astype(f32)
    own_tail[...] = tile
    for k, send in enumerate(sends, start=1):
        span = slice(k * rows, (k + 1) * rows)
        send[:rows, :] = (keep[span, :] + received[span, :].astype(f32)).astype(bf16)
        send[rows:, :] = tile


def scale_kernel(cfg, first, *refs):
    chips = cfg["cols"] // 2
    own, own_tail = refs[:2]
    received = refs[2 : 1 + chips]
    rest = refs[1 + chips :]
    rows = own.shape[0]
    projected = tree([own[...]] + [r[:rows, :].astype(f32) for r in received])
    if first:
        weights, direction, scaled, kept, spread = rest
        width = cfg["width"]
        for j in range(cfg["nb"]):
            row = jnp.broadcast_to(weights[j : j + 1, :], (width, width))
            spread[j * width : (j + 1) * width, :] = row.T
        d = direction[...]
        norm = column_sum(d * d)
    else:
        spread, residual, old, before, norm_now, scaled, kept, direction, norm_out, beta_out = rest
        tile = tree([own_tail[...].astype(f32)] + [tail_of(r) for r in received])
        norm = from_tail(tile)
        beta = norm / norm_now[0:1, :]
        projected = projected + beta * before[...]
        d = residual[...] + beta * old[...]
        direction[...] = d
        norm_out[...] = jnp.broadcast_to(norm, norm_out.shape)
        beta_out[...] = jnp.broadcast_to(beta, beta_out.shape)
    kept[...] = projected
    weighted = spread[...] * projected
    scaled[:rows, :] = weighted.astype(bf16)
    curvature = column_sum(weighted * projected) + RIDGE * column_sum(d * d)
    scaled[rows:, :] = to_tail([curvature, norm] if first else [curvature])


def backward_kernel(cfg, first, *refs):
    cols, rows_axis = cfg["cols"], cfg["rows"]
    place, ids, x = refs[:3]
    parts = refs[3 : 3 + cols]
    own, own_tail = refs[3 + cols : 5 + cols]
    sends = refs[5 + cols : 4 + cols + rows_axis]
    held, total = refs[4 + cols + rows_axis :]
    fb, nb, zb, width = cfg["fb"], cfg["nb"], cfg["zb"], cfg["width"]
    c, z = place[0], place[1]
    for k, part in enumerate(parts):
        held[pl.ds((c ^ k) * nb, nb)] = part[: nb * width, :].reshape((nb, width, -1))
    total[...] = jnp.zeros_like(total)

    def step(i, carry):
        products = []
        for u in range(GROUP):
            k = i * GROUP + u
            a = ids[k] // fb
            b = ids[k] - a * fb
            slot = b // zb
            target = (slot ^ z) * zb + (b - slot * zb)
            product = lax.dot_general(
                x[k], held[a], (((0,), (0,)), ((), ())), preferred_element_type=f32
            )
            products.append((target, product))
        for target, product in products:
            total[target] = total[target] + product
        return carry

    lax.fori_loop(0, x.shape[0] // GROUP, step, 0)
    tile = tree([tail_of(part) for part in parts])
    tile = to_tail([from_tail(tile, j) for j in range(2 if first else 1)])
    span = zb * width
    own[...] = total[:zb].reshape(own.shape)
    own_tail[...] = tile
    for k, send in enumerate(sends, start=1):
        send[:span, :] = total[k * zb : (k + 1) * zb].reshape(own.shape).astype(bf16)
        send[span:, :] = tile


def update_kernel(cfg, first, *refs):
    others = cfg["rows"] - 1
    own, own_tail = refs[:2]
    received = refs[2 : 2 + others]
    direction, residual, norm_now, share, after, norm_out, alpha_out = refs[2 + others :]
    rows = own.shape[0]
    image = tree([own[...]] + [r[:rows, :].astype(f32) for r in received])
    image = image + RIDGE * direction[...]
    tile = tree([own_tail[...].astype(f32)] + [tail_of(r) for r in received])
    norm = from_tail(tile, 1) if first else norm_now[0:1, :]
    alpha = norm / from_tail(tile)
    left = residual[...] - alpha * image
    after[...] = left
    norm_out[...] = jnp.broadcast_to(norm, norm_out.shape)
    alpha_out[...] = jnp.broadcast_to(alpha, alpha_out.shape)
    share[:rows, :] = left.astype(bf16)
    share[rows:, :] = to_tail([column_sum(left * left)])


def result_kernel(count, *refs):
    grads = refs[0]
    residuals = refs[1:count]
    alphas = refs[count : 2 * count]
    betas = refs[2 * count : 3 * count - 1]
    out = refs[3 * count - 1]
    d = grads[...]
    total = alphas[0][0:1, :] * d
    for j in range(1, count):
        d = residuals[j - 1][...].astype(f32) + betas[j - 1][0:1, :] * d
        total = total + alphas[j][0:1, :] * d
    out[...] = total


def on_device(cfg, x_blocks, block_ids, margins, deleted, grads):
    width = x_blocks.shape[1]
    directions = grads.shape[1]
    cols, rows_axis = cfg["cols"], cfg["rows"]
    rb, fb = margins.shape[0] // width, grads.shape[0] // width
    nb, zb = rb // cols, fb // rows_axis
    cfg = dict(cfg, rb=rb, fb=fb, nb=nb, zb=zb, width=width)
    c, z = lax.axis_index("col"), lax.axis_index("row")
    place = jnp.stack([c, z]).astype(jnp.int32)
    ids = block_ids[:, 0]
    own_rows, own_features = nb * width, zb * width
    chips = cols // 2

    def shape(rows, dtype):
        return jax.ShapeDtypeStruct((rows, directions), dtype)

    def along_col(value, k):
        return lax.ppermute(value, "col", [(i, i ^ k) for i in range(cols)])

    def along_row(value, k):
        return lax.ppermute(value, "row", [(i, i ^ k) for i in range(rows_axis)])

    def call(kernel, out, inputs, smem=0, scratch=()):
        return pl.pallas_call(
            kernel,
            out_shape=out,
            in_specs=[SMEM] * smem + [VMEM] * (len(inputs) - smem),
            out_specs=[VMEM] * len(out),
            scratch_shapes=list(scratch),
        )(*inputs)

    row_ids = z * margins.shape[0] + c * own_rows + jnp.arange(own_rows, dtype=jnp.int32)
    row_ids = row_ids.reshape(nb, width)
    removed = jnp.any(row_ids[None] == deleted[:, None, None], axis=0)
    logistic = jax.nn.sigmoid(lax.dynamic_slice_in_dim(margins, c * own_rows, own_rows))
    logistic = logistic.reshape(nb, width)
    weights = jnp.where(removed, 0.0, logistic * (1.0 - logistic))

    residual = direction = lax.dynamic_slice_in_dim(grads, z * own_features, own_features)
    parts = [grads]
    residuals, alphas, betas = [], [], []
    norm_now = spread = before = None
    for iteration in range(ITERS):
        first = iteration == 0
        send, keep, keep_tail, full = call(
            functools.partial(forward_kernel, cfg, not first),
            [
                shape(rb // 2 * width + TAIL, bf16),
                shape(rb // 2 * width, f32),
                shape(TAIL, bf16),
                shape(fb * width if not first else TAIL, bf16),
            ],
            [place, ids, x_blocks, *parts],
            smem=2,
            scratch=[
                pltpu.VMEM((fb, width, directions), bf16),
                pltpu.VMEM((rb, width, directions), f32),
            ],
        )
        if not first:
            residuals.append(full)
        received = along_col(send, 1)
        own, own_tail, *sends = call(
            functools.partial(merge_kernel, cfg),
            [shape(own_rows, f32), shape(TAIL, bf16)]
            + [shape(own_rows + TAIL, bf16)] * (chips - 1),
            [keep, keep_tail, received],
        )
        received = [along_col(send, 2 * k) for k, send in enumerate(sends, start=1)]
        if first:
            scaled, before, spread = call(
                functools.partial(scale_kernel, cfg, True),
                [shape(own_rows + TAIL, bf16), shape(own_rows, f32), shape(own_rows, f32)],
                [own, own_tail, *received, weights, direction],
            )
        else:
            scaled, before, direction, norm_now, beta = call(
                functools.partial(scale_kernel, cfg, False),
                [
                    shape(own_rows + TAIL, bf16),
                    shape(own_rows, f32),
                    shape(own_features, f32),
                    shape(8, f32),
                    shape(8, f32),
                ],
                [own, own_tail, *received, spread, residual, direction, before, norm_now],
            )
            betas.append(beta)
        chip_parts = [scaled] + [along_col(scaled, 2 * k) for k in range(1, chips)]
        parts = [p for part in chip_parts for p in (part, along_col(part, 1))]
        own, own_tail, *sends = call(
            functools.partial(backward_kernel, cfg, first),
            [shape(own_features, f32), shape(TAIL, bf16)]
            + [shape(own_features + TAIL, bf16)] * (rows_axis - 1),
            [place, ids, x_blocks, *parts],
            smem=2,
            scratch=[
                pltpu.VMEM((rb, width, directions), bf16),
                pltpu.VMEM((fb, width, directions), f32),
            ],
        )
        received = [along_row(send, k) for k, send in enumerate(sends, start=1)]
        if first:
            norm_now = jnp.zeros((8, directions), f32)
        share, residual, norm_now, alpha = call(
            functools.partial(update_kernel, cfg, first),
            [
                shape(own_features + TAIL, bf16),
                shape(own_features, f32),
                shape(8, f32),
                shape(8, f32),
            ],
            [own, own_tail, *received, direction, residual, norm_now],
        )
        alphas.append(alpha)
        parts = [share] + [along_row(share, k) for k in range(1, rows_axis)]
    (answer,) = call(
        functools.partial(result_kernel, ITERS),
        [shape(fb * width, f32)],
        [grads, *residuals, *alphas, *betas],
    )
    left = jnp.zeros((rows_axis, own_features, directions), f32)
    left = jnp.stack([p[:own_features].astype(f32) for p in parts])
    order = jnp.arange(rows_axis, dtype=jnp.int32) ^ z
    left = left[order].reshape(fb * width, directions)
    return (answer, left)


def solution(mesh):
    cfg = {"rows": mesh.shape["row"], "cols": mesh.shape["col"]}
    placed = (P("row", "col", None), P("row", "col"), P("row"), P("row"), P("col", None))
    return jax.shard_map(
        functools.partial(on_device, cfg),
        mesh=mesh,
        in_specs=placed,
        out_specs=(P("col", None), P("col", None)),
        check_vma=False,
    )
```

time: 810 us -> 258 us (0.32)
  waiting for transfers between devices: 338 us -> 98.3 us
  local copies, waits for them, and re-layouts: 162 us -> 16.7 us
  matrix products: 141 us -> 0 us
  blocking collectives: 121 us -> 0 us
  Pallas kernels: 0 us -> 88.3 us
  starting transfers between devices: 0.88 us -> 51 us
  other arithmetic: 24.7 us -> 2.31 us
  between operations: 14.7 us -> 0.94 us
    psum x6 -> x0, waiting for transfers between devices: 338 us -> none  [the longest x3 185 us: on_device(): projected = lax.psum(partial_rows, 'col')]
    dot_general x12 -> x0, matrix products: 141 us -> none  [the longest x3 43.1 us: on_device(): jnp.einsum('bji,bjk->bik', x_blocks, picked_rows, preferred_element_type=...]
    psum x3 -> x0, blocking collectives: 121 us -> none  [the longest x2 80.2 us: on_device(): lax.psum((jnp.sum(own_rows(direction) * own_image, axis=0), jnp.sum(own_r...]
    dot_general x9 -> x0, local copies, waits for them, and re-layouts: 109 us -> none  [the longest x3 52.4 us: on_device(): jnp.einsum('bij,bjk->bik', x_blocks, picked_tiles, preferred_element_type...]
    ppermute x0 -> x51, waiting for transfers between devices: none -> 98.3 us  [the longest x18 57.6 us: along_row(): return lax.ppermute(value, 'row', [(i, i ^ k) for i in range(rows_axis)])]
    pallas_call x0 -> x16, Pallas kernels: none -> 88.3 us  [call(): pl.pallas_call(kernel, out_shape=out, in_specs=[SMEM] * smem + [VMEM] * (...]
    ppermute x0 -> x51, starting transfers between devices: none -> 51 us  [the longest x18 27.2 us: along_row(): return lax.ppermute(value, 'row', [(i, i ^ k) for i in range(rows_axis)])]
    gather x6 -> x1, local copies, waits for them, and re-layouts: 51.6 us -> 1.58 us  [on_device(): left = left[order].reshape(fb * width, directions)]
  transfers between devices with their start and end apart: 6 -> 51, of which waited for: 6 -> 31; matrix products, arithmetic and copies ran while one was open for 0% -> 2% of each run, Pallas kernels for 0% -> 1%
where the time goes in v1:
time: 258 us; the launch traced here: 257 us
  waiting for transfers between devices  98.3 us (38%)
  Pallas kernels  88.3 us (34%)
  starting transfers between devices  51 us (20%)
  local copies, waits for them, and re-layouts  16.7 us (6%)
    pallas_call x16, Pallas kernels, call(): pl.pallas_call(kernel, out_shape=out, in_specs=[SMEM] * smem + [VMEM] * (...  88.3 us
    ppermute x18, waiting for transfers between devices, along_row(): return lax.ppermute(value, 'row', [(i, i ^ k) for i in range(rows_axis)])  57.6 us
    ppermute x33, waiting for transfers between devices, along_col(): return lax.ppermute(value, 'col', [(i, i ^ k) for i in range(cols)])  40.6 us
    ppermute x18, starting transfers between devices, along_row(): return lax.ppermute(value, 'row', [(i, i ^ k) for i in range(rows_axis)])  27.2 us
    ppermute x33, starting transfers between devices, along_col(): return lax.ppermute(value, 'col', [(i, i ^ k) for i in range(cols)])  23.8 us
    unnamed x98, local copies, waits for them, and re-layouts  11.9 us
  transfers between devices with their start and end apart: 51, of which 31 were waited for; matrix products, arithmetic and copies ran while one was open for 2% of the time, Pallas kernels for 1%

profile of v1, /device:TPU:0, one launch (start us, length us, event | category | flops | bytes accessed | tf_op | source)
XLA Modules:
  0.0 257.5 jit_solution(15660329609852356344)
XLA Ops:
  1.3 10.8 %shard_map.68 = (bf16[2064,128]{1,0:T(8,128)(2,1)}, f32[2048,128]{1,0:T(8,128)}, bf16[16,128]{1,0:T(8,128)(2,1)}, bf16[16,128]{1,0:T(8,128)(2,1)}) custom-call(s32[2]{0:T(128)} %pad_add_fusion.refs_0_, s32[256]{0:T(256)} %bitcast.17, bf16[256,128,128]{2,1,0:T(8,128)(2,1)} %refs_2_.11, f32[2048,128]{1,0:T(8,128)} %refs_0_.1), custom_call_target="tpu_custom_call" | custom-call | tf_op jit(solution)/shard_map/pallas_call | solution.py:241
  15.1 2.2 shard_map.69
  17.4 2.8 %collective-permute-start.1 = (bf16[528,128]{1,0:T(8,128)(2,1)}, bf16[528,128]{1,0:T(8,128)(2,1)S(1)}, u32[]{:S(2)}, u32[]{:S(2)}) collective-permute-start(bf16[528,128]{1,0:T(8,128)(2,1)} %get-tuple-element.70), channel_id=1, source_target_pairs={{0,2},{1,3},{2,0},{3,1},{4,6},{5,7},{6,4},{7,5},{8,10},{9,11},{10,... | collective-permute-start | bytes 405512 | tf_op jit(solution)/shard_map/ppermute | solution.py:235
  23.1 1.7 constant_dynamic-slice_fusion.refs_6_.refs_5_.refs_7_
  24.8 3.9 %collective-permute-done.2.refs_3_ = bf16[528,128]{1,0:T(8,128)(2,1)S(1)} collective-permute-done((bf16[528,128]{1,0:T(8,128)(2,1)}, bf16[528,128]{1,0:T(8,128)(2,1)S(1)}, u32[]{:S(2)}, u32[]{:S(2)}) %collective-permute-start.2) | collective-permute-done | bytes 135200 | tf_op jit(solution)/shard_map/ppermute | solution.py:235
  29.4 2.2 shard_map.70
  35.0 2.8 %collective-permute-done.5.refs_5_ = bf16[528,128]{1,0:T(8,128)(2,1)S(1)} collective-permute-done((bf16[528,128]{1,0:T(8,128)(2,1)}, bf16[528,128]{1,0:T(8,128)(2,1)S(1)}, u32[]{:S(2)}, u32[]{:S(2)}) %collective-permute-start.5) | collective-permute-done | bytes 135200 | tf_op jit(solution)/shard_map/ppermute | solution.py:235
  37.8 2.5 collective-permute-done.7.refs_7_
  43.0 10.9 %shard_map.71 = (f32[512,128]{1,0:T(8,128)}, bf16[16,128]{1,0:T(8,128)(2,1)}, bf16[528,128]{1,0:T(8,128)(2,1)}, bf16[528,128]{1,0:T(8,128)(2,1)}, bf16[528,128]{1,0:T(8,128)(2,1)}) custom-call(s32[2]{0:T(128)} %pad_add_fusion.refs_0_, s32[256]{0:T(256)} %bitcast.18, bf16[256,128,128]{2,1,0:T(8,128)(2,1)} %refs_2_.11, ...), custom_call_target="tpu_custom_call" | custom-call | tf_op jit(solution)/shard_map/pallas_call | solution.py:241
  55.4 2.6 %collective-permute-start.12 = (bf16[528,128]{1,0:T(8,128)(2,1)}, bf16[528,128]{1,0:T(8,128)(2,1)S(1)}, u32[]{:S(2)}, u32[]{:S(2)}) collective-permute-start(bf16[528,128]{1,0:T(8,128)(2,1)} %get-tuple-element.77), channel_id=1, source_target_pairs={{0,16},{8,24},{16,0},{24,8},{1,17},{9,25},{17,1},{25,9},{2,18},{10... | collective-permute-start | bytes 405512 | tf_op jit(solution)/shard_map/ppermute | solution.py:238
  58.3 3.5 %collective-permute-done.11.refs_2_ = bf16[528,128]{1,0:T(8,128)(2,1)S(1)} collective-permute-done((bf16[528,128]{1,0:T(8,128)(2,1)}, bf16[528,128]{1,0:T(8,128)(2,1)S(1)}, u32[]{:S(2)}, u32[]{:S(2)}) %collective-permute-start.11) | collective-permute-done | bytes 135200 | tf_op jit(solution)/shard_map/ppermute | solution.py:238
  61.8 7.0 %collective-permute-done.12.refs_3_ = bf16[528,128]{1,0:T(8,128)(2,1)S(1)} collective-permute-done((bf16[528,128]{1,0:T(8,128)(2,1)}, bf16[528,128]{1,0:T(8,128)(2,1)S(1)}, u32[]{:S(2)}, u32[]{:S(2)}) %collective-permute-start.12) | collective-permute-done | bytes 135200 | tf_op jit(solution)/shard_map/ppermute | solution.py:238
  69.5 2.1 shard_map.72
  71.7 2.3 collective-permute-start.14
  76.5 2.2 collective-permute-done.14.refs_4_
  78.7 8.0 %collective-permute-done.15.refs_5_ = bf16[528,128]{1,0:T(8,128)(2,1)S(1)} collective-permute-done((bf16[528,128]{1,0:T(8,128)(2,1)}, bf16[528,128]{1,0:T(8,128)(2,1)S(1)}, u32[]{:S(2)}, u32[]{:S(2)}) %collective-permute-start.15) | collective-permute-done | bytes 135200 | tf_op jit(solution)/shard_map/ppermute | solution.py:238
  88.0 11.0 %shard_map.73 = (bf16[2064,128]{1,0:T(8,128)(2,1)}, f32[2048,128]{1,0:T(8,128)}, bf16[16,128]{1,0:T(8,128)(2,1)}, bf16[2048,128]{1,0:T(8,128)(2,1)}) custom-call(s32[2]{0:T(128)} %pad_add_fusion.refs_0_, s32[256]{0:T(256)} %bitcast.19, bf16[256,128,128]{2,1,0:T(8,128)(2,1)} %refs_2_.11, bf16[528,128]{1,0:T(8,128)(2,1)} %get-tuple-element.79.refs_3_, ...), custom_call_target="tpu_custom_call" | custom-call | tf_op jit(solution)/shard_map/pallas_call | solution.py:241
  99.0 2.1 collective-permute-done.17.refs_2_
  101.9 2.2 shard_map.74
  107.6 3.0 %collective-permute-done.18.refs_2_ = bf16[528,128]{1,0:T(8,128)(2,1)S(1)} collective-permute-done((bf16[528,128]{1,0:T(8,128)(2,1)}, bf16[528,128]{1,0:T(8,128)(2,1)S(1)}, u32[]{:S(2)}, u32[]{:S(2)}) %collective-permute-start.18) | collective-permute-done | bytes 135200 | tf_op jit(solution)/shard_map/ppermute | solution.py:235
  110.7 3.2 %collective-permute-done.19.refs_3_ = bf16[528,128]{1,0:T(8,128)(2,1)S(1)} collective-permute-done((bf16[528,128]{1,0:T(8,128)(2,1)}, bf16[528,128]{1,0:T(8,128)(2,1)S(1)}, u32[]{:S(2)}, u32[]{:S(2)}) %collective-permute-start.19) | collective-permute-done | bytes 135200 | tf_op jit(solution)/shard_map/ppermute | solution.py:235
  114.6 2.3 shard_map.75
  120.4 3.0 %collective-permute-done.22.refs_5_ = bf16[528,128]{1,0:T(8,128)(2,1)S(1)} collective-permute-done((bf16[528,128]{1,0:T(8,128)(2,1)}, bf16[528,128]{1,0:T(8,128)(2,1)S(1)}, u32[]{:S(2)}, u32[]{:S(2)}) %collective-permute-start.22) | collective-permute-done | bytes 135200 | tf_op jit(solution)/shard_map/ppermute | solution.py:235
  123.4 2.2 collective-permute-done.24.refs_7_
  128.3 10.9 %shard_map.76 = (f32[512,128]{1,0:T(8,128)}, bf16[16,128]{1,0:T(8,128)(2,1)}, bf16[528,128]{1,0:T(8,128)(2,1)}, bf16[528,128]{1,0:T(8,128)(2,1)}, bf16[528,128]{1,0:T(8,128)(2,1)}) custom-call(s32[2]{0:T(128)} %pad_add_fusion.refs_0_, s32[256]{0:T(256)} %bitcast.20, bf16[256,128,128]{2,1,0:T(8,128)(2,1)} %refs_2_.11, ...), custom_call_target="tpu_custom_call" | custom-call | tf_op jit(solution)/shard_map/pallas_call | solution.py:241
  141.6 1.9 collective-permute-start.30
  143.5 3.6 %collective-permute-done.28.refs_2_ = bf16[528,128]{1,0:T(8,128)(2,1)S(1)} collective-permute-done((bf16[528,128]{1,0:T(8,128)(2,1)}, bf16[528,128]{1,0:T(8,128)(2,1)S(1)}, u32[]{:S(2)}, u32[]{:S(2)}) %collective-permute-start.28) | collective-permute-done | bytes 135200 | tf_op jit(solution)/shard_map/ppermute | solution.py:238
  147.1 6.7 %collective-permute-done.29.refs_3_ = bf16[528,128]{1,0:T(8,128)(2,1)S(1)} collective-permute-done((bf16[528,128]{1,0:T(8,128)(2,1)}, bf16[528,128]{1,0:T(8,128)(2,1)S(1)}, u32[]{:S(2)}, u32[]{:S(2)}) %collective-permute-start.29) | collective-permute-done | bytes 135200 | tf_op jit(solution)/shard_map/ppermute | solution.py:238
  154.6 2.1 shard_map.77
  156.7 2.4 collective-permute-start.31
  161.5 2.2 collective-permute-done.31.refs_4_
  163.7 8.0 %collective-permute-done.32.refs_5_ = bf16[528,128]{1,0:T(8,128)(2,1)S(1)} collective-permute-done((bf16[528,128]{1,0:T(8,128)(2,1)}, bf16[528,128]{1,0:T(8,128)(2,1)S(1)}, u32[]{:S(2)}, u32[]{:S(2)}) %collective-permute-start.32) | collective-permute-done | bytes 135200 | tf_op jit(solution)/shard_map/ppermute | solution.py:238
  173.0 11.0 %shard_map.78 = (bf16[2064,128]{1,0:T(8,128)(2,1)}, f32[2048,128]{1,0:T(8,128)}, bf16[16,128]{1,0:T(8,128)(2,1)}, bf16[2048,128]{1,0:T(8,128)(2,1)}) custom-call(s32[2]{0:T(128)} %pad_add_fusion.refs_0_, s32[256]{0:T(256)} %bitcast.21, bf16[256,128,128]{2,1,0:T(8,128)(2,1)} %refs_2_.11, bf16[528,128]{1,0:T(8,128)(2,1)} %get-tuple-element.101.refs_3_, ...), custom_call_target="tpu_custom_call" | custom-call | tf_op jit(solution)/shard_map/pallas_call | solution.py:241
  184.0 2.1 collective-permute-done.34.refs_2_
  186.9 2.2 shard_map.79
  192.6 3.2 %collective-permute-done.35.refs_2_ = bf16[528,128]{1,0:T(8,128)(2,1)S(1)} collective-permute-done((bf16[528,128]{1,0:T(8,128)(2,1)}, bf16[528,128]{1,0:T(8,128)(2,1)S(1)}, u32[]{:S(2)}, u32[]{:S(2)}) %collective-permute-start.35) | collective-permute-done | bytes 135200 | tf_op jit(solution)/shard_map/ppermute | solution.py:235
  195.8 2.8 %collective-permute-done.36.refs_3_ = bf16[528,128]{1,0:T(8,128)(2,1)S(1)} collective-permute-done((bf16[528,128]{1,0:T(8,128)(2,1)}, bf16[528,128]{1,0:T(8,128)(2,1)S(1)}, u32[]{:S(2)}, u32[]{:S(2)}) %collective-permute-start.36) | collective-permute-done | bytes 135200 | tf_op jit(solution)/shard_map/ppermute | solution.py:235
  199.3 2.3 shard_map.80
  205.1 3.1 %collective-permute-done.39.refs_5_ = bf16[528,128]{1,0:T(8,128)(2,1)S(1)} collective-permute-done((bf16[528,128]{1,0:T(8,128)(2,1)}, bf16[528,128]{1,0:T(8,128)(2,1)S(1)}, u32[]{:S(2)}, u32[]{:S(2)}) %collective-permute-start.39) | collective-permute-done | bytes 135200 | tf_op jit(solution)/shard_map/ppermute | solution.py:235
  208.3 2.1 collective-permute-done.41.refs_7_
  213.1 10.9 %shard_map.81 = (f32[512,128]{1,0:T(8,128)}, bf16[16,128]{1,0:T(8,128)(2,1)}, bf16[528,128]{1,0:T(8,128)(2,1)}, bf16[528,128]{1,0:T(8,128)(2,1)}, bf16[528,128]{1,0:T(8,128)(2,1)}) custom-call(s32[2]{0:T(128)} %pad_add_fusion.refs_0_, s32[256]{0:T(256)} %bitcast.22, bf16[256,128,128]{2,1,0:T(8,128)(2,1)} %refs_2_.11, ...), custom_call_target="tpu_custom_call" | custom-call | tf_op jit(solution)/shard_map/pallas_call | solution.py:241
  226.4 1.9 collective-permute-start.47
  228.3 3.6 %collective-permute-done.45.refs_2_ = bf16[528,128]{1,0:T(8,128)(2,1)S(1)} collective-permute-done((bf16[528,128]{1,0:T(8,128)(2,1)}, bf16[528,128]{1,0:T(8,128)(2,1)S(1)}, u32[]{:S(2)}, u32[]{:S(2)}) %collective-permute-start.45) | collective-permute-done | bytes 135200 | tf_op jit(solution)/shard_map/ppermute | solution.py:238
  231.9 6.8 %collective-permute-done.46.refs_3_ = bf16[528,128]{1,0:T(8,128)(2,1)S(1)} collective-permute-done((bf16[528,128]{1,0:T(8,128)(2,1)}, bf16[528,128]{1,0:T(8,128)(2,1)S(1)}, u32[]{:S(2)}, u32[]{:S(2)}) %collective-permute-start.46) | collective-permute-done | bytes 135200 | tf_op jit(solution)/shard_map/ppermute | solution.py:238
  239.4 2.2 shard_map.82
  241.5 2.3 collective-permute-start.50
  245.9 2.9 %shard_map.83 = f32[2048,128]{1,0:T(8,128)} custom-call(f32[2048,128]{1,0:T(8,128)} %refs_0_.1, bf16[2048,128]{1,0:T(8,128)(2,1)} %get-tuple-element.80.refs_1_, bf16[2048,128]{1,0:T(8,128)(2,1)} %get-tuple-element.102.refs_2_, f32[8,128]{1,0:T(8,128)} %get-tuple-element.103.refs_3_, f32[8,128]{1,0:T(8,128)} %get-tuple-element.104.refs_4_, ...), custom_call_target="tpu_custom_call" | custom-call | tf_op jit(solution)/shard_map/pallas_call | solution.py:241
  249.7 6.0 %collective-permute-done.49 = bf16[528,128]{1,0:T(8,128)(2,1)S(1)} collective-permute-done((bf16[528,128]{1,0:T(8,128)(2,1)}, bf16[528,128]{1,0:T(8,128)(2,1)S(1)}, u32[]{:S(2)}, u32[]{:S(2)}) %collective-permute-start.49) | collective-permute-done | bytes 135200 | tf_op jit(solution)/shard_map/ppermute | solution.py:238
  (182 shorter events, 56.6 us)
Async XLA Ops:
  12.1 2.2 collective-permute-start
  17.4 7.4 %collective-permute-start.1 = (bf16[528,128]{1,0:T(8,128)(2,1)}, bf16[528,128]{1,0:T(8,128)(2,1)S(1)}, u32[]{:S(2)}, u32[]{:S(2)}) collective-permute-start(bf16[528,128]{1,0:T(8,128)(2,1)} %get-tuple-element.70), channel_id=1, source_target_pairs={{0,2},{1,3},{2,0},{3,1},{4,6},{5,7},{6,4},{7,5},{8,10},{9,11},{10,... | collective-permute-start | bytes 405512 | tf_op jit(solution)/shard_map/ppermute | solution.py:235
  20.2 8.5 %collective-permute-start.2 = (bf16[528,128]{1,0:T(8,128)(2,1)}, bf16[528,128]{1,0:T(8,128)(2,1)S(1)}, u32[]{:S(2)}, u32[]{:S(2)}) collective-permute-start(bf16[528,128]{1,0:T(8,128)(2,1)} %get-tuple-element.71), channel_id=1, source_target_pairs={{0,4},{1,5},{2,6},{3,7},{4,0},{5,1},{6,2},{7,3},{8,12},{9,13},{10,... | collective-permute-start | bytes 405512 | tf_op jit(solution)/shard_map/ppermute | solution.py:235
  21.8 6.9 %collective-permute-start.3 = (bf16[528,128]{1,0:T(8,128)(2,1)}, bf16[528,128]{1,0:T(8,128)(2,1)S(1)}, u32[]{:S(2)}, u32[]{:S(2)}) collective-permute-start(bf16[528,128]{1,0:T(8,128)(2,1)} %get-tuple-element.72), channel_id=1, source_target_pairs={{0,6},{1,7},{2,4},{3,5},{4,2},{5,3},{6,0},{7,1},{8,14},{9,15},{10,... | collective-permute-start | bytes 405512 | tf_op jit(solution)/shard_map/ppermute | solution.py:235
  31.5 6.3 %collective-permute-start.5 = (bf16[528,128]{1,0:T(8,128)(2,1)}, bf16[528,128]{1,0:T(8,128)(2,1)S(1)}, u32[]{:S(2)}, u32[]{:S(2)}) collective-permute-start(bf16[528,128]{1,0:T(8,128)(2,1)} %get-tuple-element.73.refs_3_), channel_id=1, source_target_pairs={{0,2},{1,3},{2,0},{3,1},{4,6},{5,7},{6,4},{7,5},{8,10},{9,11},{10,... | collective-permute-start | bytes 405512 | tf_op jit(solution)/shard_map/ppermute | solution.py:235
  32.7 7.6 %collective-permute-start.7 = (bf16[528,128]{1,0:T(8,128)(2,1)}, bf16[528,128]{1,0:T(8,128)(2,1)S(1)}, u32[]{:S(2)}, u32[]{:S(2)}) collective-permute-start(bf16[528,128]{1,0:T(8,128)(2,1)} %get-tuple-element.73.refs_3_), channel_id=1, source_target_pairs={{0,4},{1,5},{2,6},{3,7},{4,0},{5,1},{6,2},{7,3},{8,12},{9,13},{10,... | collective-permute-start | bytes 405512 | tf_op jit(solution)/shard_map/ppermute | solution.py:235
  33.6 6.8 %collective-permute-start.9 = (bf16[528,128]{1,0:T(8,128)(2,1)}, bf16[528,128]{1,0:T(8,128)(2,1)S(1)}, u32[]{:S(2)}, u32[]{:S(2)}) collective-permute-start(bf16[528,128]{1,0:T(8,128)(2,1)} %get-tuple-element.73.refs_3_), channel_id=1, source_target_pairs={{0,6},{1,7},{2,4},{3,5},{4,2},{5,3},{6,0},{7,1},{8,14},{9,15},{10,... | collective-permute-start | bytes 405512 | tf_op jit(solution)/shard_map/ppermute | solution.py:235
  35.0 5.8 %collective-permute-start.4 = (bf16[528,128]{1,0:T(8,128)(2,1)}, bf16[528,128]{1,0:T(8,128)(2,1)S(1)}, u32[]{:S(2)}, u32[]{:S(2)}) collective-permute-start(bf16[528,128]{1,0:T(8,128)(2,1)} %get-tuple-element.73.refs_3_), channel_id=1, source_target_pairs={{0,1},{1,0},{2,3},{3,2},{4,5},{5,4},{6,7},{7,6},{8,9},{9,8},{10,11... | collective-permute-start | bytes 405512 | tf_op jit(solution)/shard_map/ppermute | solution.py:235
  37.8 3.1 %collective-permute-start.6 = (bf16[528,128]{1,0:T(8,128)(2,1)S(1)}, bf16[528,128]{1,0:T(8,128)(2,1)S(1)}, u32[]{:S(2)}, u32[]{:S(2)}) collective-permute-start(bf16[528,128]{1,0:T(8,128)(2,1)S(1)} %collective-permute-done.5.refs_5_), channel_id=1, source_target_pairs={{0,1},{1,0},{2,3},{3,2},{4,5},{5,4},{6,7},{7,6},{8,9},{9,8},{10,11... | collective-permute-start | bytes 405512 | tf_op jit(solution)/shard_map/ppermute | solution.py:235
  40.4 1.5 collective-permute-start.10
  53.9 7.9 %collective-permute-start.11 = (bf16[528,128]{1,0:T(8,128)(2,1)}, bf16[528,128]{1,0:T(8,128)(2,1)S(1)}, u32[]{:S(2)}, u32[]{:S(2)}) collective-permute-start(bf16[528,128]{1,0:T(8,128)(2,1)} %get-tuple-element.76), channel_id=1, source_target_pairs={{0,8},{8,0},{16,24},{24,16},{1,9},{9,1},{17,25},{25,17},{2,10},{10... | collective-permute-start | bytes 405512 | tf_op jit(solution)/shard_map/ppermute | solution.py:238
  55.4 13.4 %collective-permute-start.12 = (bf16[528,128]{1,0:T(8,128)(2,1)}, bf16[528,128]{1,0:T(8,128)(2,1)S(1)}, u32[]{:S(2)}, u32[]{:S(2)}) collective-permute-start(bf16[528,128]{1,0:T(8,128)(2,1)} %get-tuple-element.77), channel_id=1, source_target_pairs={{0,16},{8,24},{16,0},{24,8},{1,17},{9,25},{17,1},{25,9},{2,18},{10... | collective-permute-start | bytes 405512 | tf_op jit(solution)/shard_map/ppermute | solution.py:238
  58.0 10.8 %collective-permute-start.13 = (bf16[528,128]{1,0:T(8,128)(2,1)}, bf16[528,128]{1,0:T(8,128)(2,1)S(1)}, u32[]{:S(2)}, u32[]{:S(2)}) collective-permute-start(bf16[528,128]{1,0:T(8,128)(2,1)} %get-tuple-element.78), channel_id=1, source_target_pairs={{0,24},{8,16},{16,8},{24,0},{1,25},{9,17},{17,9},{25,1},{2,26},{10... | collective-permute-start | bytes 405512 | tf_op jit(solution)/shard_map/ppermute | solution.py:238
  71.7 7.0 %collective-permute-start.14 = (bf16[528,128]{1,0:T(8,128)(2,1)}, bf16[528,128]{1,0:T(8,128)(2,1)S(1)}, u32[]{:S(2)}, u32[]{:S(2)}) collective-permute-start(bf16[528,128]{1,0:T(8,128)(2,1)} %get-tuple-element.79.refs_3_), channel_id=1, source_target_pairs={{0,8},{8,0},{16,24},{24,16},{1,9},{9,1},{17,25},{25,17},{2,10},{10... | collective-permute-start | bytes 405512 | tf_op jit(solution)/shard_map/ppermute | solution.py:238
  74.0 12.7 %collective-permute-start.15 = (bf16[528,128]{1,0:T(8,128)(2,1)}, bf16[528,128]{1,0:T(8,128)(2,1)S(1)}, u32[]{:S(2)}, u32[]{:S(2)}) collective-permute-start(bf16[528,128]{1,0:T(8,128)(2,1)} %get-tuple-element.79.refs_3_), channel_id=1, source_target_pairs={{0,16},{8,24},{16,0},{24,8},{1,17},{9,25},{17,1},{25,9},{2,18},{10... | collective-permute-start | bytes 405512 | tf_op jit(solution)/shard_map/ppermute | solution.py:238
  75.1 11.6 %collective-permute-start.16 = (bf16[528,128]{1,0:T(8,128)(2,1)}, bf16[528,128]{1,0:T(8,128)(2,1)S(1)}, u32[]{:S(2)}, u32[]{:S(2)}) collective-permute-start(bf16[528,128]{1,0:T(8,128)(2,1)} %get-tuple-element.79.refs_3_), channel_id=1, source_target_pairs={{0,24},{8,16},{16,8},{24,0},{1,25},{9,17},{17,9},{25,1},{2,26},{10... | collective-permute-start | bytes 405512 | tf_op jit(solution)/shard_map/ppermute | solution.py:238
  99.0 2.1 collective-permute-start.17
  104.1 6.5 %collective-permute-start.18 = (bf16[528,128]{1,0:T(8,128)(2,1)}, bf16[528,128]{1,0:T(8,128)(2,1)S(1)}, u32[]{:S(2)}, u32[]{:S(2)}) collective-permute-start(bf16[528,128]{1,0:T(8,128)(2,1)} %get-tuple-element.86), channel_id=1, source_target_pairs={{0,2},{1,3},{2,0},{3,1},{4,6},{5,7},{6,4},{7,5},{8,10},{9,11},{10,... | collective-permute-start | bytes 405512 | tf_op jit(solution)/shard_map/ppermute | solution.py:235
  105.4 8.5 %collective-permute-start.19 = (bf16[528,128]{1,0:T(8,128)(2,1)}, bf16[528,128]{1,0:T(8,128)(2,1)S(1)}, u32[]{:S(2)}, u32[]{:S(2)}) collective-permute-start(bf16[528,128]{1,0:T(8,128)(2,1)} %get-tuple-element.87), channel_id=1, source_target_pairs={{0,4},{1,5},{2,6},{3,7},{4,0},{5,1},{6,2},{7,3},{8,12},{9,13},{10,... | collective-permute-start | bytes 405512 | tf_op jit(solution)/shard_map/ppermute | solution.py:235
  106.3 7.5 %collective-permute-start.20 = (bf16[528,128]{1,0:T(8,128)(2,1)}, bf16[528,128]{1,0:T(8,128)(2,1)S(1)}, u32[]{:S(2)}, u32[]{:S(2)}) collective-permute-start(bf16[528,128]{1,0:T(8,128)(2,1)} %get-tuple-element.88), channel_id=1, source_target_pairs={{0,6},{1,7},{2,4},{3,5},{4,2},{5,3},{6,0},{7,1},{8,14},{9,15},{10,... | collective-permute-start | bytes 405512 | tf_op jit(solution)/shard_map/ppermute | solution.py:235
  116.9 6.5 %collective-permute-start.22 = (bf16[528,128]{1,0:T(8,128)(2,1)}, bf16[528,128]{1,0:T(8,128)(2,1)S(1)}, u32[]{:S(2)}, u32[]{:S(2)}) collective-permute-start(bf16[528,128]{1,0:T(8,128)(2,1)} %get-tuple-element.93.refs_3_), channel_id=1, source_target_pairs={{0,2},{1,3},{2,0},{3,1},{4,6},{5,7},{6,4},{7,5},{8,10},{9,11},{10,... | collective-permute-start | bytes 405512 | tf_op jit(solution)/shard_map/ppermute | solution.py:235
  117.7 7.9 %collective-permute-start.24 = (bf16[528,128]{1,0:T(8,128)(2,1)}, bf16[528,128]{1,0:T(8,128)(2,1)S(1)}, u32[]{:S(2)}, u32[]{:S(2)}) collective-permute-start(bf16[528,128]{1,0:T(8,128)(2,1)} %get-tuple-element.93.refs_3_), channel_id=1, source_target_pairs={{0,4},{1,5},{2,6},{3,7},{4,0},{5,1},{6,2},{7,3},{8,12},{9,13},{10,... | collective-permute-start | bytes 405512 | tf_op jit(solution)/shard_map/ppermute | solution.py:235
  118.9 6.7 %collective-permute-start.26 = (bf16[528,128]{1,0:T(8,128)(2,1)}, bf16[528,128]{1,0:T(8,128)(2,1)S(1)}, u32[]{:S(2)}, u32[]{:S(2)}) collective-permute-start(bf16[528,128]{1,0:T(8,128)(2,1)} %get-tuple-element.93.refs_3_), channel_id=1, source_target_pairs={{0,6},{1,7},{2,4},{3,5},{4,2},{5,3},{6,0},{7,1},{8,14},{9,15},{10,... | collective-permute-start | bytes 405512 | tf_op jit(solution)/shard_map/ppermute | solution.py:235
  120.4 5.7 %collective-permute-start.21 = (bf16[528,128]{1,0:T(8,128)(2,1)}, bf16[528,128]{1,0:T(8,128)(2,1)S(1)}, u32[]{:S(2)}, u32[]{:S(2)}) collective-permute-start(bf16[528,128]{1,0:T(8,128)(2,1)} %get-tuple-element.93.refs_3_), channel_id=1, source_target_pairs={{0,1},{1,0},{2,3},{3,2},{4,5},{5,4},{6,7},{7,6},{8,9},{9,8},{10,11... | collective-permute-start | bytes 405512 | tf_op jit(solution)/shard_map/ppermute | solution.py:235
  123.4 2.7 %collective-permute-start.23 = (bf16[528,128]{1,0:T(8,128)(2,1)S(1)}, bf16[528,128]{1,0:T(8,128)(2,1)S(1)}, u32[]{:S(2)}, u32[]{:S(2)}) collective-permute-start(bf16[528,128]{1,0:T(8,128)(2,1)S(1)} %collective-permute-done.22.refs_5_), channel_id=1, source_target_pairs={{0,1},{1,0},{2,3},{3,2},{4,5},{5,4},{6,7},{7,6},{8,9},{9,8},{10,11... | collective-permute-start | bytes 405512 | tf_op jit(solution)/shard_map/ppermute | solution.py:235
  125.6 1.5 collective-permute-start.27
  139.2 8.0 %collective-permute-start.28 = (bf16[528,128]{1,0:T(8,128)(2,1)}, bf16[528,128]{1,0:T(8,128)(2,1)S(1)}, u32[]{:S(2)}, u32[]{:S(2)}) collective-permute-start(bf16[528,128]{1,0:T(8,128)(2,1)} %get-tuple-element.96), channel_id=1, source_target_pairs={{0,8},{8,0},{16,24},{24,16},{1,9},{9,1},{17,25},{25,17},{2,10},{10... | collective-permute-start | bytes 405512 | tf_op jit(solution)/shard_map/ppermute | solution.py:238
  140.5 13.4 %collective-permute-start.29 = (bf16[528,128]{1,0:T(8,128)(2,1)}, bf16[528,128]{1,0:T(8,128)(2,1)S(1)}, u32[]{:S(2)}, u32[]{:S(2)}) collective-permute-start(bf16[528,128]{1,0:T(8,128)(2,1)} %get-tuple-element.97), channel_id=1, source_target_pairs={{0,16},{8,24},{16,0},{24,8},{1,17},{9,25},{17,1},{25,9},{2,18},{10... | collective-permute-start | bytes 405512 | tf_op jit(solution)/shard_map/ppermute | solution.py:238
  141.6 12.2 %collective-permute-start.30 = (bf16[528,128]{1,0:T(8,128)(2,1)}, bf16[528,128]{1,0:T(8,128)(2,1)S(1)}, u32[]{:S(2)}, u32[]{:S(2)}) collective-permute-start(bf16[528,128]{1,0:T(8,128)(2,1)} %get-tuple-element.98), channel_id=1, source_target_pairs={{0,24},{8,16},{16,8},{24,0},{1,25},{9,17},{17,9},{25,1},{2,26},{10... | collective-permute-start | bytes 405512 | tf_op jit(solution)/shard_map/ppermute | solution.py:238
  156.7 7.0 %collective-permute-start.31 = (bf16[528,128]{1,0:T(8,128)(2,1)}, bf16[528,128]{1,0:T(8,128)(2,1)S(1)}, u32[]{:S(2)}, u32[]{:S(2)}) collective-permute-start(bf16[528,128]{1,0:T(8,128)(2,1)} %get-tuple-element.101.refs_3_), channel_id=1, source_target_pairs={{0,8},{8,0},{16,24},{24,16},{1,9},{9,1},{17,25},{25,17},{2,10},{10... | collective-permute-start | bytes 405512 | tf_op jit(solution)/shard_map/ppermute | solution.py:238
  159.1 12.7 %collective-permute-start.32 = (bf16[528,128]{1,0:T(8,128)(2,1)}, bf16[528,128]{1,0:T(8,128)(2,1)S(1)}, u32[]{:S(2)}, u32[]{:S(2)}) collective-permute-start(bf16[528,128]{1,0:T(8,128)(2,1)} %get-tuple-element.101.refs_3_), channel_id=1, source_target_pairs={{0,16},{8,24},{16,0},{24,8},{1,17},{9,25},{17,1},{25,9},{2,18},{10... | collective-permute-start | bytes 405512 | tf_op jit(solution)/shard_map/ppermute | solution.py:238
  160.1 11.6 %collective-permute-start.33 = (bf16[528,128]{1,0:T(8,128)(2,1)}, bf16[528,128]{1,0:T(8,128)(2,1)S(1)}, u32[]{:S(2)}, u32[]{:S(2)}) collective-permute-start(bf16[528,128]{1,0:T(8,128)(2,1)} %get-tuple-element.101.refs_3_), channel_id=1, source_target_pairs={{0,24},{8,16},{16,8},{24,0},{1,25},{9,17},{17,9},{25,1},{2,26},{10... | collective-permute-start | bytes 405512 | tf_op jit(solution)/shard_map/ppermute | solution.py:238
  184.0 2.1 collective-permute-start.34
  189.1 6.7 %collective-permute-start.35 = (bf16[528,128]{1,0:T(8,128)(2,1)}, bf16[528,128]{1,0:T(8,128)(2,1)S(1)}, u32[]{:S(2)}, u32[]{:S(2)}) collective-permute-start(bf16[528,128]{1,0:T(8,128)(2,1)} %get-tuple-element.110), channel_id=1, source_target_pairs={{0,2},{1,3},{2,0},{3,1},{4,6},{5,7},{6,4},{7,5},{8,10},{9,11},{10,... | collective-permute-start | bytes 405512 | tf_op jit(solution)/shard_map/ppermute | solution.py:235
  190.1 8.5 %collective-permute-start.36 = (bf16[528,128]{1,0:T(8,128)(2,1)}, bf16[528,128]{1,0:T(8,128)(2,1)S(1)}, u32[]{:S(2)}, u32[]{:S(2)}) collective-permute-start(bf16[528,128]{1,0:T(8,128)(2,1)} %get-tuple-element.111), channel_id=1, source_target_pairs={{0,4},{1,5},{2,6},{3,7},{4,0},{5,1},{6,2},{7,3},{8,12},{9,13},{10,... | collective-permute-start | bytes 405512 | tf_op jit(solution)/shard_map/ppermute | solution.py:235
  191.3 7.3 %collective-permute-start.37 = (bf16[528,128]{1,0:T(8,128)(2,1)}, bf16[528,128]{1,0:T(8,128)(2,1)S(1)}, u32[]{:S(2)}, u32[]{:S(2)}) collective-permute-start(bf16[528,128]{1,0:T(8,128)(2,1)} %get-tuple-element.112), channel_id=1, source_target_pairs={{0,6},{1,7},{2,4},{3,5},{4,2},{5,3},{6,0},{7,1},{8,14},{9,15},{10,... | collective-permute-start | bytes 405512 | tf_op jit(solution)/shard_map/ppermute | solution.py:235
  201.6 6.6 %collective-permute-start.39 = (bf16[528,128]{1,0:T(8,128)(2,1)}, bf16[528,128]{1,0:T(8,128)(2,1)S(1)}, u32[]{:S(2)}, u32[]{:S(2)}) collective-permute-start(bf16[528,128]{1,0:T(8,128)(2,1)} %get-tuple-element.116.refs_3_), channel_id=1, source_target_pairs={{0,2},{1,3},{2,0},{3,1},{4,6},{5,7},{6,4},{7,5},{8,10},{9,11},{10,... | collective-permute-start | bytes 405512 | tf_op jit(solution)/shard_map/ppermute | solution.py:235
  202.7 7.7 %collective-permute-start.41 = (bf16[528,128]{1,0:T(8,128)(2,1)}, bf16[528,128]{1,0:T(8,128)(2,1)S(1)}, u32[]{:S(2)}, u32[]{:S(2)}) collective-permute-start(bf16[528,128]{1,0:T(8,128)(2,1)} %get-tuple-element.116.refs_3_), channel_id=1, source_target_pairs={{0,4},{1,5},{2,6},{3,7},{4,0},{5,1},{6,2},{7,3},{8,12},{9,13},{10,... | collective-permute-start | bytes 405512 | tf_op jit(solution)/shard_map/ppermute | solution.py:235
  203.7 6.7 %collective-permute-start.43 = (bf16[528,128]{1,0:T(8,128)(2,1)}, bf16[528,128]{1,0:T(8,128)(2,1)S(1)}, u32[]{:S(2)}, u32[]{:S(2)}) collective-permute-start(bf16[528,128]{1,0:T(8,128)(2,1)} %get-tuple-element.116.refs_3_), channel_id=1, source_target_pairs={{0,6},{1,7},{2,4},{3,5},{4,2},{5,3},{6,0},{7,1},{8,14},{9,15},{10,... | collective-permute-start | bytes 405512 | tf_op jit(solution)/shard_map/ppermute | solution.py:235
  205.1 5.8 %collective-permute-start.38 = (bf16[528,128]{1,0:T(8,128)(2,1)}, bf16[528,128]{1,0:T(8,128)(2,1)S(1)}, u32[]{:S(2)}, u32[]{:S(2)}) collective-permute-start(bf16[528,128]{1,0:T(8,128)(2,1)} %get-tuple-element.116.refs_3_), channel_id=1, source_target_pairs={{0,1},{1,0},{2,3},{3,2},{4,5},{5,4},{6,7},{7,6},{8,9},{9,8},{10,11... | collective-permute-start | bytes 405512 | tf_op jit(solution)/shard_map/ppermute | solution.py:235
  208.3 2.6 %collective-permute-start.40 = (bf16[528,128]{1,0:T(8,128)(2,1)S(1)}, bf16[528,128]{1,0:T(8,128)(2,1)S(1)}, u32[]{:S(2)}, u32[]{:S(2)}) collective-permute-start(bf16[528,128]{1,0:T(8,128)(2,1)S(1)} %collective-permute-done.39.refs_5_), channel_id=1, source_target_pairs={{0,1},{1,0},{2,3},{3,2},{4,5},{5,4},{6,7},{7,6},{8,9},{9,8},{10,11... | collective-permute-start | bytes 405512 | tf_op jit(solution)/shard_map/ppermute | solution.py:235
  210.4 1.5 collective-permute-start.44
  223.9 8.0 %collective-permute-start.45 = (bf16[528,128]{1,0:T(8,128)(2,1)}, bf16[528,128]{1,0:T(8,128)(2,1)S(1)}, u32[]{:S(2)}, u32[]{:S(2)}) collective-permute-start(bf16[528,128]{1,0:T(8,128)(2,1)} %get-tuple-element.119), channel_id=1, source_target_pairs={{0,8},{8,0},{16,24},{24,16},{1,9},{9,1},{17,25},{25,17},{2,10},{10... | collective-permute-start | bytes 405512 | tf_op jit(solution)/shard_map/ppermute | solution.py:238
  225.3 13.4 %collective-permute-start.46 = (bf16[528,128]{1,0:T(8,128)(2,1)}, bf16[528,128]{1,0:T(8,128)(2,1)S(1)}, u32[]{:S(2)}, u32[]{:S(2)}) collective-permute-start(bf16[528,128]{1,0:T(8,128)(2,1)} %get-tuple-element.120), channel_id=1, source_target_pairs={{0,16},{8,24},{16,0},{24,8},{1,17},{9,25},{17,1},{25,9},{2,18},{10... | collective-permute-start | bytes 405512 | tf_op jit(solution)/shard_map/ppermute | solution.py:238
  226.4 12.3 %collective-permute-start.47 = (bf16[528,128]{1,0:T(8,128)(2,1)}, bf16[528,128]{1,0:T(8,128)(2,1)S(1)}, u32[]{:S(2)}, u32[]{:S(2)}) collective-permute-start(bf16[528,128]{1,0:T(8,128)(2,1)} %get-tuple-element.121), channel_id=1, source_target_pairs={{0,24},{8,16},{16,8},{24,0},{1,25},{9,17},{17,9},{25,1},{2,26},{10... | collective-permute-start | bytes 405512 | tf_op jit(solution)/shard_map/ppermute | solution.py:238
  241.5 8.2 %collective-permute-start.50 = (bf16[528,128]{1,0:T(8,128)(2,1)}, bf16[528,128]{1,0:T(8,128)(2,1)S(1)}, u32[]{:S(2)}, u32[]{:S(2)}) collective-permute-start(bf16[528,128]{1,0:T(8,128)(2,1)} %get-tuple-element.127), channel_id=1, source_target_pairs={{0,24},{8,16},{16,8},{24,0},{1,25},{9,17},{17,9},{25,1},{2,26},{10... | collective-permute-start | bytes 405512 | tf_op jit(solution)/shard_map/ppermute | solution.py:238
  243.8 11.9 %collective-permute-start.49 = (bf16[528,128]{1,0:T(8,128)(2,1)}, bf16[528,128]{1,0:T(8,128)(2,1)S(1)}, u32[]{:S(2)}, u32[]{:S(2)}) collective-permute-start(bf16[528,128]{1,0:T(8,128)(2,1)} %get-tuple-element.127), channel_id=1, source_target_pairs={{0,16},{8,24},{16,0},{24,8},{1,17},{9,25},{17,1},{25,9},{2,18},{10... | collective-permute-start | bytes 405512 | tf_op jit(solution)/shard_map/ppermute | solution.py:238
  245.3 10.4 %collective-permute-start.48 = (bf16[528,128]{1,0:T(8,128)(2,1)}, bf16[528,128]{1,0:T(8,128)(2,1)S(1)}, u32[]{:S(2)}, u32[]{:S(2)}) collective-permute-start(bf16[528,128]{1,0:T(8,128)(2,1)} %get-tuple-element.127), channel_id=1, source_target_pairs={{0,8},{8,0},{16,24},{24,16},{1,9},{9,1},{17,25},{25,17},{2,10},{10... | collective-permute-start | bytes 405512 | tf_op jit(solution)/shard_map/ppermute | solution.py:238
  (52 other events, 107.2 us)

commit v2 on v1

v2 whole, which is shorter than its diff:
```python
import functools

import jax
import jax.numpy as jnp
from jax import lax
from jax.experimental import pallas as pl
from jax.experimental.pallas import tpu as pltpu
from jax.sharding import PartitionSpec as P


ITERS = 3
RIDGE = 0.2
TAIL = 16

GROUP = 8
CHUNKS = 8


def row_order(n):
    return list(range(1, n))


def row_groups(n):
    return [[k] for k in range(n)]


def chip_order(n):
    return list(range(1, n))


def column_groups(n):
    order = chip_order(n)
    between = [[2 * before + 1, 2 * k] for before, k in zip(order, order[1:])]
    return [[0, 1], [2 * order[0]], *between, [2 * order[-1] + 1]]


f32 = jnp.float32
bf16 = jnp.bfloat16
VMEM = pl.BlockSpec(memory_space=pltpu.VMEM)


def tree(values):
    while len(values) > 1:
        values = [values[i] + values[i + 1] for i in range(0, len(values), 2)]
    return values[0]


def to_tail(sums):
    rows = lax.broadcasted_iota(jnp.int32, (TAIL, sums[0].shape[1]), 0)
    tile = jnp.zeros(rows.shape, f32)
    for position, value in enumerate(sums):
        for part in range(3):
            piece = value.astype(bf16).astype(f32)
            tile = jnp.where(rows == 3 * position + part, piece, tile)
            value = value - piece
    return tile.astype(bf16)


def from_tail(tile, position=0):
    start = 3 * position
    return tile[start : start + 1] + tile[start + 1 : start + 2] + tile[start + 2 : start + 3]


def tail_of(ref):
    rows = ref.shape[0]
    return ref[rows - TAIL : rows, :].astype(f32)


def column_sum(value):
    return jnp.sum(value, axis=0, keepdims=True)


def here():
    return lax.axis_index("col"), lax.axis_index("row")


def place_of(cfg, relative):
    return (relative & 1) * (cfg["cols"] // 2) + (relative >> 1)


def first_kernel(
    cfg,
    ids_far,
    listed,
    far,
    send,
    keep,
    keep_tail,
    direction,
    ids,
    x,
    near,
    held,
    total,
    arrived,
):
    fb, nb = cfg["fb"], cfg["nb"]
    c, z = here()
    count = ids.shape[0]
    size = count // CHUNKS
    numbers = pltpu.make_async_copy(ids_far, ids, arrived.at[CHUNKS + 1])
    head = pltpu.make_async_copy(far, near, arrived.at[CHUNKS])
    numbers.start()
    head.start()
    copies = [
        pltpu.make_async_copy(
            listed.at[pl.ds(i * size, size)], x.at[pl.ds(i * size, size)], arrived.at[i]
        )
        for i in range(CHUNKS)
    ]
    for copy in copies:
        copy.start()
    total[...] = jnp.zeros_like(total)
    numbers.wait()
    head.wait()
    own = direction.shape[0]
    direction[...] = near[pl.ds(pl.multiple_of(z * own, own), own), :]
    held[...] = near[...].astype(bf16).reshape(held.shape)
    for i, copy in enumerate(copies):
        copy.wait()

        def step(j, carry, i=i):
            products = []
            for u in range(GROUP):
                k = i * size + j * GROUP + u
                a = ids[k] // fb
                b = ids[k] - a * fb
                slot = a // nb
                target = place_of(cfg, slot ^ c) * nb + (a - slot * nb)
                products.append((target, jnp.dot(x[k], held[b], preferred_element_type=f32)))
            for target, product in products:
                total[target] = total[target] + product
            return carry

        lax.fori_loop(0, size // GROUP, step, 0)
    half = total.shape[0] // 2
    rows = keep.shape[0]
    keep[...] = total[:half].reshape(keep.shape)
    send[:rows, :] = total[half:].reshape(keep.shape).astype(bf16)
    send[rows:, :] = jnp.zeros((TAIL, send.shape[1]), bf16)
    keep_tail[...] = jnp.zeros(keep_tail.shape, bf16)


def dense_kernel(cfg, ids_far, listed, dense, ids, x, arrived):
    fb, zb, width = cfg["fb"], cfg["zb"], cfg["width"]
    size = x.shape[0] // CHUNKS
    copies = [
        pltpu.make_async_copy(
            listed.at[pl.ds(i * size, size)], x.at[pl.ds(i * size, size)], arrived.at[i]
        )
        for i in range(CHUNKS)
    ]
    numbers = pltpu.make_async_copy(ids_far, ids, arrived.at[CHUNKS])
    numbers.start()
    for copy in copies:
        copy.start()

    def clear(a, carry):
        rows = pl.ds(pl.multiple_of(a * width, width), width)
        dense[:, rows, :] = jnp.zeros((dense.shape[0], width, dense.shape[2]), bf16)
        return carry

    lax.fori_loop(0, cfg["rb"], clear, 0)
    numbers.wait()
    for i, copy in enumerate(copies):
        copy.wait()

        def step(j, carry, i=i):
            for u in range(GROUP):
                k = i * size + j * GROUP + u
                a = ids[k] // fb
                b = ids[k] - a * fb
                h = b // zb
                down = pl.ds(pl.multiple_of(a * width, width), width)
                across = pl.ds(pl.multiple_of((b - h * zb) * width, width), width)
                dense[h, down, across] = x[k]
            return carry

        lax.fori_loop(0, size // GROUP, step, 0)


def forward_kernel(cfg, group, x, *refs):
    parts, total = refs[: len(group)], refs[-1]
    rows = cfg["nb"] * cfg["width"]

    for i in range(cfg["cols"]):
        span = slice(i * rows, (i + 1) * rows)
        product = sum(
            jnp.dot(
                x[here()[1] ^ g, span, :], part[: x.shape[2], :], preferred_element_type=f32
            )
            for g, part in zip(group, parts)
        )
        if len(refs) > len(group) + 1:
            product = refs[len(group)][span, :] + product
        total[span, :] = product


def forward_last_kernel(cfg, group, sent, x, *refs):
    parts = refs[: cfg["rows"]]
    total, out = refs[cfg["rows"] : cfg["rows"] + 2]
    rows = cfg["nb"] * cfg["width"]
    chips = cfg["cols"] // 2
    for i in range(chips):
        slot = (2 * i + (1 if sent else 0)) ^ here()[0]
        span = pl.ds(pl.multiple_of(slot * rows, rows), rows)
        value = total[span, :]
        for g in group:
            value = value + jnp.dot(
                x[here()[1] ^ g, span, :], parts[g][: x.shape[2], :], preferred_element_type=f32
            )
        out[i * rows : (i + 1) * rows, :] = value.astype(out.dtype)
    if sent:
        tile = to_tail([from_tail(tree([tail_of(part) for part in parts]))])
        out[chips * rows :, :] = tile
        refs[-1][...] = tile


def merge_kernel(cfg, *refs):
    keep, keep_tail, received = refs[:3]
    own, own_tail, *sends = refs[3:]
    rows = cfg["nb"] * cfg["width"]
    tile = keep_tail[...].astype(f32) + tail_of(received)
    tile = to_tail([from_tail(tile)])
    own[...] = keep[:rows, :] + received[:rows, :].astype(f32)
    own_tail[...] = tile
    for k, send in enumerate(sends, start=1):
        span = slice(k * rows, (k + 1) * rows)
        send[:rows, :] = (keep[span, :] + received[span, :].astype(f32)).astype(bf16)
        send[rows:, :] = tile


def scale_kernel(cfg, first, *refs):
    chips = cfg["cols"] // 2
    own, own_tail = refs[:2]
    received = refs[2 : 1 + chips]
    rest = refs[1 + chips :]
    rows = own.shape[0]
    projected = tree([own[...]] + [r[:rows, :].astype(f32) for r in received])
    if first:
        removed, margins, direction, scaled, kept, spread = rest
        width = cfg["width"]
        for j in range(cfg["nb"]):
            logistic = 1.0 / (1.0 + jnp.exp(-margins[pl.ds(here()[0] * cfg["nb"] + j, 1), :]))
            weight = jnp.where(removed[j : j + 1, :] > 0.0, 0.0, logistic * (1.0 - logistic))
            row = jnp.broadcast_to(weight, (width, width))
            spread[j * width : (j + 1) * width, :] = row.T
        d = direction[...]
        norm = column_sum(d * d)
    else:
        spread, residual, old, before, norm_now, scaled, kept, direction, norm_out, beta_out = rest
        tile = tree([own_tail[...].astype(f32)] + [tail_of(r) for r in received])
        norm = from_tail(tile)
        beta = norm / norm_now[0:1, :]
        projected = projected + beta * before[...]
        d = residual[...] + beta * old[...]
        direction[...] = d
        norm_out[...] = jnp.broadcast_to(norm, norm_out.shape)
        beta_out[...] = jnp.broadcast_to(beta, beta_out.shape)
    kept[...] = projected
    weighted = spread[...] * projected
    width = cfg["width"]
    for j in range(cfg["nb"]):
        tile = weighted[j * width : (j + 1) * width, :]
        scaled[j * width : (j + 1) * width, :] = tile.T.astype(bf16)
    curvature = column_sum(weighted * projected) + RIDGE * column_sum(d * d)
    scaled[rows:, :] = to_tail([curvature, norm] if first else [curvature])


def turned(cfg, part):
    width = cfg["width"]
    return jnp.concatenate(
        [part[j * width : (j + 1) * width, :] for j in range(cfg["nb"])], axis=1
    )


def backward_sum(cfg, group, x, near, h):
    rows = cfg["nb"] * cfg["width"]
    products = []
    for g, part in zip(group, near):
        span = pl.ds(pl.multiple_of((here()[0] ^ g) * rows, rows), rows)
        products.append(jnp.dot(part, x[h, span, :], preferred_element_type=f32))
    return sum(products)


def backward_kernel(cfg, group, x, *refs):
    near = [turned(cfg, part) for part in refs[: len(group)]]
    total = refs[-1]
    for h in range(cfg["rows"]):
        product = backward_sum(cfg, group, x, near, h)
        if len(refs) > len(group) + 1:
            product = refs[len(group)][h] + product
        total[h] = product


def backward_last_kernel(cfg, group, first, sent, x, *refs):
    cols, width = cfg["cols"], cfg["width"]
    parts, total = refs[:cols], refs[cols]
    near = [turned(cfg, parts[g]) for g in group]
    outs = refs[cols + 1 :]
    if sent:
        tile = tree([tail_of(part) for part in parts])
        tile = to_tail([from_tail(tile, j) for j in range(2 if first else 1)])
        outs[-1][...] = tile
    for k in range(1, cfg["rows"]) if sent else [0]:
        out = outs[k - 1] if sent else outs[0]
        h = here()[1] ^ k
        value = total[h] + backward_sum(cfg, group, x, near, h)
        for j in range(cfg["zb"]):
            out[j * width : (j + 1) * width, :] = value[:, j * width : (j + 1) * width].astype(
                out.dtype
            )
        if sent:
            out[cfg["zb"] * width :, :] = tile


def update_kernel(cfg, first, *refs):
    others = cfg["rows"] - 1
    own, own_tail = refs[:2]
    received = refs[2 : 2 + others]
    direction, residual, norm_now, share, after, norm_out, alpha_out = refs[2 + others :]
    rows = own.shape[0]
    image = tree([own[...]] + [r[:rows, :].astype(f32) for r in received])
    width = cfg["width"]
    image = [image[j * width : (j + 1) * width, :].T for j in range(cfg["zb"])]
    image = jnp.concatenate(image, axis=0) + RIDGE * direction[...]
    tile = tree([own_tail[...].astype(f32)] + [tail_of(r) for r in received])
    norm = from_tail(tile, 1) if first else norm_now[0:1, :]
    alpha = norm / from_tail(tile)
    left = residual[...] - alpha * image
    after[...] = left
    norm_out[...] = jnp.broadcast_to(norm, norm_out.shape)
    alpha_out[...] = jnp.broadcast_to(alpha, alpha_out.shape)
    share[:rows, :] = left.astype(bf16)
    share[rows:, :] = to_tail([column_sum(left * left)])


def result_kernel(cfg, count, *refs):
    others = cfg["rows"]
    grads = refs[0]
    shares = refs[1 : 1 + others * (count - 1)]
    rest = refs[1 + len(shares) :]
    alphas, betas, out = rest[:count], rest[count : 2 * count - 1], rest[-1]
    rows = grads.shape[0] // others
    for k in range(others):
        span = pl.ds(pl.multiple_of((here()[1] ^ k) * rows, rows), rows)
        d = grads[span, :]
        total = alphas[0][0:1, :] * d
        for j in range(1, count):
            share = shares[(j - 1) * others + k]
            d = share[:rows, :].astype(f32) + betas[j - 1][0:1, :] * d
            total = total + alphas[j][0:1, :] * d
        out[span, :] = total


def residual_kernel(cfg, *refs):
    shares, out = refs[:-1], refs[-1]
    rows = out.shape[0] // cfg["rows"]
    for k, share in enumerate(shares):
        span = pl.ds(pl.multiple_of((here()[1] ^ k) * rows, rows), rows)
        out[span, :] = share[:rows, :].astype(f32)


def on_device(cfg, x_blocks, block_ids, margins, deleted, grads):
    width = x_blocks.shape[1]
    directions = grads.shape[1]
    cols, rows_axis = cfg["cols"], cfg["rows"]
    rb, fb = margins.shape[0] // width, grads.shape[0] // width
    nb, zb = rb // cols, fb // rows_axis
    cfg = dict(cfg, rb=rb, fb=fb, nb=nb, zb=zb, width=width)
    c, z = lax.axis_index("col"), lax.axis_index("row")
    ids = block_ids[:, 0]
    own_rows, own_features = nb * width, zb * width
    chips = cols // 2
    half = rb // 2 * width

    def shape(rows, dtype):
        return jax.ShapeDtypeStruct((rows, directions), dtype)

    def along(axis, value, k):
        n = rows_axis if axis == "row" else cols
        return lax.ppermute(value, axis, [(i, i ^ k) for i in range(n)])

    def exchange(axis, values, order, step=1):
        received = {k: along(axis, values[k - 1], step * k) for k in order}
        return [received[k] for k in range(1, len(order) + 1)]

    def near(value):
        return pltpu.with_memory_space_constraint(value, pltpu.VMEM)

    def far(value):
        return pltpu.with_memory_space_constraint(value, pltpu.HBM)

    def call(kernel, out, inputs, stay=True, aliases=None):
        if stay:
            out = [pltpu.VMEM(o.shape, o.dtype) for o in out]
        return pl.pallas_call(
            kernel,
            out_shape=out,
            in_specs=[VMEM] * len(inputs),
            out_specs=[VMEM] * len(out),
            input_output_aliases=aliases or {},
            compiler_params=pltpu.CompilerParams(vmem_limit_bytes=4 << 20),
        )(*map(near, inputs))

    matrix = []

    def multiply(kernel, out, inputs, aliases=None):
        at = len(inputs)

        def body(*refs):
            kernel(refs[at], *refs[:at], *refs[at + 1 : -1])

        x = matrix.pop()
        *results, x = call(
            body,
            [*out, jax.ShapeDtypeStruct(x.shape, x.dtype)],
            [*inputs, x],
            aliases={**(aliases or {}), at: len(out)},
        )
        matrix.append(x)
        return results

    def begin():
        return pl.pallas_call(
            functools.partial(first_kernel, cfg),
            out_shape=[
                pltpu.VMEM((half + TAIL, directions), bf16),
                pltpu.VMEM((half, directions), f32),
                pltpu.VMEM((TAIL, directions), bf16),
                pltpu.VMEM((own_features, directions), f32),
            ],
            in_specs=[pl.BlockSpec(memory_space=pltpu.HBM)] * 3,
            out_specs=[VMEM] * 4,
            scratch_shapes=[
                pltpu.SMEM(ids.shape, jnp.int32),
                pltpu.VMEM(x_blocks.shape, bf16),
                pltpu.VMEM(grads.shape, f32),
                pltpu.VMEM((fb, width, directions), bf16),
                pltpu.VMEM((rb, width, directions), f32),
                pltpu.SemaphoreType.DMA((CHUNKS + 2,)),
            ],
            compiler_params=pltpu.CompilerParams(vmem_limit_bytes=16 << 20),
        )(far(ids), far(x_blocks), far(grads))

    def lay_out():
        return pl.pallas_call(
            functools.partial(dense_kernel, cfg),
            out_shape=pltpu.VMEM((rows_axis, rb * width, own_features), bf16),
            in_specs=[pl.BlockSpec(memory_space=pltpu.HBM)] * 2,
            out_specs=VMEM,
            scratch_shapes=[
                pltpu.SMEM(ids.shape, jnp.int32),
                pltpu.VMEM(x_blocks.shape, bf16),
                pltpu.SemaphoreType.DMA((CHUNKS + 1,)),
            ],
            compiler_params=pltpu.CompilerParams(vmem_limit_bytes=12 << 20),
        )(far(ids), far(x_blocks))

    def forward(parts):
        total = []
        *groups, group = row_groups(rows_axis)
        for some in groups:
            total = multiply(
                functools.partial(forward_kernel, cfg, some),
                [shape(rb * width, f32)],
                [parts[g] for g in some] + total,
                aliases={len(some): 0} if total else {},
            )
        send, keep_tail = multiply(
            functools.partial(forward_last_kernel, cfg, group, True),
            [shape(half + TAIL, bf16), shape(TAIL, bf16)],
            [*parts, *total],
        )
        (keep,) = multiply(
            functools.partial(forward_last_kernel, cfg, group, False),
            [shape(half, f32)],
            [*parts, *total],
        )
        return send, keep, keep_tail

    def backward(scaled, first):
        others = exchange("col", [scaled] * (chips - 1), chip_order(chips), 2)
        parts = []
        for part in [scaled, *others]:
            parts += [part, along("col", part, 1)]
        total = []
        *groups, group = column_groups(chips)
        for some in groups:
            total = multiply(
                functools.partial(backward_kernel, cfg, some),
                [jax.ShapeDtypeStruct((rows_axis, directions, own_features), f32)],
                [parts[g] for g in some] + total,
                aliases={len(some): 0} if total else {},
            )
        *sends, own_tail = multiply(
            functools.partial(backward_last_kernel, cfg, group, first, True),
            [shape(own_features + TAIL, bf16)] * (rows_axis - 1) + [shape(TAIL, bf16)],
            [*parts, *total],
        )
        (own,) = multiply(
            functools.partial(backward_last_kernel, cfg, group, first, False),
            [shape(own_features, f32)],
            [*parts, *total],
        )
        return sends, own, own_tail

    row_ids = z * margins.shape[0] + c * own_rows + jnp.arange(own_rows, dtype=jnp.int32)
    row_ids = row_ids.reshape(nb, width)
    removed = jnp.any(row_ids[None] == deleted[:, None, None], axis=0)
    removed = removed.astype(f32)
    margins = margins.reshape(rb, width)
    parts, shares, alphas, betas = [], [], [], []
    share = spread = before = None
    norm_now = jnp.zeros((8, directions), f32)
    for iteration in range(ITERS):
        first = iteration == 0
        if first:
            send, keep, keep_tail, direction = begin()
            residual = direction
        else:
            parts = [share, *exchange("row", [share] * (rows_axis - 1), row_order(rows_axis))]
            shares += parts
            send, keep, keep_tail = forward(parts)
        received = along("col", send, 1)
        own, own_tail, *sends = call(
            functools.partial(merge_kernel, cfg),
            [shape(own_rows, f32), shape(TAIL, bf16)]
            + [shape(own_rows + TAIL, bf16)] * (chips - 1),
            [keep, keep_tail, received],
        )
        received = exchange("col", sends, chip_order(chips), 2)
        if first:
            matrix.append(lay_out())
            scaled, before, spread = call(
                functools.partial(scale_kernel, cfg, True),
                [shape(own_rows + TAIL, bf16), shape(own_rows, f32), shape(own_rows, f32)],
                [own, own_tail, *received, removed, margins, direction],
            )
        else:
            scaled, before, direction, norm_now, beta = call(
                functools.partial(scale_kernel, cfg, False),
                [
                    shape(own_rows + TAIL, bf16),
                    shape(own_rows, f32),
                    shape(own_features, f32),
                    shape(8, f32),
                    shape(8, f32),
                ],
                [own, own_tail, *received, spread, residual, direction, before, norm_now],
            )
            betas.append(beta)
        sends, own, own_tail = backward(scaled, first)
        received = exchange("row", sends, row_order(rows_axis))
        share, residual, norm_now, alpha = call(
            functools.partial(update_kernel, cfg, first),
            [
                shape(own_features + TAIL, bf16),
                shape(own_features, f32),
                shape(8, f32),
                shape(8, f32),
            ],
            [own, own_tail, *received, direction, residual, norm_now],
        )
        alphas.append(alpha)
    parts = [share, *exchange("row", [share] * (rows_axis - 1), row_order(rows_axis))]
    (answer,) = call(
        functools.partial(result_kernel, cfg, ITERS),
        [shape(fb * width, f32)],
        [grads, *shares, *alphas, *betas],
        stay=False,
    )
    (left,) = call(
        functools.partial(residual_kernel, cfg), [shape(fb * width, f32)], parts, stay=False
    )
    return (answer, left)


def solution(mesh):
    cfg = {"rows": mesh.shape["row"], "cols": mesh.shape["col"]}
    placed = (P("row", "col", None), P("row", "col"), P("row"), P("row"), P("col", None))
    return jax.shard_map(
        functools.partial(on_device, cfg),
        mesh=mesh,
        in_specs=placed,
        out_specs=(P("col", None), P("col", None)),
        check_vma=False,
    )
```

time: 258 us -> 185 us (0.72)
  Pallas kernels: 88.3 us -> 42.4 us
  local copies, waits for them, and re-layouts: 16.7 us -> 0.73 us
  waiting for transfers between devices: 98.3 us -> 87.3 us
    pallas_call x16 -> x41, Pallas kernels: 88.3 us -> 42.4 us  [the longest x39 27.3 us: call(): pl.pallas_call(kernel, out_shape=out, in_specs=[VMEM] * len(inputs), out_...]
    unnamed x98 -> x4, local copies, waits for them, and re-layouts: 11.9 us -> 0.72 us
    ppermute x51, waiting for transfers between devices: 98.3 us -> 87.3 us  [along(): return lax.ppermute(value, axis, [(i, i ^ k) for i in range(n)])]
  transfers between devices with their start and end apart: 51 -> 51, of which waited for: 31 -> 27; matrix products, arithmetic and copies ran while one was open for 2% -> 0% of each run, Pallas kernels for 1% -> 14%
where the time goes in v2:
time: 185 us
  waiting for transfers between devices  87.3 us (47%)
  starting transfers between devices  52.2 us (28%)
  Pallas kernels  42.4 us (23%)
    ppermute x51, waiting for transfers between devices, along(): return lax.ppermute(value, axis, [(i, i ^ k) for i in range(n)])  87.3 us
    ppermute x51, starting transfers between devices, along(): return lax.ppermute(value, axis, [(i, i ^ k) for i in range(n)])  52.2 us
    pallas_call x39, Pallas kernels, call(): pl.pallas_call(kernel, out_shape=out, in_specs=[VMEM] * len(inputs), out_...  27.3 us
    pallas_call x1, Pallas kernels, begin(): pl.pallas_call(functools.partial(first_kernel, cfg), out_shape=[pltpu.VME...  9.31 us
    pallas_call x1, Pallas kernels, lay_out(): pl.pallas_call(functools.partial(dense_kernel, cfg), out_shape=pltpu.VMEM...  5.78 us
  transfers between devices with their start and end apart: 51, of which 27 were waited for; matrix products, arithmetic and copies ran while one was open for 0% of the time, Pallas kernels for 14%

profile of v2, /device:TPU:0, one launch (start us, length us, event | category | flops | bytes accessed | tf_op | source)
XLA Modules:
  0.0 184.6 jit_solution(6684223678908017460)
XLA Ops:
  0.6 9.3 %shard_map.68 = (bf16[2064,128]{1,0:T(8,128)(2,1)S(1)}, f32[2048,128]{1,0:T(8,128)S(1)}, bf16[16,128]{1,0:T(8,128)(2,1)S(1)}, f32[512,128]{1,0:T(8,128)S(1)}) custom-call(s32[256]{0:T(256)} %bitcast.3, bf16[256,128,128]{2,1,0:T(8,128)(2,1)} %listed.3, f32[2048,128]{1,0:T(8,128)} %refs_0_.1), custom_call_target="tpu_custom_call" | custom-call | tf_op jit(solution)/shard_map/pallas_call | solution.py:425
  10.5 1.5 collective-permute-done.refs_2_
  12.1 2.9 %collective-permute-start.1 = (bf16[528,128]{1,0:T(8,128)(2,1)S(1)}, bf16[528,128]{1,0:T(8,128)(2,1)S(1)}, u32[]{:S(2)}, u32[]{:S(2)}) collective-permute-start(bf16[528,128]{1,0:T(8,128)(2,1)S(1)} %get-tuple-element.114), channel_id=1, source_target_pairs={{0,2},{1,3},{2,0},{3,1},{4,6},{5,7},{6,4},{7,5},{8,10},{9,11},{10,... | collective-permute-start | bytes 405512 | tf_op jit(solution)/shard_map/ppermute | solution.py:382
  15.1 1.5 collective-permute-start.2
  17.5 1.7 collective-permute-done.1.refs_2_
  19.2 4.1 %collective-permute-done.2.refs_3_ = bf16[528,128]{1,0:T(8,128)(2,1)S(1)} collective-permute-done((bf16[528,128]{1,0:T(8,128)(2,1)S(1)}, bf16[528,128]{1,0:T(8,128)(2,1)S(1)}, u32[]{:S(2)}, u32[]{:S(2)}) %collective-permute-start.2) | collective-permute-done | bytes 135200 | tf_op jit(solution)/shard_map/ppermute | solution.py:382
  26.4 1.4 collective-permute-start.9
  27.8 2.5 %collective-permute-done.5.refs_0_.refs_2_ = bf16[528,128]{1,0:T(8,128)(2,1)S(1)} collective-permute-done((bf16[528,128]{1,0:T(8,128)(2,1)S(1)}, bf16[528,128]{1,0:T(8,128)(2,1)S(1)}, u32[]{:S(2)}, u32[]{:S(2)}) %collective-permute-start.5) | collective-permute-done | bytes 135200 | tf_op jit(solution)/shard_map/ppermute | solution.py:382
  30.3 2.6 %collective-permute-done.7.refs_1_.refs_4_ = bf16[528,128]{1,0:T(8,128)(2,1)S(1)} collective-permute-done((bf16[528,128]{1,0:T(8,128)(2,1)S(1)}, bf16[528,128]{1,0:T(8,128)(2,1)S(1)}, u32[]{:S(2)}, u32[]{:S(2)}) %collective-permute-start.7) | collective-permute-done | bytes 135200 | tf_op jit(solution)/shard_map/ppermute | solution.py:382
  33.5 5.8 %shard_map.71.refs_2_ = bf16[4,4096,512]{2,1,0:T(8,128)(2,1)S(1)} custom-call(s32[256]{0:T(256)} %bitcast.4, bf16[256,128,128]{2,1,0:T(8,128)(2,1)} %listed.3), custom_call_target="tpu_custom_call" | custom-call | tf_op jit(solution)/shard_map/pallas_call | solution.py:447
  42.6 1.6 collective-permute-start.11
  44.2 2.6 %collective-permute-start.12 = (bf16[528,128]{1,0:T(8,128)(2,1)S(1)}, bf16[528,128]{1,0:T(8,128)(2,1)S(1)}, u32[]{:S(2)}, u32[]{:S(2)}) collective-permute-start(bf16[528,128]{1,0:T(8,128)(2,1)S(1)} %get-tuple-element.131), channel_id=1, source_target_pairs={{0,16},{8,24},{16,0},{24,8},{1,17},{9,25},{17,1},{25,9},{2,18},{10... | collective-permute-start | bytes 405512 | tf_op jit(solution)/shard_map/ppermute | solution.py:382
  47.3 2.8 %collective-permute-done.11.refs_2_ = bf16[528,128]{1,0:T(8,128)(2,1)S(1)} collective-permute-done((bf16[528,128]{1,0:T(8,128)(2,1)S(1)}, bf16[528,128]{1,0:T(8,128)(2,1)S(1)}, u32[]{:S(2)}, u32[]{:S(2)}) %collective-permute-start.11) | collective-permute-done | bytes 135200 | tf_op jit(solution)/shard_map/ppermute | solution.py:382
  50.1 7.3 %collective-permute-done.12.refs_3_ = bf16[528,128]{1,0:T(8,128)(2,1)S(1)} collective-permute-done((bf16[528,128]{1,0:T(8,128)(2,1)S(1)}, bf16[528,128]{1,0:T(8,128)(2,1)S(1)}, u32[]{:S(2)}, u32[]{:S(2)}) %collective-permute-start.12) | collective-permute-done | bytes 135200 | tf_op jit(solution)/shard_map/ppermute | solution.py:382
  57.6 2.3 %collective-permute-start.14 = (bf16[528,128]{1,0:T(8,128)(2,1)S(1)}, bf16[528,128]{1,0:T(8,128)(2,1)S(1)}, u32[]{:S(2)}, u32[]{:S(2)}) collective-permute-start(bf16[528,128]{1,0:T(8,128)(2,1)S(1)} %get-tuple-element.133.refs_0_.refs_1_), channel_id=1, source_target_pairs={{0,8},{8,0},{16,24},{24,16},{1,9},{9,1},{17,25},{25,17},{2,10},{10... | collective-permute-start | bytes 405512 | tf_op jit(solution)/shard_map/ppermute | solution.py:382
  61.0 1.4 collective-permute-start.16
  64.3 1.5 shard_map.80
  65.9 6.3 %collective-permute-done.15.refs_0_.refs_2_.refs_3_ = bf16[528,128]{1,0:T(8,128)(2,1)S(1)} collective-permute-done((bf16[528,128]{1,0:T(8,128)(2,1)S(1)}, bf16[528,128]{1,0:T(8,128)(2,1)S(1)}, u32[]{:S(2)}, u32[]{:S(2)}) %collective-permute-start.15) | collective-permute-done | bytes 135200 | tf_op jit(solution)/shard_map/ppermute | solution.py:382
  72.2 1.6 shard_map.81
  76.5 1.4 collective-permute-start.18
  80.1 2.8 %collective-permute-done.18.refs_2_ = bf16[528,128]{1,0:T(8,128)(2,1)S(1)} collective-permute-done((bf16[528,128]{1,0:T(8,128)(2,1)S(1)}, bf16[528,128]{1,0:T(8,128)(2,1)S(1)}, u32[]{:S(2)}, u32[]{:S(2)}) %collective-permute-start.18) | collective-permute-done | bytes 135200 | tf_op jit(solution)/shard_map/ppermute | solution.py:382
  82.9 3.3 %collective-permute-done.19.refs_3_ = bf16[528,128]{1,0:T(8,128)(2,1)S(1)} collective-permute-done((bf16[528,128]{1,0:T(8,128)(2,1)S(1)}, bf16[528,128]{1,0:T(8,128)(2,1)S(1)}, u32[]{:S(2)}, u32[]{:S(2)}) %collective-permute-start.19) | collective-permute-done | bytes 135200 | tf_op jit(solution)/shard_map/ppermute | solution.py:382
  87.2 1.3 collective-permute-start.24
  88.5 1.5 collective-permute-start.26
  90.0 2.8 %collective-permute-done.22.refs_0_.refs_2_ = bf16[528,128]{1,0:T(8,128)(2,1)S(1)} collective-permute-done((bf16[528,128]{1,0:T(8,128)(2,1)S(1)}, bf16[528,128]{1,0:T(8,128)(2,1)S(1)}, u32[]{:S(2)}, u32[]{:S(2)}) %collective-permute-start.22) | collective-permute-done | bytes 135200 | tf_op jit(solution)/shard_map/ppermute | solution.py:382
  92.8 2.2 %collective-permute-done.24.refs_1_.refs_4_ = bf16[528,128]{1,0:T(8,128)(2,1)S(1)} collective-permute-done((bf16[528,128]{1,0:T(8,128)(2,1)S(1)}, bf16[528,128]{1,0:T(8,128)(2,1)S(1)}, u32[]{:S(2)}, u32[]{:S(2)}) %collective-permute-start.24) | collective-permute-done | bytes 135200 | tf_op jit(solution)/shard_map/ppermute | solution.py:382
  99.3 2.1 %collective-permute-start.29 = (bf16[528,128]{1,0:T(8,128)(2,1)S(1)}, bf16[528,128]{1,0:T(8,128)(2,1)S(1)}, u32[]{:S(2)}, u32[]{:S(2)}) collective-permute-start(bf16[528,128]{1,0:T(8,128)(2,1)S(1)} %get-tuple-element.168), channel_id=1, source_target_pairs={{0,16},{8,24},{16,0},{24,8},{1,17},{9,25},{17,1},{25,9},{2,18},{10... | collective-permute-start | bytes 405512 | tf_op jit(solution)/shard_map/ppermute | solution.py:382
  101.4 1.9 %collective-permute-start.30 = (bf16[528,128]{1,0:T(8,128)(2,1)S(1)}, bf16[528,128]{1,0:T(8,128)(2,1)S(1)}, u32[]{:S(2)}, u32[]{:S(2)}) collective-permute-start(bf16[528,128]{1,0:T(8,128)(2,1)S(1)} %get-tuple-element.169), channel_id=1, source_target_pairs={{0,24},{8,16},{16,8},{24,0},{1,25},{9,17},{17,9},{25,1},{2,26},{10... | collective-permute-start | bytes 405512 | tf_op jit(solution)/shard_map/ppermute | solution.py:382
  103.5 3.1 %collective-permute-done.28.refs_2_ = bf16[528,128]{1,0:T(8,128)(2,1)S(1)} collective-permute-done((bf16[528,128]{1,0:T(8,128)(2,1)S(1)}, bf16[528,128]{1,0:T(8,128)(2,1)S(1)}, u32[]{:S(2)}, u32[]{:S(2)}) %collective-permute-start.28) | collective-permute-done | bytes 135200 | tf_op jit(solution)/shard_map/ppermute | solution.py:382
  106.7 5.8 %collective-permute-done.29.refs_3_ = bf16[528,128]{1,0:T(8,128)(2,1)S(1)} collective-permute-done((bf16[528,128]{1,0:T(8,128)(2,1)S(1)}, bf16[528,128]{1,0:T(8,128)(2,1)S(1)}, u32[]{:S(2)}, u32[]{:S(2)}) %collective-permute-start.29) | collective-permute-done | bytes 135200 | tf_op jit(solution)/shard_map/ppermute | solution.py:382
  112.7 2.3 %collective-permute-start.31 = (bf16[528,128]{1,0:T(8,128)(2,1)S(1)}, bf16[528,128]{1,0:T(8,128)(2,1)S(1)}, u32[]{:S(2)}, u32[]{:S(2)}) collective-permute-start(bf16[528,128]{1,0:T(8,128)(2,1)S(1)} %get-tuple-element.172.refs_0_.refs_5_), channel_id=1, source_target_pairs={{0,8},{8,0},{16,24},{24,16},{1,9},{9,1},{17,25},{25,17},{2,10},{10... | collective-permute-start | bytes 405512 | tf_op jit(solution)/shard_map/ppermute | solution.py:382
  116.1 1.4 collective-permute-start.33
  119.4 1.5 shard_map.94
  121.0 6.4 %collective-permute-done.32.refs_0_.refs_2_.refs_7_ = bf16[528,128]{1,0:T(8,128)(2,1)S(1)} collective-permute-done((bf16[528,128]{1,0:T(8,128)(2,1)S(1)}, bf16[528,128]{1,0:T(8,128)(2,1)S(1)}, u32[]{:S(2)}, u32[]{:S(2)}) %collective-permute-start.32) | collective-permute-done | bytes 135200 | tf_op jit(solution)/shard_map/ppermute | solution.py:382
  127.4 1.6 shard_map.95
  134.0 1.4 collective-permute-start.37
  135.3 3.0 %collective-permute-done.35.refs_2_ = bf16[528,128]{1,0:T(8,128)(2,1)S(1)} collective-permute-done((bf16[528,128]{1,0:T(8,128)(2,1)S(1)}, bf16[528,128]{1,0:T(8,128)(2,1)S(1)}, u32[]{:S(2)}, u32[]{:S(2)}) %collective-permute-start.35) | collective-permute-done | bytes 135200 | tf_op jit(solution)/shard_map/ppermute | solution.py:382
  138.3 2.7 %collective-permute-done.36.refs_3_ = bf16[528,128]{1,0:T(8,128)(2,1)S(1)} collective-permute-done((bf16[528,128]{1,0:T(8,128)(2,1)S(1)}, bf16[528,128]{1,0:T(8,128)(2,1)S(1)}, u32[]{:S(2)}, u32[]{:S(2)}) %collective-permute-start.36) | collective-permute-done | bytes 135200 | tf_op jit(solution)/shard_map/ppermute | solution.py:382
  145.3 2.8 %collective-permute-done.39.refs_0_.refs_2_ = bf16[528,128]{1,0:T(8,128)(2,1)S(1)} collective-permute-done((bf16[528,128]{1,0:T(8,128)(2,1)S(1)}, bf16[528,128]{1,0:T(8,128)(2,1)S(1)}, u32[]{:S(2)}, u32[]{:S(2)}) %collective-permute-start.39) | collective-permute-done | bytes 135200 | tf_op jit(solution)/shard_map/ppermute | solution.py:382
  148.1 2.3 %collective-permute-done.41.refs_1_.refs_4_ = bf16[528,128]{1,0:T(8,128)(2,1)S(1)} collective-permute-done((bf16[528,128]{1,0:T(8,128)(2,1)S(1)}, bf16[528,128]{1,0:T(8,128)(2,1)S(1)}, u32[]{:S(2)}, u32[]{:S(2)}) %collective-permute-start.41) | collective-permute-done | bytes 135200 | tf_op jit(solution)/shard_map/ppermute | solution.py:382
  154.8 2.0 %collective-permute-start.46 = (bf16[528,128]{1,0:T(8,128)(2,1)S(1)}, bf16[528,128]{1,0:T(8,128)(2,1)S(1)}, u32[]{:S(2)}, u32[]{:S(2)}) collective-permute-start(bf16[528,128]{1,0:T(8,128)(2,1)S(1)} %get-tuple-element.208), channel_id=1, source_target_pairs={{0,16},{8,24},{16,0},{24,8},{1,17},{9,25},{17,1},{25,9},{2,18},{10... | collective-permute-start | bytes 405512 | tf_op jit(solution)/shard_map/ppermute | solution.py:382
  156.8 1.9 %collective-permute-start.47 = (bf16[528,128]{1,0:T(8,128)(2,1)S(1)}, bf16[528,128]{1,0:T(8,128)(2,1)S(1)}, u32[]{:S(2)}, u32[]{:S(2)}) collective-permute-start(bf16[528,128]{1,0:T(8,128)(2,1)S(1)} %get-tuple-element.209), channel_id=1, source_target_pairs={{0,24},{8,16},{16,8},{24,0},{1,25},{9,17},{17,9},{25,1},{2,26},{10... | collective-permute-start | bytes 405512 | tf_op jit(solution)/shard_map/ppermute | solution.py:382
  159.0 3.2 %collective-permute-done.45.refs_2_ = bf16[528,128]{1,0:T(8,128)(2,1)S(1)} collective-permute-done((bf16[528,128]{1,0:T(8,128)(2,1)S(1)}, bf16[528,128]{1,0:T(8,128)(2,1)S(1)}, u32[]{:S(2)}, u32[]{:S(2)}) %collective-permute-start.45) | collective-permute-done | bytes 135200 | tf_op jit(solution)/shard_map/ppermute | solution.py:382
  162.1 5.8 %collective-permute-done.46.refs_3_ = bf16[528,128]{1,0:T(8,128)(2,1)S(1)} collective-permute-done((bf16[528,128]{1,0:T(8,128)(2,1)S(1)}, bf16[528,128]{1,0:T(8,128)(2,1)S(1)}, u32[]{:S(2)}, u32[]{:S(2)}) %collective-permute-start.46) | collective-permute-done | bytes 135200 | tf_op jit(solution)/shard_map/ppermute | solution.py:382
  168.8 2.3 %collective-permute-start.48 = (bf16[528,128]{1,0:T(8,128)(2,1)S(1)}, bf16[528,128]{1,0:T(8,128)(2,1)S(1)}, u32[]{:S(2)}, u32[]{:S(2)}) collective-permute-start(bf16[528,128]{1,0:T(8,128)(2,1)S(1)} %get-tuple-element.215.refs_0_), channel_id=1, source_target_pairs={{0,8},{8,0},{16,24},{24,16},{1,9},{9,1},{17,25},{25,17},{2,10},{10... | collective-permute-start | bytes 405512 | tf_op jit(solution)/shard_map/ppermute | solution.py:382
  172.1 1.5 collective-permute-start.50
  173.6 1.4 shard_map.107
  175.5 8.0 %collective-permute-done.49.refs_2_ = bf16[528,128]{1,0:T(8,128)(2,1)S(1)} collective-permute-done((bf16[528,128]{1,0:T(8,128)(2,1)S(1)}, bf16[528,128]{1,0:T(8,128)(2,1)S(1)}, u32[]{:S(2)}, u32[]{:S(2)}) %collective-permute-start.49) | collective-permute-done | bytes 135200 | tf_op jit(solution)/shard_map/ppermute | solution.py:382
  (103 shorter events, 43.2 us)
Async XLA Ops:
  12.1 7.0 %collective-permute-start.1 = (bf16[528,128]{1,0:T(8,128)(2,1)S(1)}, bf16[528,128]{1,0:T(8,128)(2,1)S(1)}, u32[]{:S(2)}, u32[]{:S(2)}) collective-permute-start(bf16[528,128]{1,0:T(8,128)(2,1)S(1)} %get-tuple-element.114), channel_id=1, source_target_pairs={{0,2},{1,3},{2,0},{3,1},{4,6},{5,7},{6,4},{7,5},{8,10},{9,11},{10,... | collective-permute-start | bytes 405512 | tf_op jit(solution)/shard_map/ppermute | solution.py:382
  15.1 8.2 %collective-permute-start.2 = (bf16[528,128]{1,0:T(8,128)(2,1)S(1)}, bf16[528,128]{1,0:T(8,128)(2,1)S(1)}, u32[]{:S(2)}, u32[]{:S(2)}) collective-permute-start(bf16[528,128]{1,0:T(8,128)(2,1)S(1)} %get-tuple-element.115), channel_id=1, source_target_pairs={{0,4},{1,5},{2,6},{3,7},{4,0},{5,1},{6,2},{7,3},{8,12},{9,13},{10,... | collective-permute-start | bytes 405512 | tf_op jit(solution)/shard_map/ppermute | solution.py:382
  16.6 6.7 %collective-permute-start.3 = (bf16[528,128]{1,0:T(8,128)(2,1)S(1)}, bf16[528,128]{1,0:T(8,128)(2,1)S(1)}, u32[]{:S(2)}, u32[]{:S(2)}) collective-permute-start(bf16[528,128]{1,0:T(8,128)(2,1)S(1)} %get-tuple-element.116), channel_id=1, source_target_pairs={{0,6},{1,7},{2,4},{3,5},{4,2},{5,3},{6,0},{7,1},{8,14},{9,15},{10,... | collective-permute-start | bytes 405512 | tf_op jit(solution)/shard_map/ppermute | solution.py:382
  24.3 6.1 %collective-permute-start.5 = (bf16[528,128]{1,0:T(8,128)(2,1)S(1)}, bf16[528,128]{1,0:T(8,128)(2,1)S(1)}, u32[]{:S(2)}, u32[]{:S(2)}) collective-permute-start(bf16[528,128]{1,0:T(8,128)(2,1)S(1)} %get-tuple-element.118.refs_0_), channel_id=1, source_target_pairs={{0,2},{1,3},{2,0},{3,1},{4,6},{5,7},{6,4},{7,5},{8,10},{9,11},{10,... | collective-permute-start | bytes 405512 | tf_op jit(solution)/shard_map/ppermute | solution.py:382
  25.6 7.4 %collective-permute-start.7 = (bf16[528,128]{1,0:T(8,128)(2,1)S(1)}, bf16[528,128]{1,0:T(8,128)(2,1)S(1)}, u32[]{:S(2)}, u32[]{:S(2)}) collective-permute-start(bf16[528,128]{1,0:T(8,128)(2,1)S(1)} %get-tuple-element.118.refs_0_), channel_id=1, source_target_pairs={{0,4},{1,5},{2,6},{3,7},{4,0},{5,1},{6,2},{7,3},{8,12},{9,13},{10,... | collective-permute-start | bytes 405512 | tf_op jit(solution)/shard_map/ppermute | solution.py:382
  26.4 6.6 %collective-permute-start.9 = (bf16[528,128]{1,0:T(8,128)(2,1)S(1)}, bf16[528,128]{1,0:T(8,128)(2,1)S(1)}, u32[]{:S(2)}, u32[]{:S(2)}) collective-permute-start(bf16[528,128]{1,0:T(8,128)(2,1)S(1)} %get-tuple-element.118.refs_0_), channel_id=1, source_target_pairs={{0,6},{1,7},{2,4},{3,5},{4,2},{5,3},{6,0},{7,1},{8,14},{9,15},{10,... | collective-permute-start | bytes 405512 | tf_op jit(solution)/shard_map/ppermute | solution.py:382
  27.8 11.4 %collective-permute-start.4 = (bf16[528,128]{1,0:T(8,128)(2,1)S(1)}, bf16[528,128]{1,0:T(8,128)(2,1)S(1)}, u32[]{:S(2)}, u32[]{:S(2)}) collective-permute-start(bf16[528,128]{1,0:T(8,128)(2,1)S(1)} %get-tuple-element.118.refs_0_), channel_id=1, source_target_pairs={{0,1},{1,0},{2,3},{3,2},{4,5},{5,4},{6,7},{7,6},{8,9},{9,8},{10,11... | collective-permute-start | bytes 405512 | tf_op jit(solution)/shard_map/ppermute | solution.py:382
  30.3 10.2 %collective-permute-start.6 = (bf16[528,128]{1,0:T(8,128)(2,1)S(1)}, bf16[528,128]{1,0:T(8,128)(2,1)S(1)}, u32[]{:S(2)}, u32[]{:S(2)}) collective-permute-start(bf16[528,128]{1,0:T(8,128)(2,1)S(1)} %collective-permute-done.5.refs_0_.refs_2_), channel_id=1, source_target_pairs={{0,1},{1,0},{2,3},{3,2},{4,5},{5,4},{6,7},{7,6},{8,9},{9,8},{10,11... | collective-permute-start | bytes 405512 | tf_op jit(solution)/shard_map/ppermute | solution.py:382
  32.9 8.4 %collective-permute-start.8 = (bf16[528,128]{1,0:T(8,128)(2,1)S(1)}, bf16[528,128]{1,0:T(8,128)(2,1)S(1)}, u32[]{:S(2)}, u32[]{:S(2)}) collective-permute-start(bf16[528,128]{1,0:T(8,128)(2,1)S(1)} %collective-permute-done.7.refs_1_.refs_4_), channel_id=1, source_target_pairs={{0,1},{1,0},{2,3},{3,2},{4,5},{5,4},{6,7},{7,6},{8,9},{9,8},{10,11... | collective-permute-start | bytes 405512 | tf_op jit(solution)/shard_map/ppermute | solution.py:382
  33.0 9.2 %collective-permute-start.10 = (bf16[528,128]{1,0:T(8,128)(2,1)S(1)}, bf16[528,128]{1,0:T(8,128)(2,1)S(1)}, u32[]{:S(2)}, u32[]{:S(2)}) collective-permute-start(bf16[528,128]{1,0:T(8,128)(2,1)S(1)} %collective-permute-done.9.refs_1_.refs_6_), channel_id=1, source_target_pairs={{0,1},{1,0},{2,3},{3,2},{4,5},{5,4},{6,7},{7,6},{8,9},{9,8},{10,11... | collective-permute-start | bytes 405512 | tf_op jit(solution)/shard_map/ppermute | solution.py:382
  42.6 7.5 %collective-permute-start.11 = (bf16[528,128]{1,0:T(8,128)(2,1)S(1)}, bf16[528,128]{1,0:T(8,128)(2,1)S(1)}, u32[]{:S(2)}, u32[]{:S(2)}) collective-permute-start(bf16[528,128]{1,0:T(8,128)(2,1)S(1)} %get-tuple-element.130), channel_id=1, source_target_pairs={{0,8},{8,0},{16,24},{24,16},{1,9},{9,1},{17,25},{25,17},{2,10},{10... | collective-permute-start | bytes 405512 | tf_op jit(solution)/shard_map/ppermute | solution.py:382
  44.2 13.1 %collective-permute-start.12 = (bf16[528,128]{1,0:T(8,128)(2,1)S(1)}, bf16[528,128]{1,0:T(8,128)(2,1)S(1)}, u32[]{:S(2)}, u32[]{:S(2)}) collective-permute-start(bf16[528,128]{1,0:T(8,128)(2,1)S(1)} %get-tuple-element.131), channel_id=1, source_target_pairs={{0,16},{8,24},{16,0},{24,8},{1,17},{9,25},{17,1},{25,9},{2,18},{10... | collective-permute-start | bytes 405512 | tf_op jit(solution)/shard_map/ppermute | solution.py:382
  46.8 10.6 %collective-permute-start.13 = (bf16[528,128]{1,0:T(8,128)(2,1)S(1)}, bf16[528,128]{1,0:T(8,128)(2,1)S(1)}, u32[]{:S(2)}, u32[]{:S(2)}) collective-permute-start(bf16[528,128]{1,0:T(8,128)(2,1)S(1)} %get-tuple-element.132), channel_id=1, source_target_pairs={{0,24},{8,16},{16,8},{24,0},{1,25},{9,17},{17,9},{25,1},{2,26},{10... | collective-permute-start | bytes 405512 | tf_op jit(solution)/shard_map/ppermute | solution.py:382
  57.6 6.7 %collective-permute-start.14 = (bf16[528,128]{1,0:T(8,128)(2,1)S(1)}, bf16[528,128]{1,0:T(8,128)(2,1)S(1)}, u32[]{:S(2)}, u32[]{:S(2)}) collective-permute-start(bf16[528,128]{1,0:T(8,128)(2,1)S(1)} %get-tuple-element.133.refs_0_.refs_1_), channel_id=1, source_target_pairs={{0,8},{8,0},{16,24},{24,16},{1,9},{9,1},{17,25},{25,17},{2,10},{10... | collective-permute-start | bytes 405512 | tf_op jit(solution)/shard_map/ppermute | solution.py:382
  59.9 12.3 %collective-permute-start.15 = (bf16[528,128]{1,0:T(8,128)(2,1)S(1)}, bf16[528,128]{1,0:T(8,128)(2,1)S(1)}, u32[]{:S(2)}, u32[]{:S(2)}) collective-permute-start(bf16[528,128]{1,0:T(8,128)(2,1)S(1)} %get-tuple-element.133.refs_0_.refs_1_), channel_id=1, source_target_pairs={{0,16},{8,24},{16,0},{24,8},{1,17},{9,25},{17,1},{25,9},{2,18},{10... | collective-permute-start | bytes 405512 | tf_op jit(solution)/shard_map/ppermute | solution.py:382
  61.0 12.7 %collective-permute-start.16 = (bf16[528,128]{1,0:T(8,128)(2,1)S(1)}, bf16[528,128]{1,0:T(8,128)(2,1)S(1)}, u32[]{:S(2)}, u32[]{:S(2)}) collective-permute-start(bf16[528,128]{1,0:T(8,128)(2,1)S(1)} %get-tuple-element.133.refs_0_.refs_1_), channel_id=1, source_target_pairs={{0,24},{8,16},{16,8},{24,0},{1,25},{9,17},{17,9},{25,1},{2,26},{10... | collective-permute-start | bytes 405512 | tf_op jit(solution)/shard_map/ppermute | solution.py:382
  76.5 6.3 %collective-permute-start.18 = (bf16[528,128]{1,0:T(8,128)(2,1)S(1)}, bf16[528,128]{1,0:T(8,128)(2,1)S(1)}, u32[]{:S(2)}, u32[]{:S(2)}) collective-permute-start(bf16[528,128]{1,0:T(8,128)(2,1)S(1)} %get-tuple-element.147), channel_id=1, source_target_pairs={{0,2},{1,3},{2,0},{3,1},{4,6},{5,7},{6,4},{7,5},{8,10},{9,11},{10,... | collective-permute-start | bytes 405512 | tf_op jit(solution)/shard_map/ppermute | solution.py:382
  77.9 8.2 %collective-permute-start.19 = (bf16[528,128]{1,0:T(8,128)(2,1)S(1)}, bf16[528,128]{1,0:T(8,128)(2,1)S(1)}, u32[]{:S(2)}, u32[]{:S(2)}) collective-permute-start(bf16[528,128]{1,0:T(8,128)(2,1)S(1)} %get-tuple-element.148), channel_id=1, source_target_pairs={{0,4},{1,5},{2,6},{3,7},{4,0},{5,1},{6,2},{7,3},{8,12},{9,13},{10,... | collective-permute-start | bytes 405512 | tf_op jit(solution)/shard_map/ppermute | solution.py:382
  78.8 7.4 %collective-permute-start.20 = (bf16[528,128]{1,0:T(8,128)(2,1)S(1)}, bf16[528,128]{1,0:T(8,128)(2,1)S(1)}, u32[]{:S(2)}, u32[]{:S(2)}) collective-permute-start(bf16[528,128]{1,0:T(8,128)(2,1)S(1)} %get-tuple-element.149), channel_id=1, source_target_pairs={{0,6},{1,7},{2,4},{3,5},{4,2},{5,3},{6,0},{7,1},{8,14},{9,15},{10,... | collective-permute-start | bytes 405512 | tf_op jit(solution)/shard_map/ppermute | solution.py:382
  86.4 6.4 %collective-permute-start.22 = (bf16[528,128]{1,0:T(8,128)(2,1)S(1)}, bf16[528,128]{1,0:T(8,128)(2,1)S(1)}, u32[]{:S(2)}, u32[]{:S(2)}) collective-permute-start(bf16[528,128]{1,0:T(8,128)(2,1)S(1)} %get-tuple-element.154.refs_0_), channel_id=1, source_target_pairs={{0,2},{1,3},{2,0},{3,1},{4,6},{5,7},{6,4},{7,5},{8,10},{9,11},{10,... | collective-permute-start | bytes 405512 | tf_op jit(solution)/shard_map/ppermute | solution.py:382
  87.2 7.8 %collective-permute-start.24 = (bf16[528,128]{1,0:T(8,128)(2,1)S(1)}, bf16[528,128]{1,0:T(8,128)(2,1)S(1)}, u32[]{:S(2)}, u32[]{:S(2)}) collective-permute-start(bf16[528,128]{1,0:T(8,128)(2,1)S(1)} %get-tuple-element.154.refs_0_), channel_id=1, source_target_pairs={{0,4},{1,5},{2,6},{3,7},{4,0},{5,1},{6,2},{7,3},{8,12},{9,13},{10,... | collective-permute-start | bytes 405512 | tf_op jit(solution)/shard_map/ppermute | solution.py:382
  88.5 6.5 %collective-permute-start.26 = (bf16[528,128]{1,0:T(8,128)(2,1)S(1)}, bf16[528,128]{1,0:T(8,128)(2,1)S(1)}, u32[]{:S(2)}, u32[]{:S(2)}) collective-permute-start(bf16[528,128]{1,0:T(8,128)(2,1)S(1)} %get-tuple-element.154.refs_0_), channel_id=1, source_target_pairs={{0,6},{1,7},{2,4},{3,5},{4,2},{5,3},{6,0},{7,1},{8,14},{9,15},{10,... | collective-permute-start | bytes 405512 | tf_op jit(solution)/shard_map/ppermute | solution.py:382
  90.0 5.5 %collective-permute-start.21 = (bf16[528,128]{1,0:T(8,128)(2,1)S(1)}, bf16[528,128]{1,0:T(8,128)(2,1)S(1)}, u32[]{:S(2)}, u32[]{:S(2)}) collective-permute-start(bf16[528,128]{1,0:T(8,128)(2,1)S(1)} %get-tuple-element.154.refs_0_), channel_id=1, source_target_pairs={{0,1},{1,0},{2,3},{3,2},{4,5},{5,4},{6,7},{7,6},{8,9},{9,8},{10,11... | collective-permute-start | bytes 405512 | tf_op jit(solution)/shard_map/ppermute | solution.py:382
  92.8 4.0 %collective-permute-start.23 = (bf16[528,128]{1,0:T(8,128)(2,1)S(1)}, bf16[528,128]{1,0:T(8,128)(2,1)S(1)}, u32[]{:S(2)}, u32[]{:S(2)}) collective-permute-start(bf16[528,128]{1,0:T(8,128)(2,1)S(1)} %collective-permute-done.22.refs_0_.refs_2_), channel_id=1, source_target_pairs={{0,1},{1,0},{2,3},{3,2},{4,5},{5,4},{6,7},{7,6},{8,9},{9,8},{10,11... | collective-permute-start | bytes 405512 | tf_op jit(solution)/shard_map/ppermute | solution.py:382
  95.0 2.6 %collective-permute-start.25 = (bf16[528,128]{1,0:T(8,128)(2,1)S(1)}, bf16[528,128]{1,0:T(8,128)(2,1)S(1)}, u32[]{:S(2)}, u32[]{:S(2)}) collective-permute-start(bf16[528,128]{1,0:T(8,128)(2,1)S(1)} %collective-permute-done.24.refs_1_.refs_4_), channel_id=1, source_target_pairs={{0,1},{1,0},{2,3},{3,2},{4,5},{5,4},{6,7},{7,6},{8,9},{9,8},{10,11... | collective-permute-start | bytes 405512 | tf_op jit(solution)/shard_map/ppermute | solution.py:382
  95.0 3.4 %collective-permute-start.27 = (bf16[528,128]{1,0:T(8,128)(2,1)S(1)}, bf16[528,128]{1,0:T(8,128)(2,1)S(1)}, u32[]{:S(2)}, u32[]{:S(2)}) collective-permute-start(bf16[528,128]{1,0:T(8,128)(2,1)S(1)} %collective-permute-done.26.refs_1_.refs_6_), channel_id=1, source_target_pairs={{0,1},{1,0},{2,3},{3,2},{4,5},{5,4},{6,7},{7,6},{8,9},{9,8},{10,11... | collective-permute-start | bytes 405512 | tf_op jit(solution)/shard_map/ppermute | solution.py:382
  98.8 7.8 %collective-permute-start.28 = (bf16[528,128]{1,0:T(8,128)(2,1)S(1)}, bf16[528,128]{1,0:T(8,128)(2,1)S(1)}, u32[]{:S(2)}, u32[]{:S(2)}) collective-permute-start(bf16[528,128]{1,0:T(8,128)(2,1)S(1)} %get-tuple-element.167), channel_id=1, source_target_pairs={{0,8},{8,0},{16,24},{24,16},{1,9},{9,1},{17,25},{25,17},{2,10},{10... | collective-permute-start | bytes 405512 | tf_op jit(solution)/shard_map/ppermute | solution.py:382
  99.3 13.1 %collective-permute-start.29 = (bf16[528,128]{1,0:T(8,128)(2,1)S(1)}, bf16[528,128]{1,0:T(8,128)(2,1)S(1)}, u32[]{:S(2)}, u32[]{:S(2)}) collective-permute-start(bf16[528,128]{1,0:T(8,128)(2,1)S(1)} %get-tuple-element.168), channel_id=1, source_target_pairs={{0,16},{8,24},{16,0},{24,8},{1,17},{9,25},{17,1},{25,9},{2,18},{10... | collective-permute-start | bytes 405512 | tf_op jit(solution)/shard_map/ppermute | solution.py:382
  101.4 11.1 %collective-permute-start.30 = (bf16[528,128]{1,0:T(8,128)(2,1)S(1)}, bf16[528,128]{1,0:T(8,128)(2,1)S(1)}, u32[]{:S(2)}, u32[]{:S(2)}) collective-permute-start(bf16[528,128]{1,0:T(8,128)(2,1)S(1)} %get-tuple-element.169), channel_id=1, source_target_pairs={{0,24},{8,16},{16,8},{24,0},{1,25},{9,17},{17,9},{25,1},{2,26},{10... | collective-permute-start | bytes 405512 | tf_op jit(solution)/shard_map/ppermute | solution.py:382
  112.7 6.8 %collective-permute-start.31 = (bf16[528,128]{1,0:T(8,128)(2,1)S(1)}, bf16[528,128]{1,0:T(8,128)(2,1)S(1)}, u32[]{:S(2)}, u32[]{:S(2)}) collective-permute-start(bf16[528,128]{1,0:T(8,128)(2,1)S(1)} %get-tuple-element.172.refs_0_.refs_5_), channel_id=1, source_target_pairs={{0,8},{8,0},{16,24},{24,16},{1,9},{9,1},{17,25},{25,17},{2,10},{10... | collective-permute-start | bytes 405512 | tf_op jit(solution)/shard_map/ppermute | solution.py:382
  115.0 12.4 %collective-permute-start.32 = (bf16[528,128]{1,0:T(8,128)(2,1)S(1)}, bf16[528,128]{1,0:T(8,128)(2,1)S(1)}, u32[]{:S(2)}, u32[]{:S(2)}) collective-permute-start(bf16[528,128]{1,0:T(8,128)(2,1)S(1)} %get-tuple-element.172.refs_0_.refs_5_), channel_id=1, source_target_pairs={{0,16},{8,24},{16,0},{24,8},{1,17},{9,25},{17,1},{25,9},{2,18},{10... | collective-permute-start | bytes 405512 | tf_op jit(solution)/shard_map/ppermute | solution.py:382
  116.1 12.8 %collective-permute-start.33 = (bf16[528,128]{1,0:T(8,128)(2,1)S(1)}, bf16[528,128]{1,0:T(8,128)(2,1)S(1)}, u32[]{:S(2)}, u32[]{:S(2)}) collective-permute-start(bf16[528,128]{1,0:T(8,128)(2,1)S(1)} %get-tuple-element.172.refs_0_.refs_5_), channel_id=1, source_target_pairs={{0,24},{8,16},{16,8},{24,0},{1,25},{9,17},{17,9},{25,1},{2,26},{10... | collective-permute-start | bytes 405512 | tf_op jit(solution)/shard_map/ppermute | solution.py:382
  131.8 6.5 %collective-permute-start.35 = (bf16[528,128]{1,0:T(8,128)(2,1)S(1)}, bf16[528,128]{1,0:T(8,128)(2,1)S(1)}, u32[]{:S(2)}, u32[]{:S(2)}) collective-permute-start(bf16[528,128]{1,0:T(8,128)(2,1)S(1)} %get-tuple-element.188), channel_id=1, source_target_pairs={{0,2},{1,3},{2,0},{3,1},{4,6},{5,7},{6,4},{7,5},{8,10},{9,11},{10,... | collective-permute-start | bytes 405512 | tf_op jit(solution)/shard_map/ppermute | solution.py:382
  132.8 8.2 %collective-permute-start.36 = (bf16[528,128]{1,0:T(8,128)(2,1)S(1)}, bf16[528,128]{1,0:T(8,128)(2,1)S(1)}, u32[]{:S(2)}, u32[]{:S(2)}) collective-permute-start(bf16[528,128]{1,0:T(8,128)(2,1)S(1)} %get-tuple-element.189), channel_id=1, source_target_pairs={{0,4},{1,5},{2,6},{3,7},{4,0},{5,1},{6,2},{7,3},{8,12},{9,13},{10,... | collective-permute-start | bytes 405512 | tf_op jit(solution)/shard_map/ppermute | solution.py:382
  134.0 7.0 %collective-permute-start.37 = (bf16[528,128]{1,0:T(8,128)(2,1)S(1)}, bf16[528,128]{1,0:T(8,128)(2,1)S(1)}, u32[]{:S(2)}, u32[]{:S(2)}) collective-permute-start(bf16[528,128]{1,0:T(8,128)(2,1)S(1)} %get-tuple-element.190), channel_id=1, source_target_pairs={{0,6},{1,7},{2,4},{3,5},{4,2},{5,3},{6,0},{7,1},{8,14},{9,15},{10,... | collective-permute-start | bytes 405512 | tf_op jit(solution)/shard_map/ppermute | solution.py:382
  141.9 6.3 %collective-permute-start.39 = (bf16[528,128]{1,0:T(8,128)(2,1)S(1)}, bf16[528,128]{1,0:T(8,128)(2,1)S(1)}, u32[]{:S(2)}, u32[]{:S(2)}) collective-permute-start(bf16[528,128]{1,0:T(8,128)(2,1)S(1)} %get-tuple-element.194.refs_0_), channel_id=1, source_target_pairs={{0,2},{1,3},{2,0},{3,1},{4,6},{5,7},{6,4},{7,5},{8,10},{9,11},{10,... | collective-permute-start | bytes 405512 | tf_op jit(solution)/shard_map/ppermute | solution.py:382
  143.0 7.4 %collective-permute-start.41 = (bf16[528,128]{1,0:T(8,128)(2,1)S(1)}, bf16[528,128]{1,0:T(8,128)(2,1)S(1)}, u32[]{:S(2)}, u32[]{:S(2)}) collective-permute-start(bf16[528,128]{1,0:T(8,128)(2,1)S(1)} %get-tuple-element.194.refs_0_), channel_id=1, source_target_pairs={{0,4},{1,5},{2,6},{3,7},{4,0},{5,1},{6,2},{7,3},{8,12},{9,13},{10,... | collective-permute-start | bytes 405512 | tf_op jit(solution)/shard_map/ppermute | solution.py:382
  144.1 6.4 %collective-permute-start.43 = (bf16[528,128]{1,0:T(8,128)(2,1)S(1)}, bf16[528,128]{1,0:T(8,128)(2,1)S(1)}, u32[]{:S(2)}, u32[]{:S(2)}) collective-permute-start(bf16[528,128]{1,0:T(8,128)(2,1)S(1)} %get-tuple-element.194.refs_0_), channel_id=1, source_target_pairs={{0,6},{1,7},{2,4},{3,5},{4,2},{5,3},{6,0},{7,1},{8,14},{9,15},{10,... | collective-permute-start | bytes 405512 | tf_op jit(solution)/shard_map/ppermute | solution.py:382
  145.3 5.6 %collective-permute-start.38 = (bf16[528,128]{1,0:T(8,128)(2,1)S(1)}, bf16[528,128]{1,0:T(8,128)(2,1)S(1)}, u32[]{:S(2)}, u32[]{:S(2)}) collective-permute-start(bf16[528,128]{1,0:T(8,128)(2,1)S(1)} %get-tuple-element.194.refs_0_), channel_id=1, source_target_pairs={{0,1},{1,0},{2,3},{3,2},{4,5},{5,4},{6,7},{7,6},{8,9},{9,8},{10,11... | collective-permute-start | bytes 405512 | tf_op jit(solution)/shard_map/ppermute | solution.py:382
  148.1 4.1 %collective-permute-start.40 = (bf16[528,128]{1,0:T(8,128)(2,1)S(1)}, bf16[528,128]{1,0:T(8,128)(2,1)S(1)}, u32[]{:S(2)}, u32[]{:S(2)}) collective-permute-start(bf16[528,128]{1,0:T(8,128)(2,1)S(1)} %collective-permute-done.39.refs_0_.refs_2_), channel_id=1, source_target_pairs={{0,1},{1,0},{2,3},{3,2},{4,5},{5,4},{6,7},{7,6},{8,9},{9,8},{10,11... | collective-permute-start | bytes 405512 | tf_op jit(solution)/shard_map/ppermute | solution.py:382
  150.4 2.6 %collective-permute-start.42 = (bf16[528,128]{1,0:T(8,128)(2,1)S(1)}, bf16[528,128]{1,0:T(8,128)(2,1)S(1)}, u32[]{:S(2)}, u32[]{:S(2)}) collective-permute-start(bf16[528,128]{1,0:T(8,128)(2,1)S(1)} %collective-permute-done.41.refs_1_.refs_4_), channel_id=1, source_target_pairs={{0,1},{1,0},{2,3},{3,2},{4,5},{5,4},{6,7},{7,6},{8,9},{9,8},{10,11... | collective-permute-start | bytes 405512 | tf_op jit(solution)/shard_map/ppermute | solution.py:382
  150.4 3.4 %collective-permute-start.44 = (bf16[528,128]{1,0:T(8,128)(2,1)S(1)}, bf16[528,128]{1,0:T(8,128)(2,1)S(1)}, u32[]{:S(2)}, u32[]{:S(2)}) collective-permute-start(bf16[528,128]{1,0:T(8,128)(2,1)S(1)} %collective-permute-done.43.refs_1_.refs_6_), channel_id=1, source_target_pairs={{0,1},{1,0},{2,3},{3,2},{4,5},{5,4},{6,7},{7,6},{8,9},{9,8},{10,11... | collective-permute-start | bytes 405512 | tf_op jit(solution)/shard_map/ppermute | solution.py:382
  154.3 7.9 %collective-permute-start.45 = (bf16[528,128]{1,0:T(8,128)(2,1)S(1)}, bf16[528,128]{1,0:T(8,128)(2,1)S(1)}, u32[]{:S(2)}, u32[]{:S(2)}) collective-permute-start(bf16[528,128]{1,0:T(8,128)(2,1)S(1)} %get-tuple-element.207), channel_id=1, source_target_pairs={{0,8},{8,0},{16,24},{24,16},{1,9},{9,1},{17,25},{25,17},{2,10},{10... | collective-permute-start | bytes 405512 | tf_op jit(solution)/shard_map/ppermute | solution.py:382
  154.8 13.2 %collective-permute-start.46 = (bf16[528,128]{1,0:T(8,128)(2,1)S(1)}, bf16[528,128]{1,0:T(8,128)(2,1)S(1)}, u32[]{:S(2)}, u32[]{:S(2)}) collective-permute-start(bf16[528,128]{1,0:T(8,128)(2,1)S(1)} %get-tuple-element.208), channel_id=1, source_target_pairs={{0,16},{8,24},{16,0},{24,8},{1,17},{9,25},{17,1},{25,9},{2,18},{10... | collective-permute-start | bytes 405512 | tf_op jit(solution)/shard_map/ppermute | solution.py:382
  156.8 11.1 %collective-permute-start.47 = (bf16[528,128]{1,0:T(8,128)(2,1)S(1)}, bf16[528,128]{1,0:T(8,128)(2,1)S(1)}, u32[]{:S(2)}, u32[]{:S(2)}) collective-permute-start(bf16[528,128]{1,0:T(8,128)(2,1)S(1)} %get-tuple-element.209), channel_id=1, source_target_pairs={{0,24},{8,16},{16,8},{24,0},{1,25},{9,17},{17,9},{25,1},{2,26},{10... | collective-permute-start | bytes 405512 | tf_op jit(solution)/shard_map/ppermute | solution.py:382
  168.8 6.7 %collective-permute-start.48 = (bf16[528,128]{1,0:T(8,128)(2,1)S(1)}, bf16[528,128]{1,0:T(8,128)(2,1)S(1)}, u32[]{:S(2)}, u32[]{:S(2)}) collective-permute-start(bf16[528,128]{1,0:T(8,128)(2,1)S(1)} %get-tuple-element.215.refs_0_), channel_id=1, source_target_pairs={{0,8},{8,0},{16,24},{24,16},{1,9},{9,1},{17,25},{25,17},{2,10},{10... | collective-permute-start | bytes 405512 | tf_op jit(solution)/shard_map/ppermute | solution.py:382
  171.1 12.4 %collective-permute-start.49 = (bf16[528,128]{1,0:T(8,128)(2,1)S(1)}, bf16[528,128]{1,0:T(8,128)(2,1)S(1)}, u32[]{:S(2)}, u32[]{:S(2)}) collective-permute-start(bf16[528,128]{1,0:T(8,128)(2,1)S(1)} %get-tuple-element.215.refs_0_), channel_id=1, source_target_pairs={{0,16},{8,24},{16,0},{24,8},{1,17},{9,25},{17,1},{25,9},{2,18},{10... | collective-permute-start | bytes 405512 | tf_op jit(solution)/shard_map/ppermute | solution.py:382
  172.1 11.4 %collective-permute-start.50 = (bf16[528,128]{1,0:T(8,128)(2,1)S(1)}, bf16[528,128]{1,0:T(8,128)(2,1)S(1)}, u32[]{:S(2)}, u32[]{:S(2)}) collective-permute-start(bf16[528,128]{1,0:T(8,128)(2,1)S(1)} %get-tuple-element.215.refs_0_), channel_id=1, source_target_pairs={{0,24},{8,16},{16,8},{24,0},{1,25},{9,17},{17,9},{25,1},{2,26},{10... | collective-permute-start | bytes 405512 | tf_op jit(solution)/shard_map/ppermute | solution.py:382
  (5 other events, 26.5 us)

commit v3 on v2

--- a/solution.py
+++ b/solution.py
@@ -12,8 +12,25 @@
 RIDGE = 0.2
 TAIL = 16
 
-GROUP = 8
+GROUP = 32
 CHUNKS = 8
+
+
+def crossed(k, n):
+    return (k & ~3) | ((k & 1) << 1) | ((k >> 1) & 1) if n > 2 else k
+
+
+def row_partners(n):
+    basis = [n - 1, *(1 << b for b in range(n.bit_length() - 2))]
+    order = [0]
+    for value in basis:
+        order += [k ^ value for k in order]
+    return order
+
+
+def partner(order, i, odd):
+    k = order[i]
+    return k + odd * (crossed(k, len(order)) - k)
 
 
 def row_order(n):
@@ -74,8 +91,14 @@
     return lax.axis_index("col"), lax.axis_index("row")
 
 
-def place_of(cfg, relative):
-    return (relative & 1) * (cfg["cols"] // 2) + (relative >> 1)
+def row_slot(cfg, i):
+    c, z = here()
+    return z ^ partner(row_partners(cfg["rows"]), i, c & 1)
+
+
+def column_slot(cfg, i, across):
+    c = here()[0] ^ across
+    return c ^ (2 * partner(range(cfg["cols"] // 2), i, c & 1))
 
 
 def first_kernel(
@@ -88,6 +111,7 @@
     keep_tail,
     direction,
     ids,
+    places,
     x,
     near,
     held,
@@ -95,7 +119,11 @@
     arrived,
 ):
     fb, nb = cfg["fb"], cfg["nb"]
-    c, z = here()
+    chips = cfg["cols"] // 2
+    for across in range(2):
+        for i in range(chips):
+            places[column_slot(cfg, i, across)] = across * chips + i
+    z = here()[1]
     count = ids.shape[0]
     size = count // CHUNKS
     numbers = pltpu.make_async_copy(ids_far, ids, arrived.at[CHUNKS + 1])
@@ -126,7 +154,7 @@
                 a = ids[k] // fb
                 b = ids[k] - a * fb
                 slot = a // nb
-                target = place_of(cfg, slot ^ c) * nb + (a - slot * nb)
+                target = places[slot] * nb + (a - slot * nb)
                 products.append((target, jnp.dot(x[k], held[b], preferred_element_type=f32)))
             for target, product in products:
                 total[target] = total[target] + product
@@ -187,7 +215,7 @@
         span = slice(i * rows, (i + 1) * rows)
         product = sum(
             jnp.dot(
-                x[here()[1] ^ g, span, :], part[: x.shape[2], :], preferred_element_type=f32
+                x[row_slot(cfg, g), span, :], part[: x.shape[2], :], preferred_element_type=f32
             )
             for g, part in zip(group, parts)
         )
@@ -202,12 +230,12 @@
     rows = cfg["nb"] * cfg["width"]
     chips = cfg["cols"] // 2
     for i in range(chips):
-        slot = (2 * i + (1 if sent else 0)) ^ here()[0]
+        slot = column_slot(cfg, i, 1 if sent else 0)
         span = pl.ds(pl.multiple_of(slot * rows, rows), rows)
         value = total[span, :]
         for g in group:
             value = value + jnp.dot(
-                x[here()[1] ^ g, span, :], parts[g][: x.shape[2], :], preferred_element_type=f32
+                x[row_slot(cfg, g), span, :], parts[g][: x.shape[2], :], preferred_element_type=f32
             )
         out[i * rows : (i + 1) * rows, :] = value.astype(out.dtype)
     if sent:
@@ -278,7 +306,8 @@
     rows = cfg["nb"] * cfg["width"]
     products = []
     for g, part in zip(group, near):
-        span = pl.ds(pl.multiple_of((here()[0] ^ g) * rows, rows), rows)
+        slot = column_slot(cfg, g // 2, g % 2)
+        span = pl.ds(pl.multiple_of(slot * rows, rows), rows)
         products.append(jnp.dot(part, x[h, span, :], preferred_element_type=f32))
     return sum(products)
 
@@ -304,7 +333,7 @@
         outs[-1][...] = tile
     for k in range(1, cfg["rows"]) if sent else [0]:
         out = outs[k - 1] if sent else outs[0]
-        h = here()[1] ^ k
+        h = row_slot(cfg, k)
         value = total[h] + backward_sum(cfg, group, x, near, h)
         for j in range(cfg["zb"]):
             out[j * width : (j + 1) * width, :] = value[:, j * width : (j + 1) * width].astype(
@@ -343,7 +372,7 @@
     alphas, betas, out = rest[:count], rest[count : 2 * count - 1], rest[-1]
     rows = grads.shape[0] // others
     for k in range(others):
-        span = pl.ds(pl.multiple_of((here()[1] ^ k) * rows, rows), rows)
+        span = pl.ds(pl.multiple_of(row_slot(cfg, k) * rows, rows), rows)
         d = grads[span, :]
         total = alphas[0][0:1, :] * d
         for j in range(1, count):
@@ -357,7 +386,7 @@
     shares, out = refs[:-1], refs[-1]
     rows = out.shape[0] // cfg["rows"]
     for k, share in enumerate(shares):
-        span = pl.ds(pl.multiple_of((here()[1] ^ k) * rows, rows), rows)
+        span = pl.ds(pl.multiple_of(row_slot(cfg, k) * rows, rows), rows)
         out[span, :] = share[:rows, :].astype(f32)
 
 
@@ -377,13 +406,30 @@
     def shape(rows, dtype):
         return jax.ShapeDtypeStruct((rows, directions), dtype)
 
-    def along(axis, value, k):
-        n = rows_axis if axis == "row" else cols
-        return lax.ppermute(value, axis, [(i, i ^ k) for i in range(n)])
-
-    def exchange(axis, values, order, step=1):
-        received = {k: along(axis, values[k - 1], step * k) for k in order}
-        return [received[k] for k in range(1, len(order) + 1)]
+    def moved(value, to):
+        pairs = [(r * cols + q, to(r, q)) for r in range(rows_axis) for q in range(cols)]
+        return lax.ppermute(value, ("row", "col"), pairs)
+
+    def across(value):
+        return moved(value, lambda r, q: r * cols + (q ^ 1))
+
+    def along_row(values):
+        return [
+            moved(
+                values[i - 1],
+                lambda r, q, i=i: (r ^ partner(row_partners(rows_axis), i, q & 1)) * cols + q,
+            )
+            for i in row_order(rows_axis)
+        ]
+
+    def along_col(values):
+        return [
+            moved(
+                values[i - 1],
+                lambda r, q, i=i: r * cols + (q ^ (2 * partner(range(chips), i, q & 1))),
+            )
+            for i in chip_order(chips)
+        ]
 
     def near(value):
         return pltpu.with_memory_space_constraint(value, pltpu.VMEM)
@@ -434,6 +480,7 @@
             out_specs=[VMEM] * 4,
             scratch_shapes=[
                 pltpu.SMEM(ids.shape, jnp.int32),
+                pltpu.SMEM((cols,), jnp.int32),
                 pltpu.VMEM(x_blocks.shape, bf16),
                 pltpu.VMEM(grads.shape, f32),
                 pltpu.VMEM((fb, width, directions), bf16),
@@ -480,10 +527,10 @@
         return send, keep, keep_tail
 
     def backward(scaled, first):
-        others = exchange("col", [scaled] * (chips - 1), chip_order(chips), 2)
+        others = along_col([scaled] * (chips - 1))
         parts = []
         for part in [scaled, *others]:
-            parts += [part, along("col", part, 1)]
+            parts += [part, across(part)]
         total = []
         *groups, group = column_groups(chips)
         for some in groups:
@@ -507,8 +554,7 @@
 
     row_ids = z * margins.shape[0] + c * own_rows + jnp.arange(own_rows, dtype=jnp.int32)
     row_ids = row_ids.reshape(nb, width)
-    removed = jnp.any(row_ids[None] == deleted[:, None, None], axis=0)
-    removed = removed.astype(f32)
+    removed = jnp.any(row_ids[None] == deleted[:, None, None], axis=0).astype(f32)
     margins = margins.reshape(rb, width)
     parts, shares, alphas, betas = [], [], [], []
     share = spread = before = None
@@ -519,17 +565,17 @@
             send, keep, keep_tail, direction = begin()
             residual = direction
         else:
-            parts = [share, *exchange("row", [share] * (rows_axis - 1), row_order(rows_axis))]
+            parts = [share, *along_row([share] * (rows_axis - 1))]
             shares += parts
             send, keep, keep_tail = forward(parts)
-        received = along("col", send, 1)
+        received = across(send)
         own, own_tail, *sends = call(
             functools.partial(merge_kernel, cfg),
             [shape(own_rows, f32), shape(TAIL, bf16)]
             + [shape(own_rows + TAIL, bf16)] * (chips - 1),
             [keep, keep_tail, received],
         )
-        received = exchange("col", sends, chip_order(chips), 2)
+        received = along_col(sends)
         if first:
             matrix.append(lay_out())
             scaled, before, spread = call(
@@ -551,7 +597,7 @@
             )
             betas.append(beta)
         sends, own, own_tail = backward(scaled, first)
-        received = exchange("row", sends, row_order(rows_axis))
+        received = along_row(sends)
         share, residual, norm_now, alpha = call(
             functools.partial(update_kernel, cfg, first),
             [
@@ -563,7 +609,7 @@
             [own, own_tail, *received, direction, residual, norm_now],
         )
         alphas.append(alpha)
-    parts = [share, *exchange("row", [share] * (rows_axis - 1), row_order(rows_axis))]
+    parts = [share, *along_row([share] * (rows_axis - 1))]
     (answer,) = call(
         functools.partial(result_kernel, cfg, ITERS),
         [shape(fb * width, f32)],

time: 185 us -> 178 us (0.962)
  Pallas kernels: 42.4 us -> 38.1 us
    pallas_call x1, Pallas kernels: 9.31 us -> 6.13 us  [begin(): pl.pallas_call(functools.partial(first_kernel, cfg), out_shape=[pltpu.VME...]
  transfers between devices with their start and end apart: 51 -> 51, of which waited for: 27 -> 32; matrix products, arithmetic and copies ran while one was open for 0% -> 1% of each run, Pallas kernels for 14% -> 14%
where the time goes in v3:
time: 178 us
  waiting for transfers between devices  85.9 us (48%)
  starting transfers between devices  51.3 us (29%)
  Pallas kernels  38.1 us (21%)
    ppermute x51, waiting for transfers between devices, moved(): return lax.ppermute(value, ('row', 'col'), pairs)  85.9 us
    ppermute x51, starting transfers between devices, moved(): return lax.ppermute(value, ('row', 'col'), pairs)  51.3 us
    pallas_call x39, Pallas kernels, call(): pl.pallas_call(kernel, out_shape=out, in_specs=[VMEM] * len(inputs), out_...  27.3 us
    pallas_call x1, Pallas kernels, begin(): pl.pallas_call(functools.partial(first_kernel, cfg), out_shape=[pltpu.VME...  6.13 us
    pallas_call x1, Pallas kernels, lay_out(): pl.pallas_call(functools.partial(dense_kernel, cfg), out_shape=pltpu.VMEM...  4.67 us
  transfers between devices with their start and end apart: 51, of which 32 were waited for; matrix products, arithmetic and copies ran while one was open for 1% of the time, Pallas kernels for 14%

profile of v3, /device:TPU:0, one launch (start us, length us, event | category | flops | bytes accessed | tf_op | source)
XLA Modules:
  0.0 177.9 jit_solution(11472106022256205378)
XLA Ops:
  0.6 6.1 %shard_map.68 = (bf16[2064,128]{1,0:T(8,128)(2,1)S(1)}, f32[2048,128]{1,0:T(8,128)S(1)}, bf16[16,128]{1,0:T(8,128)(2,1)S(1)}, f32[512,128]{1,0:T(8,128)S(1)}) custom-call(s32[256]{0:T(256)} %bitcast.3, bf16[256,128,128]{2,1,0:T(8,128)(2,1)} %listed.3, f32[2048,128]{1,0:T(8,128)} %refs_0_.1), custom_call_target="tpu_custom_call" | custom-call | tf_op jit(solution)/shard_map/pallas_call | solution.py:471
  7.3 1.5 collective-permute-done.refs_2_
  9.0 2.9 %collective-permute-start.1 = (bf16[528,128]{1,0:T(8,128)(2,1)S(1)}, bf16[528,128]{1,0:T(8,128)(2,1)S(1)}, u32[]{:S(2)}, u32[]{:S(2)}) collective-permute-start(bf16[528,128]{1,0:T(8,128)(2,1)S(1)} %get-tuple-element.114), channel_id=1, source_target_pairs={{0,2},{1,5},{2,0},{3,7},{4,6},{5,1},{6,4},{7,3},{8,10},{9,13},{10,... | collective-permute-start | bytes 405512 | tf_op jit(solution)/shard_map/ppermute | solution.py:411
  11.9 1.5 collective-permute-start.2
  15.4 3.4 %collective-permute-done.2.refs_3_ = bf16[528,128]{1,0:T(8,128)(2,1)S(1)} collective-permute-done((bf16[528,128]{1,0:T(8,128)(2,1)S(1)}, bf16[528,128]{1,0:T(8,128)(2,1)S(1)}, u32[]{:S(2)}, u32[]{:S(2)}) %collective-permute-start.2) | collective-permute-done | bytes 135200 | tf_op jit(solution)/shard_map/ppermute | solution.py:411
  20.9 1.7 collective-permute-start.5
  24.5 3.0 %collective-permute-done.5.refs_0_.refs_2_ = bf16[528,128]{1,0:T(8,128)(2,1)S(1)} collective-permute-done((bf16[528,128]{1,0:T(8,128)(2,1)S(1)}, bf16[528,128]{1,0:T(8,128)(2,1)S(1)}, u32[]{:S(2)}, u32[]{:S(2)}) %collective-permute-start.5) | collective-permute-done | bytes 135200 | tf_op jit(solution)/shard_map/ppermute | solution.py:411
  27.4 3.1 %collective-permute-done.7.refs_1_.refs_4_ = bf16[528,128]{1,0:T(8,128)(2,1)S(1)} collective-permute-done((bf16[528,128]{1,0:T(8,128)(2,1)S(1)}, bf16[528,128]{1,0:T(8,128)(2,1)S(1)}, u32[]{:S(2)}, u32[]{:S(2)}) %collective-permute-start.7) | collective-permute-done | bytes 135200 | tf_op jit(solution)/shard_map/ppermute | solution.py:411
  31.0 4.7 %shard_map.71.refs_2_ = bf16[4,4096,512]{2,1,0:T(8,128)(2,1)S(1)} custom-call(s32[256]{0:T(256)} %bitcast.4, bf16[256,128,128]{2,1,0:T(8,128)(2,1)} %listed.3), custom_call_target="tpu_custom_call" | custom-call | tf_op jit(solution)/shard_map/pallas_call | solution.py:494
  39.1 3.7 %collective-permute-start.11 = (bf16[528,128]{1,0:T(8,128)(2,1)S(1)}, bf16[528,128]{1,0:T(8,128)(2,1)S(1)}, u32[]{:S(2)}, u32[]{:S(2)}) collective-permute-start(bf16[528,128]{1,0:T(8,128)(2,1)S(1)} %get-tuple-element.130), channel_id=1, source_target_pairs={{0,24},{1,25},{2,26},{3,27},{4,28},{5,29},{6,30},{7,31},{8,16},{9,... | collective-permute-start | bytes 405512 | tf_op jit(solution)/shard_map/ppermute | solution.py:411
  43.8 3.7 %collective-permute-done.11.refs_2_ = bf16[528,128]{1,0:T(8,128)(2,1)S(1)} collective-permute-done((bf16[528,128]{1,0:T(8,128)(2,1)S(1)}, bf16[528,128]{1,0:T(8,128)(2,1)S(1)}, u32[]{:S(2)}, u32[]{:S(2)}) %collective-permute-start.11) | collective-permute-done | bytes 135200 | tf_op jit(solution)/shard_map/ppermute | solution.py:411
  47.5 2.4 %collective-permute-done.12.refs_3_ = bf16[528,128]{1,0:T(8,128)(2,1)S(1)} collective-permute-done((bf16[528,128]{1,0:T(8,128)(2,1)S(1)}, bf16[528,128]{1,0:T(8,128)(2,1)S(1)}, u32[]{:S(2)}, u32[]{:S(2)}) %collective-permute-start.12) | collective-permute-done | bytes 135200 | tf_op jit(solution)/shard_map/ppermute | solution.py:411
  49.9 4.4 %collective-permute-done.13.refs_4_ = bf16[528,128]{1,0:T(8,128)(2,1)S(1)} collective-permute-done((bf16[528,128]{1,0:T(8,128)(2,1)S(1)}, bf16[528,128]{1,0:T(8,128)(2,1)S(1)}, u32[]{:S(2)}, u32[]{:S(2)}) %collective-permute-start.13) | collective-permute-done | bytes 135200 | tf_op jit(solution)/shard_map/ppermute | solution.py:411
  54.5 2.6 %collective-permute-start.14 = (bf16[528,128]{1,0:T(8,128)(2,1)S(1)}, bf16[528,128]{1,0:T(8,128)(2,1)S(1)}, u32[]{:S(2)}, u32[]{:S(2)}) collective-permute-start(bf16[528,128]{1,0:T(8,128)(2,1)S(1)} %get-tuple-element.133.refs_0_.refs_1_), channel_id=1, source_target_pairs={{0,24},{1,25},{2,26},{3,27},{4,28},{5,29},{6,30},{7,31},{8,16},{9,... | collective-permute-start | bytes 405512 | tf_op jit(solution)/shard_map/ppermute | solution.py:411
  57.1 1.9 %collective-permute-start.16 = (bf16[528,128]{1,0:T(8,128)(2,1)S(1)}, bf16[528,128]{1,0:T(8,128)(2,1)S(1)}, u32[]{:S(2)}, u32[]{:S(2)}) collective-permute-start(bf16[528,128]{1,0:T(8,128)(2,1)S(1)} %get-tuple-element.133.refs_0_.refs_1_), channel_id=1, source_target_pairs={{0,16},{1,9},{2,18},{3,11},{4,20},{5,13},{6,22},{7,15},{8,24},{9,1... | collective-permute-start | bytes 405512 | tf_op jit(solution)/shard_map/ppermute | solution.py:411
  60.2 2.6 %collective-permute-done.14.refs_0_.refs_1_.refs_2_ = bf16[528,128]{1,0:T(8,128)(2,1)S(1)} collective-permute-done((bf16[528,128]{1,0:T(8,128)(2,1)S(1)}, bf16[528,128]{1,0:T(8,128)(2,1)S(1)}, u32[]{:S(2)}, u32[]{:S(2)}) %collective-permute-start.14) | collective-permute-done | bytes 135200 | tf_op jit(solution)/shard_map/ppermute | solution.py:411
  62.8 1.5 shard_map.80
  64.4 2.1 %collective-permute-done.15.refs_0_.refs_2_.refs_3_ = bf16[528,128]{1,0:T(8,128)(2,1)S(1)} collective-permute-done((bf16[528,128]{1,0:T(8,128)(2,1)S(1)}, bf16[528,128]{1,0:T(8,128)(2,1)S(1)}, u32[]{:S(2)}, u32[]{:S(2)}) %collective-permute-start.15) | collective-permute-done | bytes 135200 | tf_op jit(solution)/shard_map/ppermute | solution.py:411
  66.5 1.6 shard_map.81
  70.9 2.1 %collective-permute-start.18 = (bf16[528,128]{1,0:T(8,128)(2,1)S(1)}, bf16[528,128]{1,0:T(8,128)(2,1)S(1)}, u32[]{:S(2)}, u32[]{:S(2)}) collective-permute-start(bf16[528,128]{1,0:T(8,128)(2,1)S(1)} %get-tuple-element.147), channel_id=1, source_target_pairs={{0,2},{1,5},{2,0},{3,7},{4,6},{5,1},{6,4},{7,3},{8,10},{9,13},{10,... | collective-permute-start | bytes 405512 | tf_op jit(solution)/shard_map/ppermute | solution.py:411
  74.7 2.0 %collective-permute-done.18.refs_2_ = bf16[528,128]{1,0:T(8,128)(2,1)S(1)} collective-permute-done((bf16[528,128]{1,0:T(8,128)(2,1)S(1)}, bf16[528,128]{1,0:T(8,128)(2,1)S(1)}, u32[]{:S(2)}, u32[]{:S(2)}) %collective-permute-start.18) | collective-permute-done | bytes 135200 | tf_op jit(solution)/shard_map/ppermute | solution.py:411
  76.7 3.2 %collective-permute-done.19.refs_3_ = bf16[528,128]{1,0:T(8,128)(2,1)S(1)} collective-permute-done((bf16[528,128]{1,0:T(8,128)(2,1)S(1)}, bf16[528,128]{1,0:T(8,128)(2,1)S(1)}, u32[]{:S(2)}, u32[]{:S(2)}) %collective-permute-start.19) | collective-permute-done | bytes 135200 | tf_op jit(solution)/shard_map/ppermute | solution.py:411
  81.5 1.5 collective-permute-start.22
  85.0 3.0 %collective-permute-done.22.refs_0_.refs_2_ = bf16[528,128]{1,0:T(8,128)(2,1)S(1)} collective-permute-done((bf16[528,128]{1,0:T(8,128)(2,1)S(1)}, bf16[528,128]{1,0:T(8,128)(2,1)S(1)}, u32[]{:S(2)}, u32[]{:S(2)}) %collective-permute-start.22) | collective-permute-done | bytes 135200 | tf_op jit(solution)/shard_map/ppermute | solution.py:411
  88.0 2.9 %collective-permute-done.24.refs_1_.refs_4_ = bf16[528,128]{1,0:T(8,128)(2,1)S(1)} collective-permute-done((bf16[528,128]{1,0:T(8,128)(2,1)S(1)}, bf16[528,128]{1,0:T(8,128)(2,1)S(1)}, u32[]{:S(2)}, u32[]{:S(2)}) %collective-permute-start.24) | collective-permute-done | bytes 135200 | tf_op jit(solution)/shard_map/ppermute | solution.py:411
  94.7 2.6 %collective-permute-start.28 = (bf16[528,128]{1,0:T(8,128)(2,1)S(1)}, bf16[528,128]{1,0:T(8,128)(2,1)S(1)}, u32[]{:S(2)}, u32[]{:S(2)}) collective-permute-start(bf16[528,128]{1,0:T(8,128)(2,1)S(1)} %get-tuple-element.167), channel_id=1, source_target_pairs={{0,24},{1,25},{2,26},{3,27},{4,28},{5,29},{6,30},{7,31},{8,16},{9,... | collective-permute-start | bytes 405512 | tf_op jit(solution)/shard_map/ppermute | solution.py:411
  97.3 1.9 %collective-permute-start.30 = (bf16[528,128]{1,0:T(8,128)(2,1)S(1)}, bf16[528,128]{1,0:T(8,128)(2,1)S(1)}, u32[]{:S(2)}, u32[]{:S(2)}) collective-permute-start(bf16[528,128]{1,0:T(8,128)(2,1)S(1)} %get-tuple-element.169), channel_id=1, source_target_pairs={{0,16},{1,9},{2,18},{3,11},{4,20},{5,13},{6,22},{7,15},{8,24},{9,1... | collective-permute-start | bytes 405512 | tf_op jit(solution)/shard_map/ppermute | solution.py:411
  99.4 3.7 %collective-permute-done.28.refs_2_ = bf16[528,128]{1,0:T(8,128)(2,1)S(1)} collective-permute-done((bf16[528,128]{1,0:T(8,128)(2,1)S(1)}, bf16[528,128]{1,0:T(8,128)(2,1)S(1)}, u32[]{:S(2)}, u32[]{:S(2)}) %collective-permute-start.28) | collective-permute-done | bytes 135200 | tf_op jit(solution)/shard_map/ppermute | solution.py:411
  103.2 4.8 %collective-permute-done.29.refs_3_ = bf16[528,128]{1,0:T(8,128)(2,1)S(1)} collective-permute-done((bf16[528,128]{1,0:T(8,128)(2,1)S(1)}, bf16[528,128]{1,0:T(8,128)(2,1)S(1)}, u32[]{:S(2)}, u32[]{:S(2)}) %collective-permute-start.29) | collective-permute-done | bytes 135200 | tf_op jit(solution)/shard_map/ppermute | solution.py:411
  108.2 2.6 %collective-permute-start.31 = (bf16[528,128]{1,0:T(8,128)(2,1)S(1)}, bf16[528,128]{1,0:T(8,128)(2,1)S(1)}, u32[]{:S(2)}, u32[]{:S(2)}) collective-permute-start(bf16[528,128]{1,0:T(8,128)(2,1)S(1)} %get-tuple-element.172.refs_0_.refs_5_), channel_id=1, source_target_pairs={{0,24},{1,25},{2,26},{3,27},{4,28},{5,29},{6,30},{7,31},{8,16},{9,... | collective-permute-start | bytes 405512 | tf_op jit(solution)/shard_map/ppermute | solution.py:411
  110.8 1.8 %collective-permute-start.33 = (bf16[528,128]{1,0:T(8,128)(2,1)S(1)}, bf16[528,128]{1,0:T(8,128)(2,1)S(1)}, u32[]{:S(2)}, u32[]{:S(2)}) collective-permute-start(bf16[528,128]{1,0:T(8,128)(2,1)S(1)} %get-tuple-element.172.refs_0_.refs_5_), channel_id=1, source_target_pairs={{0,16},{1,9},{2,18},{3,11},{4,20},{5,13},{6,22},{7,15},{8,24},{9,1... | collective-permute-start | bytes 405512 | tf_op jit(solution)/shard_map/ppermute | solution.py:411
  113.9 2.7 %collective-permute-done.31.refs_0_.refs_1_.refs_6_ = bf16[528,128]{1,0:T(8,128)(2,1)S(1)} collective-permute-done((bf16[528,128]{1,0:T(8,128)(2,1)S(1)}, bf16[528,128]{1,0:T(8,128)(2,1)S(1)}, u32[]{:S(2)}, u32[]{:S(2)}) %collective-permute-start.31) | collective-permute-done | bytes 135200 | tf_op jit(solution)/shard_map/ppermute | solution.py:411
  116.6 1.5 shard_map.94
  118.2 2.8 %collective-permute-done.32.refs_0_.refs_2_.refs_7_ = bf16[528,128]{1,0:T(8,128)(2,1)S(1)} collective-permute-done((bf16[528,128]{1,0:T(8,128)(2,1)S(1)}, bf16[528,128]{1,0:T(8,128)(2,1)S(1)}, u32[]{:S(2)}, u32[]{:S(2)}) %collective-permute-start.32) | collective-permute-done | bytes 135200 | tf_op jit(solution)/shard_map/ppermute | solution.py:411
  121.0 1.6 shard_map.95
  128.9 3.0 %collective-permute-done.35.refs_2_ = bf16[528,128]{1,0:T(8,128)(2,1)S(1)} collective-permute-done((bf16[528,128]{1,0:T(8,128)(2,1)S(1)}, bf16[528,128]{1,0:T(8,128)(2,1)S(1)}, u32[]{:S(2)}, u32[]{:S(2)}) %collective-permute-start.35) | collective-permute-done | bytes 135200 | tf_op jit(solution)/shard_map/ppermute | solution.py:411
  131.9 3.0 %collective-permute-done.37.refs_4_ = bf16[528,128]{1,0:T(8,128)(2,1)S(1)} collective-permute-done((bf16[528,128]{1,0:T(8,128)(2,1)S(1)}, bf16[528,128]{1,0:T(8,128)(2,1)S(1)}, u32[]{:S(2)}, u32[]{:S(2)}) %collective-permute-start.37) | collective-permute-done | bytes 135200 | tf_op jit(solution)/shard_map/ppermute | solution.py:411
  139.2 3.0 %collective-permute-done.39.refs_0_.refs_2_ = bf16[528,128]{1,0:T(8,128)(2,1)S(1)} collective-permute-done((bf16[528,128]{1,0:T(8,128)(2,1)S(1)}, bf16[528,128]{1,0:T(8,128)(2,1)S(1)}, u32[]{:S(2)}, u32[]{:S(2)}) %collective-permute-start.39) | collective-permute-done | bytes 135200 | tf_op jit(solution)/shard_map/ppermute | solution.py:411
  142.7 2.4 %collective-permute-done.43.refs_1_.refs_6_ = bf16[528,128]{1,0:T(8,128)(2,1)S(1)} collective-permute-done((bf16[528,128]{1,0:T(8,128)(2,1)S(1)}, bf16[528,128]{1,0:T(8,128)(2,1)S(1)}, u32[]{:S(2)}, u32[]{:S(2)}) %collective-permute-start.43) | collective-permute-done | bytes 135200 | tf_op jit(solution)/shard_map/ppermute | solution.py:411
  148.4 2.5 %collective-permute-start.45 = (bf16[528,128]{1,0:T(8,128)(2,1)S(1)}, bf16[528,128]{1,0:T(8,128)(2,1)S(1)}, u32[]{:S(2)}, u32[]{:S(2)}) collective-permute-start(bf16[528,128]{1,0:T(8,128)(2,1)S(1)} %get-tuple-element.207), channel_id=1, source_target_pairs={{0,24},{1,25},{2,26},{3,27},{4,28},{5,29},{6,30},{7,31},{8,16},{9,... | collective-permute-start | bytes 405512 | tf_op jit(solution)/shard_map/ppermute | solution.py:411
  150.9 2.0 %collective-permute-start.47 = (bf16[528,128]{1,0:T(8,128)(2,1)S(1)}, bf16[528,128]{1,0:T(8,128)(2,1)S(1)}, u32[]{:S(2)}, u32[]{:S(2)}) collective-permute-start(bf16[528,128]{1,0:T(8,128)(2,1)S(1)} %get-tuple-element.209), channel_id=1, source_target_pairs={{0,16},{1,9},{2,18},{3,11},{4,20},{5,13},{6,22},{7,15},{8,24},{9,1... | collective-permute-start | bytes 405512 | tf_op jit(solution)/shard_map/ppermute | solution.py:411
  153.1 3.8 %collective-permute-done.45.refs_2_ = bf16[528,128]{1,0:T(8,128)(2,1)S(1)} collective-permute-done((bf16[528,128]{1,0:T(8,128)(2,1)S(1)}, bf16[528,128]{1,0:T(8,128)(2,1)S(1)}, u32[]{:S(2)}, u32[]{:S(2)}) %collective-permute-start.45) | collective-permute-done | bytes 135200 | tf_op jit(solution)/shard_map/ppermute | solution.py:411
  156.9 5.0 %collective-permute-done.46.refs_3_ = bf16[528,128]{1,0:T(8,128)(2,1)S(1)} collective-permute-done((bf16[528,128]{1,0:T(8,128)(2,1)S(1)}, bf16[528,128]{1,0:T(8,128)(2,1)S(1)}, u32[]{:S(2)}, u32[]{:S(2)}) %collective-permute-start.46) | collective-permute-done | bytes 135200 | tf_op jit(solution)/shard_map/ppermute | solution.py:411
  163.4 2.3 %collective-permute-start.48 = (bf16[528,128]{1,0:T(8,128)(2,1)S(1)}, bf16[528,128]{1,0:T(8,128)(2,1)S(1)}, u32[]{:S(2)}, u32[]{:S(2)}) collective-permute-start(bf16[528,128]{1,0:T(8,128)(2,1)S(1)} %get-tuple-element.215.refs_0_), channel_id=1, source_target_pairs={{0,24},{1,25},{2,26},{3,27},{4,28},{5,29},{6,30},{7,31},{8,16},{9,... | collective-permute-start | bytes 405512 | tf_op jit(solution)/shard_map/ppermute | solution.py:411
  165.7 2.1 %collective-permute-start.50 = (bf16[528,128]{1,0:T(8,128)(2,1)S(1)}, bf16[528,128]{1,0:T(8,128)(2,1)S(1)}, u32[]{:S(2)}, u32[]{:S(2)}) collective-permute-start(bf16[528,128]{1,0:T(8,128)(2,1)S(1)} %get-tuple-element.215.refs_0_), channel_id=1, source_target_pairs={{0,16},{1,9},{2,18},{3,11},{4,20},{5,13},{6,22},{7,15},{8,24},{9,1... | collective-permute-start | bytes 405512 | tf_op jit(solution)/shard_map/ppermute | solution.py:411
  169.2 2.5 %collective-permute-done.48.refs_1_ = bf16[528,128]{1,0:T(8,128)(2,1)S(1)} collective-permute-done((bf16[528,128]{1,0:T(8,128)(2,1)S(1)}, bf16[528,128]{1,0:T(8,128)(2,1)S(1)}, u32[]{:S(2)}, u32[]{:S(2)}) %collective-permute-start.48) | collective-permute-done | bytes 135200 | tf_op jit(solution)/shard_map/ppermute | solution.py:411
  171.7 3.5 %collective-permute-done.49.refs_2_ = bf16[528,128]{1,0:T(8,128)(2,1)S(1)} collective-permute-done((bf16[528,128]{1,0:T(8,128)(2,1)S(1)}, bf16[528,128]{1,0:T(8,128)(2,1)S(1)}, u32[]{:S(2)}, u32[]{:S(2)}) %collective-permute-start.49) | collective-permute-done | bytes 135200 | tf_op jit(solution)/shard_map/ppermute | solution.py:411
  175.2 1.7 collective-permute-done.50.refs_3_
  (103 shorter events, 45.0 us)
Async XLA Ops:
  9.0 6.5 %collective-permute-start.1 = (bf16[528,128]{1,0:T(8,128)(2,1)S(1)}, bf16[528,128]{1,0:T(8,128)(2,1)S(1)}, u32[]{:S(2)}, u32[]{:S(2)}) collective-permute-start(bf16[528,128]{1,0:T(8,128)(2,1)S(1)} %get-tuple-element.114), channel_id=1, source_target_pairs={{0,2},{1,5},{2,0},{3,7},{4,6},{5,1},{6,4},{7,3},{8,10},{9,13},{10,... | collective-permute-start | bytes 405512 | tf_op jit(solution)/shard_map/ppermute | solution.py:411
  11.9 7.0 %collective-permute-start.2 = (bf16[528,128]{1,0:T(8,128)(2,1)S(1)}, bf16[528,128]{1,0:T(8,128)(2,1)S(1)}, u32[]{:S(2)}, u32[]{:S(2)}) collective-permute-start(bf16[528,128]{1,0:T(8,128)(2,1)S(1)} %get-tuple-element.115), channel_id=1, source_target_pairs={{0,4},{1,3},{2,6},{3,1},{4,0},{5,7},{6,2},{7,5},{8,12},{9,11},{10,... | collective-permute-start | bytes 405512 | tf_op jit(solution)/shard_map/ppermute | solution.py:411
  13.4 6.5 %collective-permute-start.3 = (bf16[528,128]{1,0:T(8,128)(2,1)S(1)}, bf16[528,128]{1,0:T(8,128)(2,1)S(1)}, u32[]{:S(2)}, u32[]{:S(2)}) collective-permute-start(bf16[528,128]{1,0:T(8,128)(2,1)S(1)} %get-tuple-element.116), channel_id=1, source_target_pairs={{0,6},{1,7},{2,4},{3,5},{4,2},{5,3},{6,0},{7,1},{8,14},{9,15},{10,... | collective-permute-start | bytes 405512 | tf_op jit(solution)/shard_map/ppermute | solution.py:411
  20.9 6.5 %collective-permute-start.5 = (bf16[528,128]{1,0:T(8,128)(2,1)S(1)}, bf16[528,128]{1,0:T(8,128)(2,1)S(1)}, u32[]{:S(2)}, u32[]{:S(2)}) collective-permute-start(bf16[528,128]{1,0:T(8,128)(2,1)S(1)} %get-tuple-element.118.refs_0_), channel_id=1, source_target_pairs={{0,2},{1,5},{2,0},{3,7},{4,6},{5,1},{6,4},{7,3},{8,10},{9,13},{10,... | collective-permute-start | bytes 405512 | tf_op jit(solution)/shard_map/ppermute | solution.py:411
  22.6 7.9 %collective-permute-start.7 = (bf16[528,128]{1,0:T(8,128)(2,1)S(1)}, bf16[528,128]{1,0:T(8,128)(2,1)S(1)}, u32[]{:S(2)}, u32[]{:S(2)}) collective-permute-start(bf16[528,128]{1,0:T(8,128)(2,1)S(1)} %get-tuple-element.118.refs_0_), channel_id=1, source_target_pairs={{0,4},{1,3},{2,6},{3,1},{4,0},{5,7},{6,2},{7,5},{8,12},{9,11},{10,... | collective-permute-start | bytes 405512 | tf_op jit(solution)/shard_map/ppermute | solution.py:411
  23.3 7.2 %collective-permute-start.9 = (bf16[528,128]{1,0:T(8,128)(2,1)S(1)}, bf16[528,128]{1,0:T(8,128)(2,1)S(1)}, u32[]{:S(2)}, u32[]{:S(2)}) collective-permute-start(bf16[528,128]{1,0:T(8,128)(2,1)S(1)} %get-tuple-element.118.refs_0_), channel_id=1, source_target_pairs={{0,6},{1,7},{2,4},{3,5},{4,2},{5,3},{6,0},{7,1},{8,14},{9,15},{10,... | collective-permute-start | bytes 405512 | tf_op jit(solution)/shard_map/ppermute | solution.py:411
  24.5 11.3 %collective-permute-start.4 = (bf16[528,128]{1,0:T(8,128)(2,1)S(1)}, bf16[528,128]{1,0:T(8,128)(2,1)S(1)}, u32[]{:S(2)}, u32[]{:S(2)}) collective-permute-start(bf16[528,128]{1,0:T(8,128)(2,1)S(1)} %get-tuple-element.118.refs_0_), channel_id=1, source_target_pairs={{0,1},{1,0},{2,3},{3,2},{4,5},{5,4},{6,7},{7,6},{8,9},{9,8},{10,11... | collective-permute-start | bytes 405512 | tf_op jit(solution)/shard_map/ppermute | solution.py:411
  27.4 9.5 %collective-permute-start.6 = (bf16[528,128]{1,0:T(8,128)(2,1)S(1)}, bf16[528,128]{1,0:T(8,128)(2,1)S(1)}, u32[]{:S(2)}, u32[]{:S(2)}) collective-permute-start(bf16[528,128]{1,0:T(8,128)(2,1)S(1)} %collective-permute-done.5.refs_0_.refs_2_), channel_id=1, source_target_pairs={{0,1},{1,0},{2,3},{3,2},{4,5},{5,4},{6,7},{7,6},{8,9},{9,8},{10,11... | collective-permute-start | bytes 405512 | tf_op jit(solution)/shard_map/ppermute | solution.py:411
  30.5 7.3 %collective-permute-start.8 = (bf16[528,128]{1,0:T(8,128)(2,1)S(1)}, bf16[528,128]{1,0:T(8,128)(2,1)S(1)}, u32[]{:S(2)}, u32[]{:S(2)}) collective-permute-start(bf16[528,128]{1,0:T(8,128)(2,1)S(1)} %collective-permute-done.7.refs_1_.refs_4_), channel_id=1, source_target_pairs={{0,1},{1,0},{2,3},{3,2},{4,5},{5,4},{6,7},{7,6},{8,9},{9,8},{10,11... | collective-permute-start | bytes 405512 | tf_op jit(solution)/shard_map/ppermute | solution.py:411
  30.5 8.1 %collective-permute-start.10 = (bf16[528,128]{1,0:T(8,128)(2,1)S(1)}, bf16[528,128]{1,0:T(8,128)(2,1)S(1)}, u32[]{:S(2)}, u32[]{:S(2)}) collective-permute-start(bf16[528,128]{1,0:T(8,128)(2,1)S(1)} %collective-permute-done.9.refs_1_.refs_6_), channel_id=1, source_target_pairs={{0,1},{1,0},{2,3},{3,2},{4,5},{5,4},{6,7},{7,6},{8,9},{9,8},{10,11... | collective-permute-start | bytes 405512 | tf_op jit(solution)/shard_map/ppermute | solution.py:411
  39.1 8.4 %collective-permute-start.11 = (bf16[528,128]{1,0:T(8,128)(2,1)S(1)}, bf16[528,128]{1,0:T(8,128)(2,1)S(1)}, u32[]{:S(2)}, u32[]{:S(2)}) collective-permute-start(bf16[528,128]{1,0:T(8,128)(2,1)S(1)} %get-tuple-element.130), channel_id=1, source_target_pairs={{0,24},{1,25},{2,26},{3,27},{4,28},{5,29},{6,30},{7,31},{8,16},{9,... | collective-permute-start | bytes 405512 | tf_op jit(solution)/shard_map/ppermute | solution.py:411
  42.7 7.2 %collective-permute-start.12 = (bf16[528,128]{1,0:T(8,128)(2,1)S(1)}, bf16[528,128]{1,0:T(8,128)(2,1)S(1)}, u32[]{:S(2)}, u32[]{:S(2)}) collective-permute-start(bf16[528,128]{1,0:T(8,128)(2,1)S(1)} %get-tuple-element.131), channel_id=1, source_target_pairs={{0,8},{1,17},{2,10},{3,19},{4,12},{5,21},{6,14},{7,23},{8,0},{9,25... | collective-permute-start | bytes 405512 | tf_op jit(solution)/shard_map/ppermute | solution.py:411
  42.7 11.6 %collective-permute-start.13 = (bf16[528,128]{1,0:T(8,128)(2,1)S(1)}, bf16[528,128]{1,0:T(8,128)(2,1)S(1)}, u32[]{:S(2)}, u32[]{:S(2)}) collective-permute-start(bf16[528,128]{1,0:T(8,128)(2,1)S(1)} %get-tuple-element.132), channel_id=1, source_target_pairs={{0,16},{1,9},{2,18},{3,11},{4,20},{5,13},{6,22},{7,15},{8,24},{9,1... | collective-permute-start | bytes 405512 | tf_op jit(solution)/shard_map/ppermute | solution.py:411
  54.5 8.3 %collective-permute-start.14 = (bf16[528,128]{1,0:T(8,128)(2,1)S(1)}, bf16[528,128]{1,0:T(8,128)(2,1)S(1)}, u32[]{:S(2)}, u32[]{:S(2)}) collective-permute-start(bf16[528,128]{1,0:T(8,128)(2,1)S(1)} %get-tuple-element.133.refs_0_.refs_1_), channel_id=1, source_target_pairs={{0,24},{1,25},{2,26},{3,27},{4,28},{5,29},{6,30},{7,31},{8,16},{9,... | collective-permute-start | bytes 405512 | tf_op jit(solution)/shard_map/ppermute | solution.py:411
  57.1 9.4 %collective-permute-start.15 = (bf16[528,128]{1,0:T(8,128)(2,1)S(1)}, bf16[528,128]{1,0:T(8,128)(2,1)S(1)}, u32[]{:S(2)}, u32[]{:S(2)}) collective-permute-start(bf16[528,128]{1,0:T(8,128)(2,1)S(1)} %get-tuple-element.133.refs_0_.refs_1_), channel_id=1, source_target_pairs={{0,8},{1,17},{2,10},{3,19},{4,12},{5,21},{6,14},{7,23},{8,0},{9,25... | collective-permute-start | bytes 405512 | tf_op jit(solution)/shard_map/ppermute | solution.py:411
  57.1 11.0 %collective-permute-start.16 = (bf16[528,128]{1,0:T(8,128)(2,1)S(1)}, bf16[528,128]{1,0:T(8,128)(2,1)S(1)}, u32[]{:S(2)}, u32[]{:S(2)}) collective-permute-start(bf16[528,128]{1,0:T(8,128)(2,1)S(1)} %get-tuple-element.133.refs_0_.refs_1_), channel_id=1, source_target_pairs={{0,16},{1,9},{2,18},{3,11},{4,20},{5,13},{6,22},{7,15},{8,24},{9,1... | collective-permute-start | bytes 405512 | tf_op jit(solution)/shard_map/ppermute | solution.py:411
  70.9 5.8 %collective-permute-start.18 = (bf16[528,128]{1,0:T(8,128)(2,1)S(1)}, bf16[528,128]{1,0:T(8,128)(2,1)S(1)}, u32[]{:S(2)}, u32[]{:S(2)}) collective-permute-start(bf16[528,128]{1,0:T(8,128)(2,1)S(1)} %get-tuple-element.147), channel_id=1, source_target_pairs={{0,2},{1,5},{2,0},{3,7},{4,6},{5,1},{6,4},{7,3},{8,10},{9,13},{10,... | collective-permute-start | bytes 405512 | tf_op jit(solution)/shard_map/ppermute | solution.py:411
  73.0 6.9 %collective-permute-start.19 = (bf16[528,128]{1,0:T(8,128)(2,1)S(1)}, bf16[528,128]{1,0:T(8,128)(2,1)S(1)}, u32[]{:S(2)}, u32[]{:S(2)}) collective-permute-start(bf16[528,128]{1,0:T(8,128)(2,1)S(1)} %get-tuple-element.148), channel_id=1, source_target_pairs={{0,4},{1,3},{2,6},{3,1},{4,0},{5,7},{6,2},{7,5},{8,12},{9,11},{10,... | collective-permute-start | bytes 405512 | tf_op jit(solution)/shard_map/ppermute | solution.py:411
  74.4 6.8 %collective-permute-start.20 = (bf16[528,128]{1,0:T(8,128)(2,1)S(1)}, bf16[528,128]{1,0:T(8,128)(2,1)S(1)}, u32[]{:S(2)}, u32[]{:S(2)}) collective-permute-start(bf16[528,128]{1,0:T(8,128)(2,1)S(1)} %get-tuple-element.149), channel_id=1, source_target_pairs={{0,6},{1,7},{2,4},{3,5},{4,2},{5,3},{6,0},{7,1},{8,14},{9,15},{10,... | collective-permute-start | bytes 405512 | tf_op jit(solution)/shard_map/ppermute | solution.py:411
  81.5 6.5 %collective-permute-start.22 = (bf16[528,128]{1,0:T(8,128)(2,1)S(1)}, bf16[528,128]{1,0:T(8,128)(2,1)S(1)}, u32[]{:S(2)}, u32[]{:S(2)}) collective-permute-start(bf16[528,128]{1,0:T(8,128)(2,1)S(1)} %get-tuple-element.154.refs_0_), channel_id=1, source_target_pairs={{0,2},{1,5},{2,0},{3,7},{4,6},{5,1},{6,4},{7,3},{8,10},{9,13},{10,... | collective-permute-start | bytes 405512 | tf_op jit(solution)/shard_map/ppermute | solution.py:411
  83.0 7.9 %collective-permute-start.24 = (bf16[528,128]{1,0:T(8,128)(2,1)S(1)}, bf16[528,128]{1,0:T(8,128)(2,1)S(1)}, u32[]{:S(2)}, u32[]{:S(2)}) collective-permute-start(bf16[528,128]{1,0:T(8,128)(2,1)S(1)} %get-tuple-element.154.refs_0_), channel_id=1, source_target_pairs={{0,4},{1,3},{2,6},{3,1},{4,0},{5,7},{6,2},{7,5},{8,12},{9,11},{10,... | collective-permute-start | bytes 405512 | tf_op jit(solution)/shard_map/ppermute | solution.py:411
  83.8 7.1 %collective-permute-start.26 = (bf16[528,128]{1,0:T(8,128)(2,1)S(1)}, bf16[528,128]{1,0:T(8,128)(2,1)S(1)}, u32[]{:S(2)}, u32[]{:S(2)}) collective-permute-start(bf16[528,128]{1,0:T(8,128)(2,1)S(1)} %get-tuple-element.154.refs_0_), channel_id=1, source_target_pairs={{0,6},{1,7},{2,4},{3,5},{4,2},{5,3},{6,0},{7,1},{8,14},{9,15},{10,... | collective-permute-start | bytes 405512 | tf_op jit(solution)/shard_map/ppermute | solution.py:411
  85.0 6.4 %collective-permute-start.21 = (bf16[528,128]{1,0:T(8,128)(2,1)S(1)}, bf16[528,128]{1,0:T(8,128)(2,1)S(1)}, u32[]{:S(2)}, u32[]{:S(2)}) collective-permute-start(bf16[528,128]{1,0:T(8,128)(2,1)S(1)} %get-tuple-element.154.refs_0_), channel_id=1, source_target_pairs={{0,1},{1,0},{2,3},{3,2},{4,5},{5,4},{6,7},{7,6},{8,9},{9,8},{10,11... | collective-permute-start | bytes 405512 | tf_op jit(solution)/shard_map/ppermute | solution.py:411
  88.0 4.7 %collective-permute-start.23 = (bf16[528,128]{1,0:T(8,128)(2,1)S(1)}, bf16[528,128]{1,0:T(8,128)(2,1)S(1)}, u32[]{:S(2)}, u32[]{:S(2)}) collective-permute-start(bf16[528,128]{1,0:T(8,128)(2,1)S(1)} %collective-permute-done.22.refs_0_.refs_2_), channel_id=1, source_target_pairs={{0,1},{1,0},{2,3},{3,2},{4,5},{5,4},{6,7},{7,6},{8,9},{9,8},{10,11... | collective-permute-start | bytes 405512 | tf_op jit(solution)/shard_map/ppermute | solution.py:411
  90.9 2.6 %collective-permute-start.25 = (bf16[528,128]{1,0:T(8,128)(2,1)S(1)}, bf16[528,128]{1,0:T(8,128)(2,1)S(1)}, u32[]{:S(2)}, u32[]{:S(2)}) collective-permute-start(bf16[528,128]{1,0:T(8,128)(2,1)S(1)} %collective-permute-done.24.refs_1_.refs_4_), channel_id=1, source_target_pairs={{0,1},{1,0},{2,3},{3,2},{4,5},{5,4},{6,7},{7,6},{8,9},{9,8},{10,11... | collective-permute-start | bytes 405512 | tf_op jit(solution)/shard_map/ppermute | solution.py:411
  90.9 3.4 %collective-permute-start.27 = (bf16[528,128]{1,0:T(8,128)(2,1)S(1)}, bf16[528,128]{1,0:T(8,128)(2,1)S(1)}, u32[]{:S(2)}, u32[]{:S(2)}) collective-permute-start(bf16[528,128]{1,0:T(8,128)(2,1)S(1)} %collective-permute-done.26.refs_1_.refs_6_), channel_id=1, source_target_pairs={{0,1},{1,0},{2,3},{3,2},{4,5},{5,4},{6,7},{7,6},{8,9},{9,8},{10,11... | collective-permute-start | bytes 405512 | tf_op jit(solution)/shard_map/ppermute | solution.py:411
  94.7 8.4 %collective-permute-start.28 = (bf16[528,128]{1,0:T(8,128)(2,1)S(1)}, bf16[528,128]{1,0:T(8,128)(2,1)S(1)}, u32[]{:S(2)}, u32[]{:S(2)}) collective-permute-start(bf16[528,128]{1,0:T(8,128)(2,1)S(1)} %get-tuple-element.167), channel_id=1, source_target_pairs={{0,24},{1,25},{2,26},{3,27},{4,28},{5,29},{6,30},{7,31},{8,16},{9,... | collective-permute-start | bytes 405512 | tf_op jit(solution)/shard_map/ppermute | solution.py:411
  97.3 10.7 %collective-permute-start.29 = (bf16[528,128]{1,0:T(8,128)(2,1)S(1)}, bf16[528,128]{1,0:T(8,128)(2,1)S(1)}, u32[]{:S(2)}, u32[]{:S(2)}) collective-permute-start(bf16[528,128]{1,0:T(8,128)(2,1)S(1)} %get-tuple-element.168), channel_id=1, source_target_pairs={{0,8},{1,17},{2,10},{3,19},{4,12},{5,21},{6,14},{7,23},{8,0},{9,25... | collective-permute-start | bytes 405512 | tf_op jit(solution)/shard_map/ppermute | solution.py:411
  97.3 10.7 %collective-permute-start.30 = (bf16[528,128]{1,0:T(8,128)(2,1)S(1)}, bf16[528,128]{1,0:T(8,128)(2,1)S(1)}, u32[]{:S(2)}, u32[]{:S(2)}) collective-permute-start(bf16[528,128]{1,0:T(8,128)(2,1)S(1)} %get-tuple-element.169), channel_id=1, source_target_pairs={{0,16},{1,9},{2,18},{3,11},{4,20},{5,13},{6,22},{7,15},{8,24},{9,1... | collective-permute-start | bytes 405512 | tf_op jit(solution)/shard_map/ppermute | solution.py:411
  108.2 8.4 %collective-permute-start.31 = (bf16[528,128]{1,0:T(8,128)(2,1)S(1)}, bf16[528,128]{1,0:T(8,128)(2,1)S(1)}, u32[]{:S(2)}, u32[]{:S(2)}) collective-permute-start(bf16[528,128]{1,0:T(8,128)(2,1)S(1)} %get-tuple-element.172.refs_0_.refs_5_), channel_id=1, source_target_pairs={{0,24},{1,25},{2,26},{3,27},{4,28},{5,29},{6,30},{7,31},{8,16},{9,... | collective-permute-start | bytes 405512 | tf_op jit(solution)/shard_map/ppermute | solution.py:411
  110.8 10.2 %collective-permute-start.32 = (bf16[528,128]{1,0:T(8,128)(2,1)S(1)}, bf16[528,128]{1,0:T(8,128)(2,1)S(1)}, u32[]{:S(2)}, u32[]{:S(2)}) collective-permute-start(bf16[528,128]{1,0:T(8,128)(2,1)S(1)} %get-tuple-element.172.refs_0_.refs_5_), channel_id=1, source_target_pairs={{0,8},{1,17},{2,10},{3,19},{4,12},{5,21},{6,14},{7,23},{8,0},{9,25... | collective-permute-start | bytes 405512 | tf_op jit(solution)/shard_map/ppermute | solution.py:411
  110.8 11.7 %collective-permute-start.33 = (bf16[528,128]{1,0:T(8,128)(2,1)S(1)}, bf16[528,128]{1,0:T(8,128)(2,1)S(1)}, u32[]{:S(2)}, u32[]{:S(2)}) collective-permute-start(bf16[528,128]{1,0:T(8,128)(2,1)S(1)} %get-tuple-element.172.refs_0_.refs_5_), channel_id=1, source_target_pairs={{0,16},{1,9},{2,18},{3,11},{4,20},{5,13},{6,22},{7,15},{8,24},{9,1... | collective-permute-start | bytes 405512 | tf_op jit(solution)/shard_map/ppermute | solution.py:411
  125.4 6.5 %collective-permute-start.35 = (bf16[528,128]{1,0:T(8,128)(2,1)S(1)}, bf16[528,128]{1,0:T(8,128)(2,1)S(1)}, u32[]{:S(2)}, u32[]{:S(2)}) collective-permute-start(bf16[528,128]{1,0:T(8,128)(2,1)S(1)} %get-tuple-element.188), channel_id=1, source_target_pairs={{0,2},{1,5},{2,0},{3,7},{4,6},{5,1},{6,4},{7,3},{8,10},{9,13},{10,... | collective-permute-start | bytes 405512 | tf_op jit(solution)/shard_map/ppermute | solution.py:411
  126.5 5.4 %collective-permute-start.36 = (bf16[528,128]{1,0:T(8,128)(2,1)S(1)}, bf16[528,128]{1,0:T(8,128)(2,1)S(1)}, u32[]{:S(2)}, u32[]{:S(2)}) collective-permute-start(bf16[528,128]{1,0:T(8,128)(2,1)S(1)} %get-tuple-element.189), channel_id=1, source_target_pairs={{0,4},{1,3},{2,6},{3,1},{4,0},{5,7},{6,2},{7,5},{8,12},{9,11},{10,... | collective-permute-start | bytes 405512 | tf_op jit(solution)/shard_map/ppermute | solution.py:411
  127.8 7.1 %collective-permute-start.37 = (bf16[528,128]{1,0:T(8,128)(2,1)S(1)}, bf16[528,128]{1,0:T(8,128)(2,1)S(1)}, u32[]{:S(2)}, u32[]{:S(2)}) collective-permute-start(bf16[528,128]{1,0:T(8,128)(2,1)S(1)} %get-tuple-element.190), channel_id=1, source_target_pairs={{0,6},{1,7},{2,4},{3,5},{4,2},{5,3},{6,0},{7,1},{8,14},{9,15},{10,... | collective-permute-start | bytes 405512 | tf_op jit(solution)/shard_map/ppermute | solution.py:411
  135.7 6.5 %collective-permute-start.39 = (bf16[528,128]{1,0:T(8,128)(2,1)S(1)}, bf16[528,128]{1,0:T(8,128)(2,1)S(1)}, u32[]{:S(2)}, u32[]{:S(2)}) collective-permute-start(bf16[528,128]{1,0:T(8,128)(2,1)S(1)} %get-tuple-element.194.refs_0_), channel_id=1, source_target_pairs={{0,2},{1,5},{2,0},{3,7},{4,6},{5,1},{6,4},{7,3},{8,10},{9,13},{10,... | collective-permute-start | bytes 405512 | tf_op jit(solution)/shard_map/ppermute | solution.py:411
  137.0 5.2 %collective-permute-start.41 = (bf16[528,128]{1,0:T(8,128)(2,1)S(1)}, bf16[528,128]{1,0:T(8,128)(2,1)S(1)}, u32[]{:S(2)}, u32[]{:S(2)}) collective-permute-start(bf16[528,128]{1,0:T(8,128)(2,1)S(1)} %get-tuple-element.194.refs_0_), channel_id=1, source_target_pairs={{0,4},{1,3},{2,6},{3,1},{4,0},{5,7},{6,2},{7,5},{8,12},{9,11},{10,... | collective-permute-start | bytes 405512 | tf_op jit(solution)/shard_map/ppermute | solution.py:411
  137.9 7.2 %collective-permute-start.43 = (bf16[528,128]{1,0:T(8,128)(2,1)S(1)}, bf16[528,128]{1,0:T(8,128)(2,1)S(1)}, u32[]{:S(2)}, u32[]{:S(2)}) collective-permute-start(bf16[528,128]{1,0:T(8,128)(2,1)S(1)} %get-tuple-element.194.refs_0_), channel_id=1, source_target_pairs={{0,6},{1,7},{2,4},{3,5},{4,2},{5,3},{6,0},{7,1},{8,14},{9,15},{10,... | collective-permute-start | bytes 405512 | tf_op jit(solution)/shard_map/ppermute | solution.py:411
  139.2 5.9 %collective-permute-start.38 = (bf16[528,128]{1,0:T(8,128)(2,1)S(1)}, bf16[528,128]{1,0:T(8,128)(2,1)S(1)}, u32[]{:S(2)}, u32[]{:S(2)}) collective-permute-start(bf16[528,128]{1,0:T(8,128)(2,1)S(1)} %get-tuple-element.194.refs_0_), channel_id=1, source_target_pairs={{0,1},{1,0},{2,3},{3,2},{4,5},{5,4},{6,7},{7,6},{8,9},{9,8},{10,11... | collective-permute-start | bytes 405512 | tf_op jit(solution)/shard_map/ppermute | solution.py:411
  142.2 4.2 %collective-permute-start.40 = (bf16[528,128]{1,0:T(8,128)(2,1)S(1)}, bf16[528,128]{1,0:T(8,128)(2,1)S(1)}, u32[]{:S(2)}, u32[]{:S(2)}) collective-permute-start(bf16[528,128]{1,0:T(8,128)(2,1)S(1)} %collective-permute-done.39.refs_0_.refs_2_), channel_id=1, source_target_pairs={{0,1},{1,0},{2,3},{3,2},{4,5},{5,4},{6,7},{7,6},{8,9},{9,8},{10,11... | collective-permute-start | bytes 405512 | tf_op jit(solution)/shard_map/ppermute | solution.py:411
  142.2 5.0 %collective-permute-start.42 = (bf16[528,128]{1,0:T(8,128)(2,1)S(1)}, bf16[528,128]{1,0:T(8,128)(2,1)S(1)}, u32[]{:S(2)}, u32[]{:S(2)}) collective-permute-start(bf16[528,128]{1,0:T(8,128)(2,1)S(1)} %collective-permute-done.41.refs_1_.refs_4_), channel_id=1, source_target_pairs={{0,1},{1,0},{2,3},{3,2},{4,5},{5,4},{6,7},{7,6},{8,9},{9,8},{10,11... | collective-permute-start | bytes 405512 | tf_op jit(solution)/shard_map/ppermute | solution.py:411
  145.1 2.9 %collective-permute-start.44 = (bf16[528,128]{1,0:T(8,128)(2,1)S(1)}, bf16[528,128]{1,0:T(8,128)(2,1)S(1)}, u32[]{:S(2)}, u32[]{:S(2)}) collective-permute-start(bf16[528,128]{1,0:T(8,128)(2,1)S(1)} %collective-permute-done.43.refs_1_.refs_6_), channel_id=1, source_target_pairs={{0,1},{1,0},{2,3},{3,2},{4,5},{5,4},{6,7},{7,6},{8,9},{9,8},{10,11... | collective-permute-start | bytes 405512 | tf_op jit(solution)/shard_map/ppermute | solution.py:411
  148.4 8.5 %collective-permute-start.45 = (bf16[528,128]{1,0:T(8,128)(2,1)S(1)}, bf16[528,128]{1,0:T(8,128)(2,1)S(1)}, u32[]{:S(2)}, u32[]{:S(2)}) collective-permute-start(bf16[528,128]{1,0:T(8,128)(2,1)S(1)} %get-tuple-element.207), channel_id=1, source_target_pairs={{0,24},{1,25},{2,26},{3,27},{4,28},{5,29},{6,30},{7,31},{8,16},{9,... | collective-permute-start | bytes 405512 | tf_op jit(solution)/shard_map/ppermute | solution.py:411
  150.9 11.0 %collective-permute-start.46 = (bf16[528,128]{1,0:T(8,128)(2,1)S(1)}, bf16[528,128]{1,0:T(8,128)(2,1)S(1)}, u32[]{:S(2)}, u32[]{:S(2)}) collective-permute-start(bf16[528,128]{1,0:T(8,128)(2,1)S(1)} %get-tuple-element.208), channel_id=1, source_target_pairs={{0,8},{1,17},{2,10},{3,19},{4,12},{5,21},{6,14},{7,23},{8,0},{9,25... | collective-permute-start | bytes 405512 | tf_op jit(solution)/shard_map/ppermute | solution.py:411
  150.9 11.6 %collective-permute-start.47 = (bf16[528,128]{1,0:T(8,128)(2,1)S(1)}, bf16[528,128]{1,0:T(8,128)(2,1)S(1)}, u32[]{:S(2)}, u32[]{:S(2)}) collective-permute-start(bf16[528,128]{1,0:T(8,128)(2,1)S(1)} %get-tuple-element.209), channel_id=1, source_target_pairs={{0,16},{1,9},{2,18},{3,11},{4,20},{5,13},{6,22},{7,15},{8,24},{9,1... | collective-permute-start | bytes 405512 | tf_op jit(solution)/shard_map/ppermute | solution.py:411
  163.4 8.3 %collective-permute-start.48 = (bf16[528,128]{1,0:T(8,128)(2,1)S(1)}, bf16[528,128]{1,0:T(8,128)(2,1)S(1)}, u32[]{:S(2)}, u32[]{:S(2)}) collective-permute-start(bf16[528,128]{1,0:T(8,128)(2,1)S(1)} %get-tuple-element.215.refs_0_), channel_id=1, source_target_pairs={{0,24},{1,25},{2,26},{3,27},{4,28},{5,29},{6,30},{7,31},{8,16},{9,... | collective-permute-start | bytes 405512 | tf_op jit(solution)/shard_map/ppermute | solution.py:411
  165.7 9.5 %collective-permute-start.49 = (bf16[528,128]{1,0:T(8,128)(2,1)S(1)}, bf16[528,128]{1,0:T(8,128)(2,1)S(1)}, u32[]{:S(2)}, u32[]{:S(2)}) collective-permute-start(bf16[528,128]{1,0:T(8,128)(2,1)S(1)} %get-tuple-element.215.refs_0_), channel_id=1, source_target_pairs={{0,8},{1,17},{2,10},{3,19},{4,12},{5,21},{6,14},{7,23},{8,0},{9,25... | collective-permute-start | bytes 405512 | tf_op jit(solution)/shard_map/ppermute | solution.py:411
  165.7 11.2 %collective-permute-start.50 = (bf16[528,128]{1,0:T(8,128)(2,1)S(1)}, bf16[528,128]{1,0:T(8,128)(2,1)S(1)}, u32[]{:S(2)}, u32[]{:S(2)}) collective-permute-start(bf16[528,128]{1,0:T(8,128)(2,1)S(1)} %get-tuple-element.215.refs_0_), channel_id=1, source_target_pairs={{0,16},{1,9},{2,18},{3,11},{4,20},{5,13},{6,22},{7,15},{8,24},{9,1... | collective-permute-start | bytes 405512 | tf_op jit(solution)/shard_map/ppermute | solution.py:411
  (5 other events, 26.6 us)

commit v4 on v3

--- a/solution.py
+++ b/solution.py
@@ -10,7 +10,7 @@
 
 ITERS = 3
 RIDGE = 0.2
-TAIL = 16
+TAIL = 8
 
 GROUP = 32
 CHUNKS = 8
@@ -38,7 +38,7 @@
 
 
 def row_groups(n):
-    return [[k] for k in range(n)]
+    return [*([k] for k in range(n - 2)), [n - 2, n - 1]]
 
 
 def chip_order(n):
@@ -48,7 +48,7 @@
 def column_groups(n):
     order = chip_order(n)
     between = [[2 * before + 1, 2 * k] for before, k in zip(order, order[1:])]
-    return [[0, 1], [2 * order[0]], *between, [2 * order[-1] + 1]]
+    return [[0], [1, 2 * order[0]], *between, [2 * order[-1] + 1]]
 
 
 f32 = jnp.float32
@@ -258,7 +258,7 @@
         send[rows:, :] = tile
 
 
-def scale_kernel(cfg, first, *refs):
+def scale_kernel(cfg, first, last, *refs):
     chips = cfg["cols"] // 2
     own, own_tail = refs[:2]
     received = refs[2 : 1 + chips]
@@ -266,7 +266,7 @@
     rows = own.shape[0]
     projected = tree([own[...]] + [r[:rows, :].astype(f32) for r in received])
     if first:
-        removed, margins, direction, scaled, kept, spread = rest
+        removed, margins, direction, scaled, spread = rest[:5]
         width = cfg["width"]
         for j in range(cfg["nb"]):
             logistic = 1.0 / (1.0 + jnp.exp(-margins[pl.ds(here()[0] * cfg["nb"] + j, 1), :]))
@@ -276,7 +276,7 @@
         d = direction[...]
         norm = column_sum(d * d)
     else:
-        spread, residual, old, before, norm_now, scaled, kept, direction, norm_out, beta_out = rest
+        spread, residual, old, before, norm_now, scaled, direction, norm_out, beta_out = rest[:9]
         tile = tree([own_tail[...].astype(f32)] + [tail_of(r) for r in received])
         norm = from_tail(tile)
         beta = norm / norm_now[0:1, :]
@@ -285,7 +285,8 @@
         direction[...] = d
         norm_out[...] = jnp.broadcast_to(norm, norm_out.shape)
         beta_out[...] = jnp.broadcast_to(beta, beta_out.shape)
-    kept[...] = projected
+    if not last:
+        rest[-1][...] = projected
     weighted = spread[...] * projected
     width = cfg["width"]
     for j in range(cfg["nb"]):
@@ -347,7 +348,7 @@
     others = cfg["rows"] - 1
     own, own_tail = refs[:2]
     received = refs[2 : 2 + others]
-    direction, residual, norm_now, share, after, norm_out, alpha_out = refs[2 + others :]
+    direction, residual, norm_now, share, alpha_out, *kept = refs[2 + others :]
     rows = own.shape[0]
     image = tree([own[...]] + [r[:rows, :].astype(f32) for r in received])
     width = cfg["width"]
@@ -357,8 +358,9 @@
     norm = from_tail(tile, 1) if first else norm_now[0:1, :]
     alpha = norm / from_tail(tile)
     left = residual[...] - alpha * image
-    after[...] = left
-    norm_out[...] = jnp.broadcast_to(norm, norm_out.shape)
+    if kept:
+        kept[0][...] = left
+        kept[1][...] = jnp.broadcast_to(norm, kept[1].shape)
     alpha_out[...] = jnp.broadcast_to(alpha, alpha_out.shape)
     share[:rows, :] = left.astype(bf16)
     share[rows:, :] = to_tail([column_sum(left * left)])
@@ -560,7 +562,7 @@
     share = spread = before = None
     norm_now = jnp.zeros((8, directions), f32)
     for iteration in range(ITERS):
-        first = iteration == 0
+        first, last = iteration == 0, iteration == ITERS - 1
         if first:
             send, keep, keep_tail, direction = begin()
             residual = direction
@@ -578,36 +580,34 @@
         received = along_col(sends)
         if first:
             matrix.append(lay_out())
-            scaled, before, spread = call(
-                functools.partial(scale_kernel, cfg, True),
+            scaled, spread, before = call(
+                functools.partial(scale_kernel, cfg, True, False),
                 [shape(own_rows + TAIL, bf16), shape(own_rows, f32), shape(own_rows, f32)],
                 [own, own_tail, *received, removed, margins, direction],
             )
         else:
-            scaled, before, direction, norm_now, beta = call(
-                functools.partial(scale_kernel, cfg, False),
+            scaled, direction, norm_now, beta, *kept = call(
+                functools.partial(scale_kernel, cfg, False, last),
                 [
                     shape(own_rows + TAIL, bf16),
-                    shape(own_rows, f32),
                     shape(own_features, f32),
                     shape(8, f32),
                     shape(8, f32),
-                ],
+                ]
+                + [shape(own_rows, f32)] * (not last),
                 [own, own_tail, *received, spread, residual, direction, before, norm_now],
             )
+            before = None if last else kept[0]
             betas.append(beta)
         sends, own, own_tail = backward(scaled, first)
         received = along_row(sends)
-        share, residual, norm_now, alpha = call(
+        share, alpha, *kept = call(
             functools.partial(update_kernel, cfg, first),
-            [
-                shape(own_features + TAIL, bf16),
-                shape(own_features, f32),
-                shape(8, f32),
-                shape(8, f32),
-            ],
+            [shape(own_features + TAIL, bf16), shape(8, f32)]
+            + [shape(own_features, f32), shape(8, f32)] * (not last),
             [own, own_tail, *received, direction, residual, norm_now],
         )
+        residual, norm_now = (None, None) if last else kept
         alphas.append(alpha)
     parts = [share, *along_row([share] * (rows_axis - 1))]
     (answer,) = call(

time: 178 us -> 175 us (0.983)
  Pallas kernels: 38.1 us -> 36.2 us
    pallas_call x39 -> x37, Pallas kernels: 27.3 us -> 25.4 us  [call(): pl.pallas_call(kernel, out_shape=out, in_specs=[VMEM] * len(inputs), out_...]
  transfers between devices with their start and end apart: 51 -> 51, of which waited for: 32 -> 36; matrix products, arithmetic and copies ran while one was open for 1% -> 1% of each run, Pallas kernels for 14% -> 14%
where the time goes in v4:
time: 175 us
  waiting for transfers between devices  85.2 us (49%)
  starting transfers between devices  50.9 us (29%)
  Pallas kernels  36.2 us (21%)
    ppermute x51, waiting for transfers between devices, moved(): return lax.ppermute(value, ('row', 'col'), pairs)  85.2 us
    ppermute x51, starting transfers between devices, moved(): return lax.ppermute(value, ('row', 'col'), pairs)  50.9 us
    pallas_call x37, Pallas kernels, call(): pl.pallas_call(kernel, out_shape=out, in_specs=[VMEM] * len(inputs), out_...  25.4 us
    pallas_call x1, Pallas kernels, begin(): pl.pallas_call(functools.partial(first_kernel, cfg), out_shape=[pltpu.VME...  6.13 us
    pallas_call x1, Pallas kernels, lay_out(): pl.pallas_call(functools.partial(dense_kernel, cfg), out_shape=pltpu.VMEM...  4.67 us
  transfers between devices with their start and end apart: 51, of which 36 were waited for; matrix products, arithmetic and copies ran while one was open for 1% of the time, Pallas kernels for 14%

profile of v4, /device:TPU:0, one launch (start us, length us, event | category | flops | bytes accessed | tf_op | source)
XLA Modules:
  0.0 174.9 jit_solution(2116893771472496301)
XLA Ops:
  0.6 6.1 %shard_map.68 = (bf16[2056,128]{1,0:T(8,128)(2,1)S(1)}, f32[2048,128]{1,0:T(8,128)S(1)}, bf16[8,128]{1,0:T(8,128)(2,1)S(1)}, f32[512,128]{1,0:T(8,128)S(1)}) custom-call(s32[256]{0:T(256)} %bitcast.3, bf16[256,128,128]{2,1,0:T(8,128)(2,1)} %listed.3, f32[2048,128]{1,0:T(8,128)} %refs_0_.1), custom_call_target="tpu_custom_call" | custom-call | tf_op jit(solution)/shard_map/pallas_call | solution.py:473
  7.3 1.5 collective-permute-done.refs_2_
  9.0 2.9 %collective-permute-start.1 = (bf16[520,128]{1,0:T(8,128)(2,1)S(1)}, bf16[520,128]{1,0:T(8,128)(2,1)S(1)}, u32[]{:S(2)}, u32[]{:S(2)}) collective-permute-start(bf16[520,128]{1,0:T(8,128)(2,1)S(1)} %get-tuple-element.110), channel_id=1, source_target_pairs={{0,2},{1,5},{2,0},{3,7},{4,6},{5,1},{6,4},{7,3},{8,10},{9,13},{10,... | collective-permute-start | bytes 399368 | tf_op jit(solution)/shard_map/ppermute | solution.py:413
  11.9 1.5 collective-permute-start.2
  15.4 3.4 %collective-permute-done.2.refs_3_ = bf16[520,128]{1,0:T(8,128)(2,1)S(1)} collective-permute-done((bf16[520,128]{1,0:T(8,128)(2,1)S(1)}, bf16[520,128]{1,0:T(8,128)(2,1)S(1)}, u32[]{:S(2)}, u32[]{:S(2)}) %collective-permute-start.2) | collective-permute-done | bytes 133152 | tf_op jit(solution)/shard_map/ppermute | solution.py:413
  20.8 1.7 collective-permute-start.5
  24.4 2.9 %collective-permute-done.5.refs_1_.refs_2_ = bf16[520,128]{1,0:T(8,128)(2,1)S(1)} collective-permute-done((bf16[520,128]{1,0:T(8,128)(2,1)S(1)}, bf16[520,128]{1,0:T(8,128)(2,1)S(1)}, u32[]{:S(2)}, u32[]{:S(2)}) %collective-permute-start.5) | collective-permute-done | bytes 133152 | tf_op jit(solution)/shard_map/ppermute | solution.py:413
  27.3 3.1 %collective-permute-done.7.refs_1_.refs_4_ = bf16[520,128]{1,0:T(8,128)(2,1)S(1)} collective-permute-done((bf16[520,128]{1,0:T(8,128)(2,1)S(1)}, bf16[520,128]{1,0:T(8,128)(2,1)S(1)}, u32[]{:S(2)}, u32[]{:S(2)}) %collective-permute-start.7) | collective-permute-done | bytes 133152 | tf_op jit(solution)/shard_map/ppermute | solution.py:413
  30.9 4.7 %shard_map.71.refs_1_ = bf16[4,4096,512]{2,1,0:T(8,128)(2,1)S(1)} custom-call(s32[256]{0:T(256)} %bitcast.4, bf16[256,128,128]{2,1,0:T(8,128)(2,1)} %listed.3), custom_call_target="tpu_custom_call" | custom-call | tf_op jit(solution)/shard_map/pallas_call | solution.py:496
  39.0 3.6 %collective-permute-start.11 = (bf16[520,128]{1,0:T(8,128)(2,1)S(1)}, bf16[520,128]{1,0:T(8,128)(2,1)S(1)}, u32[]{:S(2)}, u32[]{:S(2)}) collective-permute-start(bf16[520,128]{1,0:T(8,128)(2,1)S(1)} %get-tuple-element.126), channel_id=1, source_target_pairs={{0,24},{1,25},{2,26},{3,27},{4,28},{5,29},{6,30},{7,31},{8,16},{9,... | collective-permute-start | bytes 399368 | tf_op jit(solution)/shard_map/ppermute | solution.py:413
  43.7 3.7 %collective-permute-done.11.refs_2_ = bf16[520,128]{1,0:T(8,128)(2,1)S(1)} collective-permute-done((bf16[520,128]{1,0:T(8,128)(2,1)S(1)}, bf16[520,128]{1,0:T(8,128)(2,1)S(1)}, u32[]{:S(2)}, u32[]{:S(2)}) %collective-permute-start.11) | collective-permute-done | bytes 133152 | tf_op jit(solution)/shard_map/ppermute | solution.py:413
  47.3 2.4 %collective-permute-done.12.refs_3_ = bf16[520,128]{1,0:T(8,128)(2,1)S(1)} collective-permute-done((bf16[520,128]{1,0:T(8,128)(2,1)S(1)}, bf16[520,128]{1,0:T(8,128)(2,1)S(1)}, u32[]{:S(2)}, u32[]{:S(2)}) %collective-permute-start.12) | collective-permute-done | bytes 133152 | tf_op jit(solution)/shard_map/ppermute | solution.py:413
  49.7 4.3 %collective-permute-done.13.refs_4_ = bf16[520,128]{1,0:T(8,128)(2,1)S(1)} collective-permute-done((bf16[520,128]{1,0:T(8,128)(2,1)S(1)}, bf16[520,128]{1,0:T(8,128)(2,1)S(1)}, u32[]{:S(2)}, u32[]{:S(2)}) %collective-permute-start.13) | collective-permute-done | bytes 133152 | tf_op jit(solution)/shard_map/ppermute | solution.py:413
  54.2 2.6 %collective-permute-start.14 = (bf16[520,128]{1,0:T(8,128)(2,1)S(1)}, bf16[520,128]{1,0:T(8,128)(2,1)S(1)}, u32[]{:S(2)}, u32[]{:S(2)}) collective-permute-start(bf16[520,128]{1,0:T(8,128)(2,1)S(1)} %get-tuple-element.129.refs_0_.refs_1_), channel_id=1, source_target_pairs={{0,24},{1,25},{2,26},{3,27},{4,28},{5,29},{6,30},{7,31},{8,16},{9,... | collective-permute-start | bytes 399368 | tf_op jit(solution)/shard_map/ppermute | solution.py:413
  56.8 1.9 %collective-permute-start.16 = (bf16[520,128]{1,0:T(8,128)(2,1)S(1)}, bf16[520,128]{1,0:T(8,128)(2,1)S(1)}, u32[]{:S(2)}, u32[]{:S(2)}) collective-permute-start(bf16[520,128]{1,0:T(8,128)(2,1)S(1)} %get-tuple-element.129.refs_0_.refs_1_), channel_id=1, source_target_pairs={{0,16},{1,9},{2,18},{3,11},{4,20},{5,13},{6,22},{7,15},{8,24},{9,1... | collective-permute-start | bytes 399368 | tf_op jit(solution)/shard_map/ppermute | solution.py:413
  59.9 2.6 %collective-permute-done.14.refs_0_.refs_1_.refs_2_ = bf16[520,128]{1,0:T(8,128)(2,1)S(1)} collective-permute-done((bf16[520,128]{1,0:T(8,128)(2,1)S(1)}, bf16[520,128]{1,0:T(8,128)(2,1)S(1)}, u32[]{:S(2)}, u32[]{:S(2)}) %collective-permute-start.14) | collective-permute-done | bytes 133152 | tf_op jit(solution)/shard_map/ppermute | solution.py:413
  62.5 1.6 shard_map.80
  64.0 2.1 %collective-permute-done.15.refs_2_.refs_3_ = bf16[520,128]{1,0:T(8,128)(2,1)S(1)} collective-permute-done((bf16[520,128]{1,0:T(8,128)(2,1)S(1)}, bf16[520,128]{1,0:T(8,128)(2,1)S(1)}, u32[]{:S(2)}, u32[]{:S(2)}) %collective-permute-start.15) | collective-permute-done | bytes 133152 | tf_op jit(solution)/shard_map/ppermute | solution.py:413
  71.5 1.4 collective-permute-start.19
  73.8 2.7 %collective-permute-done.18.refs_2_ = bf16[520,128]{1,0:T(8,128)(2,1)S(1)} collective-permute-done((bf16[520,128]{1,0:T(8,128)(2,1)S(1)}, bf16[520,128]{1,0:T(8,128)(2,1)S(1)}, u32[]{:S(2)}, u32[]{:S(2)}) %collective-permute-start.18) | collective-permute-done | bytes 133152 | tf_op jit(solution)/shard_map/ppermute | solution.py:413
  76.5 3.4 %collective-permute-done.20.refs_4_ = bf16[520,128]{1,0:T(8,128)(2,1)S(1)} collective-permute-done((bf16[520,128]{1,0:T(8,128)(2,1)S(1)}, bf16[520,128]{1,0:T(8,128)(2,1)S(1)}, u32[]{:S(2)}, u32[]{:S(2)}) %collective-permute-start.20) | collective-permute-done | bytes 133152 | tf_op jit(solution)/shard_map/ppermute | solution.py:413
  82.2 1.5 collective-permute-start.26
  83.7 2.9 %collective-permute-done.22.refs_1_.refs_2_ = bf16[520,128]{1,0:T(8,128)(2,1)S(1)} collective-permute-done((bf16[520,128]{1,0:T(8,128)(2,1)S(1)}, bf16[520,128]{1,0:T(8,128)(2,1)S(1)}, u32[]{:S(2)}, u32[]{:S(2)}) %collective-permute-start.22) | collective-permute-done | bytes 133152 | tf_op jit(solution)/shard_map/ppermute | solution.py:413
  87.2 2.2 %collective-permute-done.26.refs_1_.refs_6_ = bf16[520,128]{1,0:T(8,128)(2,1)S(1)} collective-permute-done((bf16[520,128]{1,0:T(8,128)(2,1)S(1)}, bf16[520,128]{1,0:T(8,128)(2,1)S(1)}, u32[]{:S(2)}, u32[]{:S(2)}) %collective-permute-start.26) | collective-permute-done | bytes 133152 | tf_op jit(solution)/shard_map/ppermute | solution.py:413
  93.0 2.9 %collective-permute-start.28 = (bf16[520,128]{1,0:T(8,128)(2,1)S(1)}, bf16[520,128]{1,0:T(8,128)(2,1)S(1)}, u32[]{:S(2)}, u32[]{:S(2)}) collective-permute-start(bf16[520,128]{1,0:T(8,128)(2,1)S(1)} %get-tuple-element.161), channel_id=1, source_target_pairs={{0,24},{1,25},{2,26},{3,27},{4,28},{5,29},{6,30},{7,31},{8,16},{9,... | collective-permute-start | bytes 399368 | tf_op jit(solution)/shard_map/ppermute | solution.py:413
  96.0 1.5 collective-permute-start.30
  97.7 3.7 %collective-permute-done.28.refs_2_ = bf16[520,128]{1,0:T(8,128)(2,1)S(1)} collective-permute-done((bf16[520,128]{1,0:T(8,128)(2,1)S(1)}, bf16[520,128]{1,0:T(8,128)(2,1)S(1)}, u32[]{:S(2)}, u32[]{:S(2)}) %collective-permute-start.28) | collective-permute-done | bytes 133152 | tf_op jit(solution)/shard_map/ppermute | solution.py:413
  101.4 4.0 %collective-permute-done.29.refs_3_ = bf16[520,128]{1,0:T(8,128)(2,1)S(1)} collective-permute-done((bf16[520,128]{1,0:T(8,128)(2,1)S(1)}, bf16[520,128]{1,0:T(8,128)(2,1)S(1)}, u32[]{:S(2)}, u32[]{:S(2)}) %collective-permute-start.29) | collective-permute-done | bytes 133152 | tf_op jit(solution)/shard_map/ppermute | solution.py:413
  105.4 2.0 %collective-permute-done.30.refs_4_ = bf16[520,128]{1,0:T(8,128)(2,1)S(1)} collective-permute-done((bf16[520,128]{1,0:T(8,128)(2,1)S(1)}, bf16[520,128]{1,0:T(8,128)(2,1)S(1)}, u32[]{:S(2)}, u32[]{:S(2)}) %collective-permute-start.30) | collective-permute-done | bytes 133152 | tf_op jit(solution)/shard_map/ppermute | solution.py:413
  107.6 2.6 %collective-permute-start.31 = (bf16[520,128]{1,0:T(8,128)(2,1)S(1)}, bf16[520,128]{1,0:T(8,128)(2,1)S(1)}, u32[]{:S(2)}, u32[]{:S(2)}) collective-permute-start(bf16[520,128]{1,0:T(8,128)(2,1)S(1)} %get-tuple-element.166.refs_0_.refs_5_), channel_id=1, source_target_pairs={{0,24},{1,25},{2,26},{3,27},{4,28},{5,29},{6,30},{7,31},{8,16},{9,... | collective-permute-start | bytes 399368 | tf_op jit(solution)/shard_map/ppermute | solution.py:413
  110.3 1.8 %collective-permute-start.33 = (bf16[520,128]{1,0:T(8,128)(2,1)S(1)}, bf16[520,128]{1,0:T(8,128)(2,1)S(1)}, u32[]{:S(2)}, u32[]{:S(2)}) collective-permute-start(bf16[520,128]{1,0:T(8,128)(2,1)S(1)} %get-tuple-element.166.refs_0_.refs_5_), channel_id=1, source_target_pairs={{0,16},{1,9},{2,18},{3,11},{4,20},{5,13},{6,22},{7,15},{8,24},{9,1... | collective-permute-start | bytes 399368 | tf_op jit(solution)/shard_map/ppermute | solution.py:413
  113.3 2.6 %collective-permute-done.31.refs_0_.refs_1_.refs_6_ = bf16[520,128]{1,0:T(8,128)(2,1)S(1)} collective-permute-done((bf16[520,128]{1,0:T(8,128)(2,1)S(1)}, bf16[520,128]{1,0:T(8,128)(2,1)S(1)}, u32[]{:S(2)}, u32[]{:S(2)}) %collective-permute-start.31) | collective-permute-done | bytes 133152 | tf_op jit(solution)/shard_map/ppermute | solution.py:413
  115.9 1.5 shard_map.93
  118.8 1.7 collective-permute-done.33.refs_3_.refs_8_
  127.4 2.6 %collective-permute-done.35.refs_2_ = bf16[520,128]{1,0:T(8,128)(2,1)S(1)} collective-permute-done((bf16[520,128]{1,0:T(8,128)(2,1)S(1)}, bf16[520,128]{1,0:T(8,128)(2,1)S(1)}, u32[]{:S(2)}, u32[]{:S(2)}) %collective-permute-start.35) | collective-permute-done | bytes 133152 | tf_op jit(solution)/shard_map/ppermute | solution.py:413
  130.1 3.4 %collective-permute-done.37.refs_4_ = bf16[520,128]{1,0:T(8,128)(2,1)S(1)} collective-permute-done((bf16[520,128]{1,0:T(8,128)(2,1)S(1)}, bf16[520,128]{1,0:T(8,128)(2,1)S(1)}, u32[]{:S(2)}, u32[]{:S(2)}) %collective-permute-start.37) | collective-permute-done | bytes 133152 | tf_op jit(solution)/shard_map/ppermute | solution.py:413
  137.3 2.9 %collective-permute-done.39.refs_1_.refs_2_ = bf16[520,128]{1,0:T(8,128)(2,1)S(1)} collective-permute-done((bf16[520,128]{1,0:T(8,128)(2,1)S(1)}, bf16[520,128]{1,0:T(8,128)(2,1)S(1)}, u32[]{:S(2)}, u32[]{:S(2)}) %collective-permute-start.39) | collective-permute-done | bytes 133152 | tf_op jit(solution)/shard_map/ppermute | solution.py:413
  140.7 2.2 %collective-permute-done.43.refs_1_.refs_6_ = bf16[520,128]{1,0:T(8,128)(2,1)S(1)} collective-permute-done((bf16[520,128]{1,0:T(8,128)(2,1)S(1)}, bf16[520,128]{1,0:T(8,128)(2,1)S(1)}, u32[]{:S(2)}, u32[]{:S(2)}) %collective-permute-start.43) | collective-permute-done | bytes 133152 | tf_op jit(solution)/shard_map/ppermute | solution.py:413
  146.3 2.4 %collective-permute-start.45 = (bf16[520,128]{1,0:T(8,128)(2,1)S(1)}, bf16[520,128]{1,0:T(8,128)(2,1)S(1)}, u32[]{:S(2)}, u32[]{:S(2)}) collective-permute-start(bf16[520,128]{1,0:T(8,128)(2,1)S(1)} %get-tuple-element.199), channel_id=1, source_target_pairs={{0,24},{1,25},{2,26},{3,27},{4,28},{5,29},{6,30},{7,31},{8,16},{9,... | collective-permute-start | bytes 399368 | tf_op jit(solution)/shard_map/ppermute | solution.py:413
  148.9 1.9 %collective-permute-start.47 = (bf16[520,128]{1,0:T(8,128)(2,1)S(1)}, bf16[520,128]{1,0:T(8,128)(2,1)S(1)}, u32[]{:S(2)}, u32[]{:S(2)}) collective-permute-start(bf16[520,128]{1,0:T(8,128)(2,1)S(1)} %get-tuple-element.201), channel_id=1, source_target_pairs={{0,16},{1,9},{2,18},{3,11},{4,20},{5,13},{6,22},{7,15},{8,24},{9,1... | collective-permute-start | bytes 399368 | tf_op jit(solution)/shard_map/ppermute | solution.py:413
  151.0 3.7 %collective-permute-done.45.refs_2_ = bf16[520,128]{1,0:T(8,128)(2,1)S(1)} collective-permute-done((bf16[520,128]{1,0:T(8,128)(2,1)S(1)}, bf16[520,128]{1,0:T(8,128)(2,1)S(1)}, u32[]{:S(2)}, u32[]{:S(2)}) %collective-permute-start.45) | collective-permute-done | bytes 133152 | tf_op jit(solution)/shard_map/ppermute | solution.py:413
  154.7 3.9 %collective-permute-done.46.refs_3_ = bf16[520,128]{1,0:T(8,128)(2,1)S(1)} collective-permute-done((bf16[520,128]{1,0:T(8,128)(2,1)S(1)}, bf16[520,128]{1,0:T(8,128)(2,1)S(1)}, u32[]{:S(2)}, u32[]{:S(2)}) %collective-permute-start.46) | collective-permute-done | bytes 133152 | tf_op jit(solution)/shard_map/ppermute | solution.py:413
  158.6 2.2 %collective-permute-done.47.refs_4_ = bf16[520,128]{1,0:T(8,128)(2,1)S(1)} collective-permute-done((bf16[520,128]{1,0:T(8,128)(2,1)S(1)}, bf16[520,128]{1,0:T(8,128)(2,1)S(1)}, u32[]{:S(2)}, u32[]{:S(2)}) %collective-permute-start.47) | collective-permute-done | bytes 133152 | tf_op jit(solution)/shard_map/ppermute | solution.py:413
  161.0 2.5 %collective-permute-start.48 = (bf16[520,128]{1,0:T(8,128)(2,1)S(1)}, bf16[520,128]{1,0:T(8,128)(2,1)S(1)}, u32[]{:S(2)}, u32[]{:S(2)}) collective-permute-start(bf16[520,128]{1,0:T(8,128)(2,1)S(1)} %get-tuple-element.207.refs_0_), channel_id=1, source_target_pairs={{0,24},{1,25},{2,26},{3,27},{4,28},{5,29},{6,30},{7,31},{8,16},{9,... | collective-permute-start | bytes 399368 | tf_op jit(solution)/shard_map/ppermute | solution.py:413
  163.5 1.9 %collective-permute-start.50 = (bf16[520,128]{1,0:T(8,128)(2,1)S(1)}, bf16[520,128]{1,0:T(8,128)(2,1)S(1)}, u32[]{:S(2)}, u32[]{:S(2)}) collective-permute-start(bf16[520,128]{1,0:T(8,128)(2,1)S(1)} %get-tuple-element.207.refs_0_), channel_id=1, source_target_pairs={{0,16},{1,9},{2,18},{3,11},{4,20},{5,13},{6,22},{7,15},{8,24},{9,1... | collective-permute-start | bytes 399368 | tf_op jit(solution)/shard_map/ppermute | solution.py:413
  166.8 2.5 %collective-permute-done.48.refs_1_ = bf16[520,128]{1,0:T(8,128)(2,1)S(1)} collective-permute-done((bf16[520,128]{1,0:T(8,128)(2,1)S(1)}, bf16[520,128]{1,0:T(8,128)(2,1)S(1)}, u32[]{:S(2)}, u32[]{:S(2)}) %collective-permute-start.48) | collective-permute-done | bytes 133152 | tf_op jit(solution)/shard_map/ppermute | solution.py:413
  169.3 2.8 %collective-permute-done.49.refs_2_ = bf16[520,128]{1,0:T(8,128)(2,1)S(1)} collective-permute-done((bf16[520,128]{1,0:T(8,128)(2,1)S(1)}, bf16[520,128]{1,0:T(8,128)(2,1)S(1)}, u32[]{:S(2)}, u32[]{:S(2)}) %collective-permute-start.49) | collective-permute-done | bytes 133152 | tf_op jit(solution)/shard_map/ppermute | solution.py:413
  172.1 1.7 collective-permute-done.50.refs_3_
  (101 shorter events, 46.0 us)
Async XLA Ops:
  9.0 6.4 %collective-permute-start.1 = (bf16[520,128]{1,0:T(8,128)(2,1)S(1)}, bf16[520,128]{1,0:T(8,128)(2,1)S(1)}, u32[]{:S(2)}, u32[]{:S(2)}) collective-permute-start(bf16[520,128]{1,0:T(8,128)(2,1)S(1)} %get-tuple-element.110), channel_id=1, source_target_pairs={{0,2},{1,5},{2,0},{3,7},{4,6},{5,1},{6,4},{7,3},{8,10},{9,13},{10,... | collective-permute-start | bytes 399368 | tf_op jit(solution)/shard_map/ppermute | solution.py:413
  11.9 6.9 %collective-permute-start.2 = (bf16[520,128]{1,0:T(8,128)(2,1)S(1)}, bf16[520,128]{1,0:T(8,128)(2,1)S(1)}, u32[]{:S(2)}, u32[]{:S(2)}) collective-permute-start(bf16[520,128]{1,0:T(8,128)(2,1)S(1)} %get-tuple-element.111), channel_id=1, source_target_pairs={{0,4},{1,3},{2,6},{3,1},{4,0},{5,7},{6,2},{7,5},{8,12},{9,11},{10,... | collective-permute-start | bytes 399368 | tf_op jit(solution)/shard_map/ppermute | solution.py:413
  13.4 6.5 %collective-permute-start.3 = (bf16[520,128]{1,0:T(8,128)(2,1)S(1)}, bf16[520,128]{1,0:T(8,128)(2,1)S(1)}, u32[]{:S(2)}, u32[]{:S(2)}) collective-permute-start(bf16[520,128]{1,0:T(8,128)(2,1)S(1)} %get-tuple-element.112), channel_id=1, source_target_pairs={{0,6},{1,7},{2,4},{3,5},{4,2},{5,3},{6,0},{7,1},{8,14},{9,15},{10,... | collective-permute-start | bytes 399368 | tf_op jit(solution)/shard_map/ppermute | solution.py:413
  20.8 6.5 %collective-permute-start.5 = (bf16[520,128]{1,0:T(8,128)(2,1)S(1)}, bf16[520,128]{1,0:T(8,128)(2,1)S(1)}, u32[]{:S(2)}, u32[]{:S(2)}) collective-permute-start(bf16[520,128]{1,0:T(8,128)(2,1)S(1)} %get-tuple-element.114.refs_0_), channel_id=1, source_target_pairs={{0,2},{1,5},{2,0},{3,7},{4,6},{5,1},{6,4},{7,3},{8,10},{9,13},{10,... | collective-permute-start | bytes 399368 | tf_op jit(solution)/shard_map/ppermute | solution.py:413
  22.5 7.8 %collective-permute-start.7 = (bf16[520,128]{1,0:T(8,128)(2,1)S(1)}, bf16[520,128]{1,0:T(8,128)(2,1)S(1)}, u32[]{:S(2)}, u32[]{:S(2)}) collective-permute-start(bf16[520,128]{1,0:T(8,128)(2,1)S(1)} %get-tuple-element.114.refs_0_), channel_id=1, source_target_pairs={{0,4},{1,3},{2,6},{3,1},{4,0},{5,7},{6,2},{7,5},{8,12},{9,11},{10,... | collective-permute-start | bytes 399368 | tf_op jit(solution)/shard_map/ppermute | solution.py:413
  23.2 7.1 %collective-permute-start.9 = (bf16[520,128]{1,0:T(8,128)(2,1)S(1)}, bf16[520,128]{1,0:T(8,128)(2,1)S(1)}, u32[]{:S(2)}, u32[]{:S(2)}) collective-permute-start(bf16[520,128]{1,0:T(8,128)(2,1)S(1)} %get-tuple-element.114.refs_0_), channel_id=1, source_target_pairs={{0,6},{1,7},{2,4},{3,5},{4,2},{5,3},{6,0},{7,1},{8,14},{9,15},{10,... | collective-permute-start | bytes 399368 | tf_op jit(solution)/shard_map/ppermute | solution.py:413
  24.4 11.6 %collective-permute-start.4 = (bf16[520,128]{1,0:T(8,128)(2,1)S(1)}, bf16[520,128]{1,0:T(8,128)(2,1)S(1)}, u32[]{:S(2)}, u32[]{:S(2)}) collective-permute-start(bf16[520,128]{1,0:T(8,128)(2,1)S(1)} %get-tuple-element.114.refs_0_), channel_id=1, source_target_pairs={{0,1},{1,0},{2,3},{3,2},{4,5},{5,4},{6,7},{7,6},{8,9},{9,8},{10,11... | collective-permute-start | bytes 399368 | tf_op jit(solution)/shard_map/ppermute | solution.py:413
  27.3 9.6 %collective-permute-start.6 = (bf16[520,128]{1,0:T(8,128)(2,1)S(1)}, bf16[520,128]{1,0:T(8,128)(2,1)S(1)}, u32[]{:S(2)}, u32[]{:S(2)}) collective-permute-start(bf16[520,128]{1,0:T(8,128)(2,1)S(1)} %collective-permute-done.5.refs_1_.refs_2_), channel_id=1, source_target_pairs={{0,1},{1,0},{2,3},{3,2},{4,5},{5,4},{6,7},{7,6},{8,9},{9,8},{10,11... | collective-permute-start | bytes 399368 | tf_op jit(solution)/shard_map/ppermute | solution.py:413
  30.4 7.3 %collective-permute-start.8 = (bf16[520,128]{1,0:T(8,128)(2,1)S(1)}, bf16[520,128]{1,0:T(8,128)(2,1)S(1)}, u32[]{:S(2)}, u32[]{:S(2)}) collective-permute-start(bf16[520,128]{1,0:T(8,128)(2,1)S(1)} %collective-permute-done.7.refs_1_.refs_4_), channel_id=1, source_target_pairs={{0,1},{1,0},{2,3},{3,2},{4,5},{5,4},{6,7},{7,6},{8,9},{9,8},{10,11... | collective-permute-start | bytes 399368 | tf_op jit(solution)/shard_map/ppermute | solution.py:413
  30.4 8.2 %collective-permute-start.10 = (bf16[520,128]{1,0:T(8,128)(2,1)S(1)}, bf16[520,128]{1,0:T(8,128)(2,1)S(1)}, u32[]{:S(2)}, u32[]{:S(2)}) collective-permute-start(bf16[520,128]{1,0:T(8,128)(2,1)S(1)} %collective-permute-done.9.refs_1_.refs_6_), channel_id=1, source_target_pairs={{0,1},{1,0},{2,3},{3,2},{4,5},{5,4},{6,7},{7,6},{8,9},{9,8},{10,11... | collective-permute-start | bytes 399368 | tf_op jit(solution)/shard_map/ppermute | solution.py:413
  39.0 8.4 %collective-permute-start.11 = (bf16[520,128]{1,0:T(8,128)(2,1)S(1)}, bf16[520,128]{1,0:T(8,128)(2,1)S(1)}, u32[]{:S(2)}, u32[]{:S(2)}) collective-permute-start(bf16[520,128]{1,0:T(8,128)(2,1)S(1)} %get-tuple-element.126), channel_id=1, source_target_pairs={{0,24},{1,25},{2,26},{3,27},{4,28},{5,29},{6,30},{7,31},{8,16},{9,... | collective-permute-start | bytes 399368 | tf_op jit(solution)/shard_map/ppermute | solution.py:413
  42.6 7.1 %collective-permute-start.12 = (bf16[520,128]{1,0:T(8,128)(2,1)S(1)}, bf16[520,128]{1,0:T(8,128)(2,1)S(1)}, u32[]{:S(2)}, u32[]{:S(2)}) collective-permute-start(bf16[520,128]{1,0:T(8,128)(2,1)S(1)} %get-tuple-element.127), channel_id=1, source_target_pairs={{0,8},{1,17},{2,10},{3,19},{4,12},{5,21},{6,14},{7,23},{8,0},{9,25... | collective-permute-start | bytes 399368 | tf_op jit(solution)/shard_map/ppermute | solution.py:413
  42.6 11.4 %collective-permute-start.13 = (bf16[520,128]{1,0:T(8,128)(2,1)S(1)}, bf16[520,128]{1,0:T(8,128)(2,1)S(1)}, u32[]{:S(2)}, u32[]{:S(2)}) collective-permute-start(bf16[520,128]{1,0:T(8,128)(2,1)S(1)} %get-tuple-element.128), channel_id=1, source_target_pairs={{0,16},{1,9},{2,18},{3,11},{4,20},{5,13},{6,22},{7,15},{8,24},{9,1... | collective-permute-start | bytes 399368 | tf_op jit(solution)/shard_map/ppermute | solution.py:413
  54.2 8.3 %collective-permute-start.14 = (bf16[520,128]{1,0:T(8,128)(2,1)S(1)}, bf16[520,128]{1,0:T(8,128)(2,1)S(1)}, u32[]{:S(2)}, u32[]{:S(2)}) collective-permute-start(bf16[520,128]{1,0:T(8,128)(2,1)S(1)} %get-tuple-element.129.refs_0_.refs_1_), channel_id=1, source_target_pairs={{0,24},{1,25},{2,26},{3,27},{4,28},{5,29},{6,30},{7,31},{8,16},{9,... | collective-permute-start | bytes 399368 | tf_op jit(solution)/shard_map/ppermute | solution.py:413
  56.8 9.3 %collective-permute-start.15 = (bf16[520,128]{1,0:T(8,128)(2,1)S(1)}, bf16[520,128]{1,0:T(8,128)(2,1)S(1)}, u32[]{:S(2)}, u32[]{:S(2)}) collective-permute-start(bf16[520,128]{1,0:T(8,128)(2,1)S(1)} %get-tuple-element.129.refs_0_.refs_1_), channel_id=1, source_target_pairs={{0,8},{1,17},{2,10},{3,19},{4,12},{5,21},{6,14},{7,23},{8,0},{9,25... | collective-permute-start | bytes 399368 | tf_op jit(solution)/shard_map/ppermute | solution.py:413
  56.8 10.1 %collective-permute-start.16 = (bf16[520,128]{1,0:T(8,128)(2,1)S(1)}, bf16[520,128]{1,0:T(8,128)(2,1)S(1)}, u32[]{:S(2)}, u32[]{:S(2)}) collective-permute-start(bf16[520,128]{1,0:T(8,128)(2,1)S(1)} %get-tuple-element.129.refs_0_.refs_1_), channel_id=1, source_target_pairs={{0,16},{1,9},{2,18},{3,11},{4,20},{5,13},{6,22},{7,15},{8,24},{9,1... | collective-permute-start | bytes 399368 | tf_op jit(solution)/shard_map/ppermute | solution.py:413
  70.2 6.3 %collective-permute-start.18 = (bf16[520,128]{1,0:T(8,128)(2,1)S(1)}, bf16[520,128]{1,0:T(8,128)(2,1)S(1)}, u32[]{:S(2)}, u32[]{:S(2)}) collective-permute-start(bf16[520,128]{1,0:T(8,128)(2,1)S(1)} %get-tuple-element.141), channel_id=1, source_target_pairs={{0,2},{1,5},{2,0},{3,7},{4,6},{5,1},{6,4},{7,3},{8,10},{9,13},{10,... | collective-permute-start | bytes 399368 | tf_op jit(solution)/shard_map/ppermute | solution.py:413
  71.5 5.0 %collective-permute-start.19 = (bf16[520,128]{1,0:T(8,128)(2,1)S(1)}, bf16[520,128]{1,0:T(8,128)(2,1)S(1)}, u32[]{:S(2)}, u32[]{:S(2)}) collective-permute-start(bf16[520,128]{1,0:T(8,128)(2,1)S(1)} %get-tuple-element.142), channel_id=1, source_target_pairs={{0,4},{1,3},{2,6},{3,1},{4,0},{5,7},{6,2},{7,5},{8,12},{9,11},{10,... | collective-permute-start | bytes 399368 | tf_op jit(solution)/shard_map/ppermute | solution.py:413
  72.9 7.0 %collective-permute-start.20 = (bf16[520,128]{1,0:T(8,128)(2,1)S(1)}, bf16[520,128]{1,0:T(8,128)(2,1)S(1)}, u32[]{:S(2)}, u32[]{:S(2)}) collective-permute-start(bf16[520,128]{1,0:T(8,128)(2,1)S(1)} %get-tuple-element.143), channel_id=1, source_target_pairs={{0,6},{1,7},{2,4},{3,5},{4,2},{5,3},{6,0},{7,1},{8,14},{9,15},{10,... | collective-permute-start | bytes 399368 | tf_op jit(solution)/shard_map/ppermute | solution.py:413
  80.2 6.5 %collective-permute-start.22 = (bf16[520,128]{1,0:T(8,128)(2,1)S(1)}, bf16[520,128]{1,0:T(8,128)(2,1)S(1)}, u32[]{:S(2)}, u32[]{:S(2)}) collective-permute-start(bf16[520,128]{1,0:T(8,128)(2,1)S(1)} %get-tuple-element.148.refs_0_), channel_id=1, source_target_pairs={{0,2},{1,5},{2,0},{3,7},{4,6},{5,1},{6,4},{7,3},{8,10},{9,13},{10,... | collective-permute-start | bytes 399368 | tf_op jit(solution)/shard_map/ppermute | solution.py:413
  81.4 5.3 %collective-permute-start.24 = (bf16[520,128]{1,0:T(8,128)(2,1)S(1)}, bf16[520,128]{1,0:T(8,128)(2,1)S(1)}, u32[]{:S(2)}, u32[]{:S(2)}) collective-permute-start(bf16[520,128]{1,0:T(8,128)(2,1)S(1)} %get-tuple-element.148.refs_0_), channel_id=1, source_target_pairs={{0,4},{1,3},{2,6},{3,1},{4,0},{5,7},{6,2},{7,5},{8,12},{9,11},{10,... | collective-permute-start | bytes 399368 | tf_op jit(solution)/shard_map/ppermute | solution.py:413
  82.2 7.2 %collective-permute-start.26 = (bf16[520,128]{1,0:T(8,128)(2,1)S(1)}, bf16[520,128]{1,0:T(8,128)(2,1)S(1)}, u32[]{:S(2)}, u32[]{:S(2)}) collective-permute-start(bf16[520,128]{1,0:T(8,128)(2,1)S(1)} %get-tuple-element.148.refs_0_), channel_id=1, source_target_pairs={{0,6},{1,7},{2,4},{3,5},{4,2},{5,3},{6,0},{7,1},{8,14},{9,15},{10,... | collective-permute-start | bytes 399368 | tf_op jit(solution)/shard_map/ppermute | solution.py:413
  83.7 6.1 %collective-permute-start.21 = (bf16[520,128]{1,0:T(8,128)(2,1)S(1)}, bf16[520,128]{1,0:T(8,128)(2,1)S(1)}, u32[]{:S(2)}, u32[]{:S(2)}) collective-permute-start(bf16[520,128]{1,0:T(8,128)(2,1)S(1)} %get-tuple-element.148.refs_0_), channel_id=1, source_target_pairs={{0,1},{1,0},{2,3},{3,2},{4,5},{5,4},{6,7},{7,6},{8,9},{9,8},{10,11... | collective-permute-start | bytes 399368 | tf_op jit(solution)/shard_map/ppermute | solution.py:413
  86.6 4.3 %collective-permute-start.23 = (bf16[520,128]{1,0:T(8,128)(2,1)S(1)}, bf16[520,128]{1,0:T(8,128)(2,1)S(1)}, u32[]{:S(2)}, u32[]{:S(2)}) collective-permute-start(bf16[520,128]{1,0:T(8,128)(2,1)S(1)} %collective-permute-done.22.refs_1_.refs_2_), channel_id=1, source_target_pairs={{0,1},{1,0},{2,3},{3,2},{4,5},{5,4},{6,7},{7,6},{8,9},{9,8},{10,11... | collective-permute-start | bytes 399368 | tf_op jit(solution)/shard_map/ppermute | solution.py:413
  86.6 5.1 %collective-permute-start.25 = (bf16[520,128]{1,0:T(8,128)(2,1)S(1)}, bf16[520,128]{1,0:T(8,128)(2,1)S(1)}, u32[]{:S(2)}, u32[]{:S(2)}) collective-permute-start(bf16[520,128]{1,0:T(8,128)(2,1)S(1)} %collective-permute-done.24.refs_1_.refs_4_), channel_id=1, source_target_pairs={{0,1},{1,0},{2,3},{3,2},{4,5},{5,4},{6,7},{7,6},{8,9},{9,8},{10,11... | collective-permute-start | bytes 399368 | tf_op jit(solution)/shard_map/ppermute | solution.py:413
  89.4 3.2 %collective-permute-start.27 = (bf16[520,128]{1,0:T(8,128)(2,1)S(1)}, bf16[520,128]{1,0:T(8,128)(2,1)S(1)}, u32[]{:S(2)}, u32[]{:S(2)}) collective-permute-start(bf16[520,128]{1,0:T(8,128)(2,1)S(1)} %collective-permute-done.26.refs_1_.refs_6_), channel_id=1, source_target_pairs={{0,1},{1,0},{2,3},{3,2},{4,5},{5,4},{6,7},{7,6},{8,9},{9,8},{10,11... | collective-permute-start | bytes 399368 | tf_op jit(solution)/shard_map/ppermute | solution.py:413
  93.0 8.4 %collective-permute-start.28 = (bf16[520,128]{1,0:T(8,128)(2,1)S(1)}, bf16[520,128]{1,0:T(8,128)(2,1)S(1)}, u32[]{:S(2)}, u32[]{:S(2)}) collective-permute-start(bf16[520,128]{1,0:T(8,128)(2,1)S(1)} %get-tuple-element.161), channel_id=1, source_target_pairs={{0,24},{1,25},{2,26},{3,27},{4,28},{5,29},{6,30},{7,31},{8,16},{9,... | collective-permute-start | bytes 399368 | tf_op jit(solution)/shard_map/ppermute | solution.py:413
  95.9 9.5 %collective-permute-start.29 = (bf16[520,128]{1,0:T(8,128)(2,1)S(1)}, bf16[520,128]{1,0:T(8,128)(2,1)S(1)}, u32[]{:S(2)}, u32[]{:S(2)}) collective-permute-start(bf16[520,128]{1,0:T(8,128)(2,1)S(1)} %get-tuple-element.162), channel_id=1, source_target_pairs={{0,8},{1,17},{2,10},{3,19},{4,12},{5,21},{6,14},{7,23},{8,0},{9,25... | collective-permute-start | bytes 399368 | tf_op jit(solution)/shard_map/ppermute | solution.py:413
  96.0 11.5 %collective-permute-start.30 = (bf16[520,128]{1,0:T(8,128)(2,1)S(1)}, bf16[520,128]{1,0:T(8,128)(2,1)S(1)}, u32[]{:S(2)}, u32[]{:S(2)}) collective-permute-start(bf16[520,128]{1,0:T(8,128)(2,1)S(1)} %get-tuple-element.163), channel_id=1, source_target_pairs={{0,16},{1,9},{2,18},{3,11},{4,20},{5,13},{6,22},{7,15},{8,24},{9,1... | collective-permute-start | bytes 399368 | tf_op jit(solution)/shard_map/ppermute | solution.py:413
  107.6 8.3 %collective-permute-start.31 = (bf16[520,128]{1,0:T(8,128)(2,1)S(1)}, bf16[520,128]{1,0:T(8,128)(2,1)S(1)}, u32[]{:S(2)}, u32[]{:S(2)}) collective-permute-start(bf16[520,128]{1,0:T(8,128)(2,1)S(1)} %get-tuple-element.166.refs_0_.refs_5_), channel_id=1, source_target_pairs={{0,24},{1,25},{2,26},{3,27},{4,28},{5,29},{6,30},{7,31},{8,16},{9,... | collective-permute-start | bytes 399368 | tf_op jit(solution)/shard_map/ppermute | solution.py:413
  110.2 8.5 %collective-permute-start.32 = (bf16[520,128]{1,0:T(8,128)(2,1)S(1)}, bf16[520,128]{1,0:T(8,128)(2,1)S(1)}, u32[]{:S(2)}, u32[]{:S(2)}) collective-permute-start(bf16[520,128]{1,0:T(8,128)(2,1)S(1)} %get-tuple-element.166.refs_0_.refs_5_), channel_id=1, source_target_pairs={{0,8},{1,17},{2,10},{3,19},{4,12},{5,21},{6,14},{7,23},{8,0},{9,25... | collective-permute-start | bytes 399368 | tf_op jit(solution)/shard_map/ppermute | solution.py:413
  110.3 10.2 %collective-permute-start.33 = (bf16[520,128]{1,0:T(8,128)(2,1)S(1)}, bf16[520,128]{1,0:T(8,128)(2,1)S(1)}, u32[]{:S(2)}, u32[]{:S(2)}) collective-permute-start(bf16[520,128]{1,0:T(8,128)(2,1)S(1)} %get-tuple-element.166.refs_0_.refs_5_), channel_id=1, source_target_pairs={{0,16},{1,9},{2,18},{3,11},{4,20},{5,13},{6,22},{7,15},{8,24},{9,1... | collective-permute-start | bytes 399368 | tf_op jit(solution)/shard_map/ppermute | solution.py:413
  123.8 6.2 %collective-permute-start.35 = (bf16[520,128]{1,0:T(8,128)(2,1)S(1)}, bf16[520,128]{1,0:T(8,128)(2,1)S(1)}, u32[]{:S(2)}, u32[]{:S(2)}) collective-permute-start(bf16[520,128]{1,0:T(8,128)(2,1)S(1)} %get-tuple-element.180), channel_id=1, source_target_pairs={{0,2},{1,5},{2,0},{3,7},{4,6},{5,1},{6,4},{7,3},{8,10},{9,13},{10,... | collective-permute-start | bytes 399368 | tf_op jit(solution)/shard_map/ppermute | solution.py:413
  125.1 5.0 %collective-permute-start.36 = (bf16[520,128]{1,0:T(8,128)(2,1)S(1)}, bf16[520,128]{1,0:T(8,128)(2,1)S(1)}, u32[]{:S(2)}, u32[]{:S(2)}) collective-permute-start(bf16[520,128]{1,0:T(8,128)(2,1)S(1)} %get-tuple-element.181), channel_id=1, source_target_pairs={{0,4},{1,3},{2,6},{3,1},{4,0},{5,7},{6,2},{7,5},{8,12},{9,11},{10,... | collective-permute-start | bytes 399368 | tf_op jit(solution)/shard_map/ppermute | solution.py:413
  126.4 7.1 %collective-permute-start.37 = (bf16[520,128]{1,0:T(8,128)(2,1)S(1)}, bf16[520,128]{1,0:T(8,128)(2,1)S(1)}, u32[]{:S(2)}, u32[]{:S(2)}) collective-permute-start(bf16[520,128]{1,0:T(8,128)(2,1)S(1)} %get-tuple-element.182), channel_id=1, source_target_pairs={{0,6},{1,7},{2,4},{3,5},{4,2},{5,3},{6,0},{7,1},{8,14},{9,15},{10,... | collective-permute-start | bytes 399368 | tf_op jit(solution)/shard_map/ppermute | solution.py:413
  133.8 6.5 %collective-permute-start.39 = (bf16[520,128]{1,0:T(8,128)(2,1)S(1)}, bf16[520,128]{1,0:T(8,128)(2,1)S(1)}, u32[]{:S(2)}, u32[]{:S(2)}) collective-permute-start(bf16[520,128]{1,0:T(8,128)(2,1)S(1)} %get-tuple-element.186.refs_0_), channel_id=1, source_target_pairs={{0,2},{1,5},{2,0},{3,7},{4,6},{5,1},{6,4},{7,3},{8,10},{9,13},{10,... | collective-permute-start | bytes 399368 | tf_op jit(solution)/shard_map/ppermute | solution.py:413
  135.0 5.5 %collective-permute-start.41 = (bf16[520,128]{1,0:T(8,128)(2,1)S(1)}, bf16[520,128]{1,0:T(8,128)(2,1)S(1)}, u32[]{:S(2)}, u32[]{:S(2)}) collective-permute-start(bf16[520,128]{1,0:T(8,128)(2,1)S(1)} %get-tuple-element.186.refs_0_), channel_id=1, source_target_pairs={{0,4},{1,3},{2,6},{3,1},{4,0},{5,7},{6,2},{7,5},{8,12},{9,11},{10,... | collective-permute-start | bytes 399368 | tf_op jit(solution)/shard_map/ppermute | solution.py:413
  136.0 7.0 %collective-permute-start.43 = (bf16[520,128]{1,0:T(8,128)(2,1)S(1)}, bf16[520,128]{1,0:T(8,128)(2,1)S(1)}, u32[]{:S(2)}, u32[]{:S(2)}) collective-permute-start(bf16[520,128]{1,0:T(8,128)(2,1)S(1)} %get-tuple-element.186.refs_0_), channel_id=1, source_target_pairs={{0,6},{1,7},{2,4},{3,5},{4,2},{5,3},{6,0},{7,1},{8,14},{9,15},{10,... | collective-permute-start | bytes 399368 | tf_op jit(solution)/shard_map/ppermute | solution.py:413
  137.3 6.1 %collective-permute-start.38 = (bf16[520,128]{1,0:T(8,128)(2,1)S(1)}, bf16[520,128]{1,0:T(8,128)(2,1)S(1)}, u32[]{:S(2)}, u32[]{:S(2)}) collective-permute-start(bf16[520,128]{1,0:T(8,128)(2,1)S(1)} %get-tuple-element.186.refs_0_), channel_id=1, source_target_pairs={{0,1},{1,0},{2,3},{3,2},{4,5},{5,4},{6,7},{7,6},{8,9},{9,8},{10,11... | collective-permute-start | bytes 399368 | tf_op jit(solution)/shard_map/ppermute | solution.py:413
  140.2 4.0 %collective-permute-start.40 = (bf16[520,128]{1,0:T(8,128)(2,1)S(1)}, bf16[520,128]{1,0:T(8,128)(2,1)S(1)}, u32[]{:S(2)}, u32[]{:S(2)}) collective-permute-start(bf16[520,128]{1,0:T(8,128)(2,1)S(1)} %collective-permute-done.39.refs_1_.refs_2_), channel_id=1, source_target_pairs={{0,1},{1,0},{2,3},{3,2},{4,5},{5,4},{6,7},{7,6},{8,9},{9,8},{10,11... | collective-permute-start | bytes 399368 | tf_op jit(solution)/shard_map/ppermute | solution.py:413
  140.5 4.5 %collective-permute-start.42 = (bf16[520,128]{1,0:T(8,128)(2,1)S(1)}, bf16[520,128]{1,0:T(8,128)(2,1)S(1)}, u32[]{:S(2)}, u32[]{:S(2)}) collective-permute-start(bf16[520,128]{1,0:T(8,128)(2,1)S(1)} %collective-permute-done.41.refs_1_.refs_4_), channel_id=1, source_target_pairs={{0,1},{1,0},{2,3},{3,2},{4,5},{5,4},{6,7},{7,6},{8,9},{9,8},{10,11... | collective-permute-start | bytes 399368 | tf_op jit(solution)/shard_map/ppermute | solution.py:413
  142.9 3.0 %collective-permute-start.44 = (bf16[520,128]{1,0:T(8,128)(2,1)S(1)}, bf16[520,128]{1,0:T(8,128)(2,1)S(1)}, u32[]{:S(2)}, u32[]{:S(2)}) collective-permute-start(bf16[520,128]{1,0:T(8,128)(2,1)S(1)} %collective-permute-done.43.refs_1_.refs_6_), channel_id=1, source_target_pairs={{0,1},{1,0},{2,3},{3,2},{4,5},{5,4},{6,7},{7,6},{8,9},{9,8},{10,11... | collective-permute-start | bytes 399368 | tf_op jit(solution)/shard_map/ppermute | solution.py:413
  146.3 8.4 %collective-permute-start.45 = (bf16[520,128]{1,0:T(8,128)(2,1)S(1)}, bf16[520,128]{1,0:T(8,128)(2,1)S(1)}, u32[]{:S(2)}, u32[]{:S(2)}) collective-permute-start(bf16[520,128]{1,0:T(8,128)(2,1)S(1)} %get-tuple-element.199), channel_id=1, source_target_pairs={{0,24},{1,25},{2,26},{3,27},{4,28},{5,29},{6,30},{7,31},{8,16},{9,... | collective-permute-start | bytes 399368 | tf_op jit(solution)/shard_map/ppermute | solution.py:413
  148.7 9.9 %collective-permute-start.46 = (bf16[520,128]{1,0:T(8,128)(2,1)S(1)}, bf16[520,128]{1,0:T(8,128)(2,1)S(1)}, u32[]{:S(2)}, u32[]{:S(2)}) collective-permute-start(bf16[520,128]{1,0:T(8,128)(2,1)S(1)} %get-tuple-element.200), channel_id=1, source_target_pairs={{0,8},{1,17},{2,10},{3,19},{4,12},{5,21},{6,14},{7,23},{8,0},{9,25... | collective-permute-start | bytes 399368 | tf_op jit(solution)/shard_map/ppermute | solution.py:413
  148.9 11.9 %collective-permute-start.47 = (bf16[520,128]{1,0:T(8,128)(2,1)S(1)}, bf16[520,128]{1,0:T(8,128)(2,1)S(1)}, u32[]{:S(2)}, u32[]{:S(2)}) collective-permute-start(bf16[520,128]{1,0:T(8,128)(2,1)S(1)} %get-tuple-element.201), channel_id=1, source_target_pairs={{0,16},{1,9},{2,18},{3,11},{4,20},{5,13},{6,22},{7,15},{8,24},{9,1... | collective-permute-start | bytes 399368 | tf_op jit(solution)/shard_map/ppermute | solution.py:413
  161.0 8.3 %collective-permute-start.48 = (bf16[520,128]{1,0:T(8,128)(2,1)S(1)}, bf16[520,128]{1,0:T(8,128)(2,1)S(1)}, u32[]{:S(2)}, u32[]{:S(2)}) collective-permute-start(bf16[520,128]{1,0:T(8,128)(2,1)S(1)} %get-tuple-element.207.refs_0_), channel_id=1, source_target_pairs={{0,24},{1,25},{2,26},{3,27},{4,28},{5,29},{6,30},{7,31},{8,16},{9,... | collective-permute-start | bytes 399368 | tf_op jit(solution)/shard_map/ppermute | solution.py:413
  163.5 8.6 %collective-permute-start.49 = (bf16[520,128]{1,0:T(8,128)(2,1)S(1)}, bf16[520,128]{1,0:T(8,128)(2,1)S(1)}, u32[]{:S(2)}, u32[]{:S(2)}) collective-permute-start(bf16[520,128]{1,0:T(8,128)(2,1)S(1)} %get-tuple-element.207.refs_0_), channel_id=1, source_target_pairs={{0,8},{1,17},{2,10},{3,19},{4,12},{5,21},{6,14},{7,23},{8,0},{9,25... | collective-permute-start | bytes 399368 | tf_op jit(solution)/shard_map/ppermute | solution.py:413
  163.5 10.3 %collective-permute-start.50 = (bf16[520,128]{1,0:T(8,128)(2,1)S(1)}, bf16[520,128]{1,0:T(8,128)(2,1)S(1)}, u32[]{:S(2)}, u32[]{:S(2)}) collective-permute-start(bf16[520,128]{1,0:T(8,128)(2,1)S(1)} %get-tuple-element.207.refs_0_), channel_id=1, source_target_pairs={{0,16},{1,9},{2,18},{3,11},{4,20},{5,13},{6,22},{7,15},{8,24},{9,1... | collective-permute-start | bytes 399368 | tf_op jit(solution)/shard_map/ppermute | solution.py:413
  (5 other events, 26.3 us)
